TPU v7x, 256 devices: a whole 4x4x8 slice. The times are simulated.
256 devices in a mesh: blk: 32 (over y, z), rep: 8 (over x, core).
Axes of the slice: x: 4, y: 4, z: 8, core: 2. Of those that a mesh axis runs over, the one named last changes fastest.
Arguments:
- hidden_in: bfloat16 [8, 512, 2560], P('rep', 'blk'), may hold values from -6 to 6
- w_z: bfloat16 [2560, 4096], P(None, 'blk'), may hold values from -0.125 to 0.125
- w_x: bfloat16 [2560, 4096], P(None, 'blk'), may hold values from -0.125 to 0.125
- w_bc: bfloat16 [2560, 256], replicated, may hold values from -0.125 to 0.125
- w_dt: bfloat16 [2560, 64], P(None, 'blk'), may hold values from -0.125 to 0.125
- conv_x: float32 [4, 4096], P(None, 'blk'), may hold values from -3 to 3
- conv_bc: float32 [4, 256], replicated, may hold values from -3 to 3
- dt_bias: float32 [4, 64], P(None, 'blk'), may hold values from -3 to -0.5
- a_log: float32 [64], P('blk'), may hold values from -2.5 to 0.5
- d_skip: float32 [64], P('blk'), may hold values from 0.5 to 1.5
- norm_gain: float32 [4096], P('blk'), may hold values from 0.5 to 1.5
- w_out: bfloat16 [4096, 2560], P('blk'), may hold values from -0.09375 to 0.09375
- edge_x: bfloat16 [256, 3, 4096], P('rep', None, 'blk'), may hold values from -6 to 6
- edge_bc: bfloat16 [256, 3, 256], P('rep'), may hold values from -6 to 6
- pool: float32 [384, 64, 64, 128], P('rep', 'blk'), may hold values from -0.6 to 0.6
- tenant_sizes: int32 [4], replicated, may hold values from 1 to 128, 256 in all
- owner: int32 [256, 1], P('rep'), may hold values from 0 to 7; in each aligned block of 32 rows (0 to 31, 32 to 63, ...) at most 6 rows name the same one
- accepted: int32 [256], P('rep'), may hold values from 1 to 16
- prompt_len: int32 [256], P('rep'), may hold values from 1 to 11
Outputs:
- hidden_out: bfloat16 [8, 512, 2560], P('rep', 'blk')
- new_pool: float32 [384, 64, 64, 128], P('rep', 'blk')
Inputs may be any that keep to these rules, and one draw needn't show every extreme that they name: Among the requests of one group (aligned blocks of 32 requests) each owner is named at most 6 times, a bound that some block reaches. `tenant_sizes`: the sizes sum to 256.
All inputs are finite; a program needn't handle non-finite values.
Results may differ from a plain program's by a relative error of at most 0.025.
Values may be sent and summed in bfloat16 or wider, within the bound.
A program may use at most 64 MiB of HBM per device.

v0:
```python
import jax
import jax.numpy as jnp
from jax import lax
from jax.sharding import PartitionSpec as P


def convolve(edge_cells, fresh_cells, kernel, edge_mask):
    sequence = jnp.concatenate(
        [edge_cells * edge_mask[:, :, None].astype(edge_cells.dtype), fresh_cells], 1
    ).astype(jnp.float32)
    steps_count = fresh_cells.shape[1]
    summed = kernel[0] * sequence[:, 0:steps_count]
    for offset in range(1, kernel.shape[0]):
        summed = summed + kernel[offset] * sequence[:, offset : offset + steps_count]
    return jax.nn.silu(summed).astype(jnp.bfloat16)


def shards(
    hidden_in,
    w_z,
    w_x,
    w_bc,
    w_dt,
    conv_x,
    conv_bc,
    dt_bias,
    a_log,
    d_skip,
    norm_gain,
    w_out,
    edge_x,
    edge_bc,
    pool,
    tenant_sizes,
    owner,
    accepted,
    prompt_len,
):
    highest = lax.Precision.HIGHEST
    rows_in = hidden_in[0]
    local_rows = rows_in.shape[0]
    n_req = edge_x.shape[0]
    drafts = local_rows * lax.axis_size("blk") // n_req
    state_dim = w_bc.shape[1] // 2
    heads_here = w_dt.shape[1]
    inner_here = w_z.shape[1]
    head_dim = inner_here // heads_here
    slots_here = pool.shape[0]
    cap_group = slots_here // lax.axis_size("rep")
    weights_in = (w_z, w_x, w_dt, w_bc)
    block_rows = lax.all_gather(rows_in, "blk", axis=0, tiled=True)
    projected = jnp.concatenate(
        [
            jnp.dot(block_rows, weight_cols, preferred_element_type=jnp.float32)
            for weight_cols in weights_in
        ],
        1,
    ).astype(jnp.bfloat16)
    z_all = projected[:, :inner_here]
    u_all = projected[:, inner_here : 2 * inner_here]
    dt_raw = projected[:, 2 * inner_here : 2 * inner_here + heads_here]
    bc_all = projected[:, 2 * inner_here + heads_here :]
    edge_len = edge_x.shape[1]
    edge_mask = prompt_len[:, None] >= (edge_len - jnp.arange(edge_len, dtype=jnp.int32))[None, :]
    x_conv = convolve(edge_x, u_all.reshape(n_req, drafts, inner_here), conv_x, edge_mask)
    bc_conv = convolve(edge_bc, bc_all.reshape(n_req, drafts, 2 * state_dim), conv_bc, edge_mask)
    b_half = bc_conv[:, :, :state_dim]
    c_half = bc_conv[:, :, state_dim:]
    b_float = b_half.astype(jnp.float32)
    c_float = c_half.astype(jnp.float32)
    x_heads = x_conv.reshape(n_req, drafts, heads_here, head_dim).astype(jnp.float32)
    req_index = lax.axis_index("rep") * n_req + jnp.arange(n_req, dtype=jnp.int32)
    tenant_ends = jnp.cumsum(tenant_sizes)
    tenant_id = jnp.sum((req_index[:, None] >= tenant_ends[None, :-1]).astype(jnp.int32), axis=1)
    tenant_pick = (
        tenant_id[:, None] == jnp.arange(tenant_sizes.shape[0], dtype=jnp.int32)[None, :]
    ).astype(jnp.float32)
    bias_req = jnp.dot(tenant_pick, dt_bias, precision=highest)
    step_size = jax.nn.softplus(
        dt_raw.reshape(n_req, drafts, heads_here).astype(jnp.float32) + bias_req[:, None, :]
    )
    log_decay = jnp.cumsum(step_size * (-jnp.exp(a_log))[None, None, :], axis=1)
    draft_index = jnp.arange(drafts, dtype=jnp.int32)
    causal = draft_index[:, None] >= draft_index[None, :]
    scores = jnp.einsum("rtn,rsn->rts", c_float, b_float, precision=highest)
    log_gap = log_decay[:, :, None, :] - log_decay[:, None, :, :]
    weight = (
        jnp.where(causal[None, :, :, None], jnp.exp(jnp.minimum(log_gap, 0.0)), 0.0)
        * step_size[:, None, :, :]
        * scores[:, :, :, None]
    )
    y_local = (
        jnp.einsum("rtsh,rshp->rthp", weight, x_heads, precision=highest)
        + d_skip[None, None, :, None] * x_heads
    )
    pick_last = (draft_index[None, :] == accepted[:, None] - 1).astype(jnp.float32)
    log_accept = jnp.sum(pick_last[:, :, None] * log_decay, axis=1)
    keep_draft = draft_index[None, :] < accepted[:, None]
    coef = (
        jnp.where(
            keep_draft[:, :, None],
            jnp.exp(jnp.minimum(log_accept[:, None, :] - log_decay, 0.0)),
            0.0,
        )
        * step_size
    )
    carry_decay = jnp.exp(log_accept)
    decay_now = jnp.exp(log_decay)
    owner_of = owner[:, 0]
    local_index = jnp.arange(n_req, dtype=jnp.int32)
    earlier = (owner_of[None, :] == owner_of[:, None]) & (
        local_index[None, :] < local_index[:, None]
    )
    rank_within = jnp.sum(earlier.astype(jnp.int32), axis=1)
    slot_index = owner_of * cap_group + rank_within
    fetched = lax.all_to_all(
        pool.astype(jnp.bfloat16), "rep", split_axis=0, concat_axis=0, tiled=True
    ).astype(pool.dtype)
    start_state = jnp.take(fetched, slot_index, axis=0)
    y_prior = decay_now[:, :, :, None] * jnp.einsum(
        "rhpn,rtn->rthp", start_state, c_float, precision=highest
    )
    accepted_state = carry_decay[:, :, None, None] * start_state + jnp.einsum(
        "rsh,rshp,rsn->rhpn", coef, x_heads, b_float, precision=highest
    )
    buffer = jnp.zeros(pool.shape, jnp.float32).at[slot_index].set(accepted_state)
    new_pool = lax.all_to_all(
        buffer.astype(jnp.bfloat16), "rep", split_axis=0, concat_axis=0, tiled=True
    ).astype(buffer.dtype)
    y_total = (y_local + y_prior).reshape(n_req * drafts, inner_here)
    gated = y_total * jax.nn.silu(z_all.astype(jnp.float32))
    sq_total = lax.psum(jnp.sum(gated * gated, axis=1), "blk")
    inner_all = inner_here * lax.axis_size("blk")
    normed = (gated * lax.rsqrt(sq_total / inner_all + 1e-05)[:, None] * norm_gain[None, :]).astype(
        jnp.bfloat16
    )
    block_rows = normed
    mixed = lax.psum_scatter(
        jnp.dot(block_rows, w_out, preferred_element_type=jnp.float32).astype(jnp.bfloat16),
        "blk",
        scatter_dimension=0,
        tiled=True,
    )
    return (mixed[None], new_pool)


def solution(mesh):
    placed = (
        P("rep", "blk", None),
        P(None, "blk"),
        P(None, "blk"),
        P(),
        P(None, "blk"),
        P(None, "blk"),
        P(),
        P(None, "blk"),
        P("blk"),
        P("blk"),
        P("blk"),
        P("blk", None),
        P("rep", None, "blk"),
        P("rep", None, None),
        P("rep", "blk", None, None),
        P(),
        P("rep", None),
        P("rep"),
        P("rep"),
    )
    return jax.shard_map(
        shards,
        mesh=mesh,
        in_specs=placed,
        out_specs=(P("rep", "blk", None), P("rep", "blk", None, None)),
        check_vma=False,
    )
```

profile of v0, /device:TPU:1, one launch (start us, length us, event | category | flops | bytes accessed | tf_op | source)
XLA Modules:
  0.0 414.0 jit_solution(11525417549869949106)
XLA Ops:
  7.2 0.7 all-gather.3.cloned.1.call-update
  7.9 3.4 convert_element_type.82
  11.4 6.9 %all-to-all-start = ((bf16[48,2,64,128]{3,2,1,0:T(8,128)(2,1)}), bf16[48,2,64,128]{3,2,1,0:T(8,128)(2,1)S(1)}, u32[]{:S(2)}, u32[]{:S(2)}) async-start(bf16[48,2,64,128]{3,2,1,0:T(8,128)(2,1)} %convert_element_type.82), calls=%async_computation | async-start | bytes 3145728 | tf_op jit(solution)/shard_map/all_to_all | solution.py:116
  18.7 0.5 and_bitcast_fusion
  19.3 0.5 copy-done.10
  19.9 0.6 iota_compare_fusion.5
  20.6 0.6 copy.75
  21.2 0.2 fusion.70
  21.4 0.6 slice_bitcast_fusion.4
  22.0 0.6 fusion.75
  22.6 0.6 fusion.72
  23.2 0.7 copy_multiply_fusion
  24.0 15.1 %all-to-all-done = bf16[48,2,64,128]{3,2,1,0:T(8,128)(2,1)S(1)} async-done(((bf16[48,2,64,128]{3,2,1,0:T(8,128)(2,1)}), bf16[48,2,64,128]{3,2,1,0:T(8,128)(2,1)S(1)}, u32[]{:S(2)}, u32[]{:S(2)}) %all-to-all-start) | async-done | bytes 1572896 | tf_op jit(solution)/shard_map/all_to_all | solution.py:116
  39.0 2.1 convert_element_type.83
  41.1 2.6 gather_fusion
  43.7 46.2 %all-gather.3.cloned.1.call-done = bf16[1,512,2560]{2,1,0:T(8,128)(2,1)} async-done(((bf16[1,16,2560]{2,1,0:T(8,128)(2,1)}), bf16[1,512,2560]{2,1,0:T(8,128)(2,1)}) %all-gather.3.cloned.1.call-update) | async-done | bytes 2621456 | tf_op jit(solution)/shard_map/all_gather | solution.py:51
  89.9 2.5 fusion.32
  92.5 0.7 broadcast_multiply_fusion.1
  93.2 0.7 copy.80
  93.9 2.7 fusion.20
  96.8 0.2 multiply_convert_fusion.2
  96.9 0.9 reshape.167
  97.8 1.6 copy.77
  99.4 1.7 fusion.76
  101.1 1.2 copy.78
  102.3 1.7 multiply_reduce_fusion
  104.0 1.2 copy.85
  105.3 2.6 fusion.17
  108.1 0.3 multiply_convert_fusion
  108.4 0.2 fusion.65
  108.6 0.2 copy-done.3
  108.8 0.6 fusion.16
  109.5 2.6 fusion.13
  112.1 1.1 copy.86
  113.2 2.0 reshape.170
  115.2 1.8 copy.87
  117.0 3.7 multiply_reduce_fusion.1
  120.7 58.3 %psum.7 = f32[512]{0:T(512)S(1)} all-reduce(f32[512]{0:T(512)S(1)} %get-tuple-element.16), channel_id=1, replica_groups=mesh['blk'=32,'rep'=8] {'blk'}, use_global_device_ids=true, to_apply=%region_5.6 | all-reduce | flops 512 | bytes 4096 | tf_op jit(solution)/shard_map/psum | solution.py:132
  179.0 3.6 convolution_convert_fusion
  182.6 0.6 copy-done.26
  183.3 1.1 copy.89
  184.6 4.6 %multiply_add_fusion = f32[32,2,64,128]{3,2,1,0:T(8,128)} fusion(f32[32,2,64,128]{3,2,1,0:T(8,128)S(1)} %gather_fusion, f32[32,2]{1,0:T(8,128)S(1)} %exp.50, pred[32]{0:T(512)(128)(4,1)S(1)} %copy-done.12, f32[32,16,2]{1,2,0:T(2,128)S(1)} %copy.90, bf16[32,16,2,64]{3,2,1,0:T(2,128)(2,1)} %reshape.167, bf16[32,16,256]{2,1,0:T(8,128)(2,1)} %copy-done.2), kind=kOutput, calls=%fused_computation.11 | convolution fusion | flops 102367232 | bytes 4591904 | tf_op jit(solution)/shard_map/rsh,rshp,rsn->rhpn/dot_general | solution.py:123
  189.1 2.1 broadcast_in_dim.31
  191.3 5.3 %scatter_fusion = f32[48,2,64,128]{3,2,1,0:T(8,128)} fusion(f32[48,2,64,128]{3,2,1,0:T(8,128)} %broadcast_in_dim.31, s32[32]{0:T(128)S(1)} %bitcast.79, f32[32,2,64,128]{3,2,1,0:T(8,128)S(1)} %copy-done.1), kind=kCustom, calls=%fused_computation.1 | custom fusion | bytes 6291584 | tf_op jit(solution)/shard_map/scatter | solution.py:126
  196.6 2.2 convert_element_type.88
  198.9 42.9 %all_to_all.10 = bf16[48,2,64,128]{3,2,1,0:T(8,128)(2,1)S(1)} all-to-all(bf16[48,2,64,128]{3,2,1,0:T(8,128)(2,1)S(1)} %convert_element_type.88), channel_id=1, replica_groups=mesh['blk'=32,'rep'=8] {'rep'}, dimensions={0} | all-to-all | bytes 3145728 | tf_op jit(solution)/shard_map/all_to_all | solution.py:127
  241.8 2.0 convert_element_type.89
  243.9 163.3 %reduce-scatter.2.cloned.1.call-done = bf16[16,2560]{1,0:T(8,128)(2,1)} async-done(((bf16[512,2560]{1,0:T(8,128)(2,1)}), bf16[16,2560]{1,0:T(8,128)(2,1)}) %reduce-scatter.2.cloned.1.call-update) | async-done | bytes 81936 | tf_op jit(solution)/shard_map/reduce_scatter | solution.py:138
  (88 shorter events, 1.5 us)
Async XLA Ops:
  7.2 98.1 %copy-start = (bf16[2560,256]{1,0:T(8,128)(2,1)S(1)}, bf16[2560,256]{1,0:T(8,128)(2,1)}, u32[]{:S(2)}) copy-start(bf16[2560,256]{1,0:T(8,128)(2,1)} %param.22) | copy-start | bytes 3932164
  7.2 82.7 %all-gather.3.cloned.1.call-start = ((), (), s32[]{:S(2)}) async-start(), calls=%async_computation.4 | async-start | bytes 2703360 | tf_op jit(solution)/shard_map/all_gather | solution.py:51
  11.3 7.0 %copy-start.30 = (s32[4]{0:T(128)S(1)}, s32[4]{0:T(128)}, u32[]{:S(2)}) copy-start(s32[4]{0:T(128)} %param.34) | copy-start | bytes 52
  11.3 7.1 %copy-start.27 = (s32[32,1]{0,1:T(1,128)S(1)}, s32[32,1]{0,1:T(1,128)}, u32[]{:S(2)}) copy-start(s32[32,1]{0,1:T(1,128)} %param.35) | copy-start | bytes 388
  11.3 8.0 %copy-start.31 = (f32[2]{0:T(128)S(1)}, f32[2]{0:T(128)}, u32[]{:S(2)}) copy-start(f32[2]{0:T(128)} %param.27) | copy-start | bytes 28
  11.3 8.4 %copy-start.28 = (s32[32]{0:T(128)S(1)}, s32[32]{0:T(128)}, u32[]{:S(2)}) copy-start(s32[32]{0:T(128)} %param.37) | copy-start | bytes 388
  11.3 8.5 %copy-start.8 = (bf16[32,3,128]{2,0,1:T(8,128)(2,1)S(1)}, bf16[32,3,128]{2,0,1:T(8,128)(2,1)}, u32[]{:S(2)}) copy-start(bf16[32,3,128]{2,0,1:T(8,128)(2,1)} %param.31) | copy-start | bytes 73732
  11.4 9.8 %copy-start.25 = (s32[32]{0:T(128)S(1)}, s32[32]{0:T(128)}, u32[]{:S(2)}) copy-start(s32[32]{0:T(128)} %param.36) | copy-start | bytes 388
  11.4 9.8 %copy-start.29 = (f32[4,2]{0,1:T(2,128)S(1)}, f32[4,2]{0,1:T(2,128)}, u32[]{:S(2)}) copy-start(f32[4,2]{0,1:T(2,128)} %param.26) | copy-start | bytes 100
  11.4 10.0 %copy-start.22 = (f32[4,128]{1,0:T(4,128)S(1)}, f32[4,128]{1,0:T(4,128)}, u32[]{:S(2)}) copy-start(f32[4,128]{1,0:T(4,128)} %param.24) | copy-start | bytes 6148
  11.4 10.6 %copy-start.17 = (f32[4,256]{1,0:T(4,128)S(1)}, f32[4,256]{1,0:T(4,128)}, u32[]{:S(2)}) copy-start(f32[4,256]{1,0:T(4,128)} %param.25) | copy-start | bytes 12292
  11.4 11.8 %copy-start.6 = (bf16[32,3,256]{2,0,1:T(8,128)(2,1)S(1)}, bf16[32,3,256]{2,0,1:T(8,128)(2,1)}, u32[]{:S(2)}) copy-start(bf16[32,3,256]{2,0,1:T(8,128)(2,1)} %param.32) | copy-start | bytes 147460
  11.4 27.6 %all-to-all-start = ((bf16[48,2,64,128]{3,2,1,0:T(8,128)(2,1)}), bf16[48,2,64,128]{3,2,1,0:T(8,128)(2,1)S(1)}, u32[]{:S(2)}, u32[]{:S(2)}) async-start(bf16[48,2,64,128]{3,2,1,0:T(8,128)(2,1)} %convert_element_type.82), calls=%async_computation | async-start | bytes 3145728 | tf_op jit(solution)/shard_map/all_to_all | solution.py:116
  18.3 388.9 %reduce-scatter.2.cloned.1.call-start = ((), (), s32[]{:S(2)}) async-start(), calls=%async_computation.3 | async-start | bytes 2703360 | tf_op jit(solution)/shard_map/reduce_scatter | solution.py:138
  19.2 0.6 copy-start.10
  41.1 48.8 %copy-start.9 = (bf16[2560,2]{0,1:T(2,128)(2,1)S(1)}, bf16[2560,2]{0,1:T(2,128)(2,1)}, u32[]{:S(2)}) copy-start(bf16[2560,2]{0,1:T(2,128)(2,1)} %param.23) | copy-start | bytes 30724
  93.9 2.8 copy-start.5
  93.9 2.8 copy-start.18
  93.9 2.8 copy-start.19
  93.9 2.8 copy-start.20
  93.9 2.8 copy-start.21
  105.2 2.7 copy-start.4
  105.2 2.8 copy-start.13
  105.2 2.8 copy-start.14
  105.3 2.8 copy-start.15
  105.3 2.8 copy-start.16
  107.9 1.0 copy-start.3
  107.9 0.9 copy-start.7
  107.9 0.9 copy-start.23
  107.9 0.9 copy-start.32
  108.1 1.4 copy-start.12
  108.4 3.7 copy-start.2
  117.0 62.0 %copy-start.24 = (f32[128]{0:T(128)S(1)}, f32[128]{0:T(128)}, u32[]{:S(2)}) copy-start(f32[128]{0:T(128)} %param.29) | copy-start | bytes 1540
  182.6 0.7 copy-start.26
  189.1 2.1 copy-start.1
  189.1 2.1 copy-start.11
Sparse Core Ops, SparseCore 0:
  10.6 79.2 all-gather.2
  182.8 224.3 reduce-scatter.1
where the time goes:
time: 419 us; the launch traced here: 414 us
  waiting for transfers between devices  225 us (54%)
  blocking collectives  101 us (24%)
  local copies, waits for them, and re-layouts  25.3 us (6%)
  matrix products  23.3 us (6%)
  other arithmetic  17.6 us (4%)
  between operations  14.4 us (3%)
  starting transfers between devices  6.91 us (2%)
    reduce_scatter x1, waiting for transfers between devices, shards(): lax.psum_scatter(jnp.dot(block_rows, w_out, preferred_element_type=jnp.fl...  163 us
    psum x1, blocking collectives, shards(): sq_total = lax.psum(jnp.sum(gated * gated, axis=1), 'blk')  58.3 us
    all_gather x1, waiting for transfers between devices, shards(): block_rows = lax.all_gather(rows_in, 'blk', axis=0, tiled=True)  46.2 us
    all_to_all x1, blocking collectives, shards(): lax.all_to_all(buffer.astype(jnp.bfloat16), 'rep', split_axis=0, concat_a...  42.9 us
    all_to_all x1, waiting for transfers between devices, shards(): lax.all_to_all(pool.astype(jnp.bfloat16), 'rep', split_axis=0, concat_axi...  15.1 us
    dot_general x4, matrix products, shards(): jnp.dot(block_rows, weight_cols, preferred_element_type=jnp.float32)  11.5 us
  transfers between devices with their start and end apart: 3, of which 3 were waited for; matrix products, arithmetic and copies ran while one was open for 7% of the time, Pallas kernels for 0%

commit v1 on v0

--- a/solution.py
+++ b/solution.py
@@ -48,7 +48,10 @@
     slots_here = pool.shape[0]
     cap_group = slots_here // lax.axis_size("rep")
     weights_in = (w_z, w_x, w_dt, w_bc)
-    block_rows = lax.all_gather(rows_in, "blk", axis=0, tiled=True)
+    n_blk = lax.axis_size("blk")
+    block_rows = lax.all_to_all(
+        jnp.broadcast_to(rows_in[None], (n_blk,) + rows_in.shape), "blk", 0, 0, tiled=True
+    ).reshape(n_blk * local_rows, rows_in.shape[1])
     projected = jnp.concatenate(
         [
             jnp.dot(block_rows, weight_cols, preferred_element_type=jnp.float32)
@@ -129,18 +132,20 @@
     ).astype(buffer.dtype)
     y_total = (y_local + y_prior).reshape(n_req * drafts, inner_here)
     gated = y_total * jax.nn.silu(z_all.astype(jnp.float32))
-    sq_total = lax.psum(jnp.sum(gated * gated, axis=1), "blk")
-    inner_all = inner_here * lax.axis_size("blk")
-    normed = (gated * lax.rsqrt(sq_total / inner_all + 1e-05)[:, None] * norm_gain[None, :]).astype(
-        jnp.bfloat16
-    )
-    block_rows = normed
-    mixed = lax.psum_scatter(
-        jnp.dot(block_rows, w_out, preferred_element_type=jnp.float32).astype(jnp.bfloat16),
-        "blk",
-        scatter_dimension=0,
-        tiled=True,
-    )
+    sq_part = jnp.sum(gated * gated, axis=1)
+    sq_hi = sq_part.astype(jnp.bfloat16)
+    sq_lo = (sq_part - sq_hi.astype(jnp.float32)).astype(jnp.bfloat16)
+    scaled = (gated * norm_gain[None, :]).astype(jnp.bfloat16)
+    partial = jnp.dot(scaled, w_out, preferred_element_type=jnp.float32).astype(jnp.bfloat16)
+    width = partial.shape[1]
+    extra = jnp.zeros((partial.shape[0], 128), jnp.bfloat16)
+    extra = extra.at[:, 0].set(sq_hi).at[:, 1].set(sq_lo)
+    packed = jnp.concatenate([partial, extra], 1).reshape(n_blk, local_rows, width + 128)
+    arrived = lax.all_to_all(packed, "blk", 0, 0, tiled=True).astype(jnp.float32)
+    summed = jnp.sum(arrived, axis=0)
+    inner_all = inner_here * n_blk
+    mean_sq = (summed[:, width] + summed[:, width + 1]) / inner_all
+    mixed = (summed[:, :width] * lax.rsqrt(mean_sq + 1e-05)[:, None]).astype(jnp.bfloat16)
     return (mixed[None], new_pool)
 
 

time: 419 us -> 246 us (0.59)
  waiting for transfers between devices: 225 us -> 115 us
  blocking collectives: 101 us -> 26.6 us
  starting transfers between devices: 6.91 us -> 24.9 us
  between operations: 14.4 us -> 1.12 us
  other arithmetic: 17.6 us -> 28.1 us
    reduce_scatter x1 -> x0, waiting for transfers between devices: 163 us -> none  [shards(): lax.psum_scatter(jnp.dot(block_rows, w_out, preferred_element_type=jnp.fl...]
    all_to_all x1 -> x3, waiting for transfers between devices: 15.1 us -> 115 us  [the longest x1 59.3 us: shards(): lax.all_to_all(packed, 'blk', 0, 0, tiled=True).astype(jnp.float32)]
    psum x1 -> x0, blocking collectives: 58.3 us -> none  [shards(): sq_total = lax.psum(jnp.sum(gated * gated, axis=1), 'blk')]
    all_gather x1 -> x0, waiting for transfers between devices: 46.2 us -> none  [shards(): block_rows = lax.all_gather(rows_in, 'blk', axis=0, tiled=True)]
    all_to_all x1 -> x3, starting transfers between devices: 6.87 us -> 24.9 us  [the longest x1 11.4 us: shards(): lax.all_to_all(jnp.broadcast_to(rows_in[None], (n_blk,) + rows_in.shape),...]
    all_to_all x1, blocking collectives: 42.9 us -> 26.6 us  [shards(): lax.all_to_all(pool.astype(jnp.bfloat16), 'rep', split_axis=0, concat_axi...]
  transfers between devices with their start and end apart: 3 -> 3, of which waited for: 3 -> 3; matrix products, arithmetic and copies ran while one was open for 7% -> 12% of each run, Pallas kernels for 0% -> 0%
where the time goes in v1:
time: 246 us; the launch traced here: 243 us
  waiting for transfers between devices  115 us (47%)
  other arithmetic  28.1 us (11%)
  blocking collectives  26.6 us (11%)
  local copies, waits for them, and re-layouts  25.5 us (10%)
  starting transfers between devices  24.9 us (10%)
  matrix products  21.7 us (9%)
    all_to_all x1, waiting for transfers between devices, shards(): lax.all_to_all(packed, 'blk', 0, 0, tiled=True).astype(jnp.float32)  59.3 us
    all_to_all x1, waiting for transfers between devices, shards(): lax.all_to_all(jnp.broadcast_to(rows_in[None], (n_blk,) + rows_in.shape),...  48.6 us
    all_to_all x1, blocking collectives, shards(): lax.all_to_all(pool.astype(jnp.bfloat16), 'rep', split_axis=0, concat_axi...  26.6 us
    all_to_all x1, starting transfers between devices, shards(): lax.all_to_all(jnp.broadcast_to(rows_in[None], (n_blk,) + rows_in.shape),...  11.4 us
    dot_general x4, matrix products, shards(): jnp.dot(block_rows, weight_cols, preferred_element_type=jnp.float32)  10.8 us
    all_to_all x1, starting transfers between devices, shards(): lax.all_to_all(buffer.astype(jnp.bfloat16), 'rep', split_axis=0, concat_a...  8.73 us
    all_to_all x1, waiting for transfers between devices, shards(): lax.all_to_all(buffer.astype(jnp.bfloat16), 'rep', split_axis=0, concat_a...  7.18 us
    scatter x1, local copies, waits for them, and re-layouts, shards(): jnp.zeros(pool.shape, jnp.float32).at[slot_index].set(accepted_state)  6.2 us
  transfers between devices with their start and end apart: 3, of which 3 were waited for; matrix products, arithmetic and copies ran while one was open for 12% of the time, Pallas kernels for 0%

profile of v1, /device:TPU:1, one launch (start us, length us, event | category | flops | bytes accessed | tf_op | source)
XLA Modules:
  0.0 243.1 jit_solution(15091095089696268387)
XLA Ops:
  0.6 2.4 convert_element_type.115
  3.0 26.6 %all_to_all.20 = bf16[48,2,64,128]{3,2,1,0:T(8,128)(2,1)S(1)} all-to-all(bf16[48,2,64,128]{3,2,1,0:T(8,128)(2,1)S(1)} %convert_element_type.115), channel_id=1, replica_groups=mesh['blk'=32,'rep'=8] {'rep'}, dimensions={0} | all-to-all | bytes 3145728 | tf_op jit(solution)/shard_map/all_to_all | solution.py:119
  29.6 1.8 broadcast_in_dim.32
  31.5 11.4 %all-to-all-start = ((bf16[32,16,2560]{2,1,0:T(8,128)(2,1)}), bf16[32,16,2560]{2,1,0:T(8,128)(2,1)}, u32[]{:S(2)}, u32[]{:S(2)}) async-start(bf16[32,16,2560]{2,1,0:T(8,128)(2,1)} %broadcast_in_dim.32), calls=%async_computation | async-start | bytes 5242880 | tf_op jit(solution)/shard_map/all_to_all | solution.py:52
  43.2 0.6 copy.81
  44.0 0.6 compare_reduce_fusion.1
  44.6 0.7 compare_reduce_fusion
  45.3 0.6 iota_compare_fusion.5
  47.6 0.6 slice_bitcast_fusion.4
  48.2 0.6 fusion.55
  48.8 0.7 copy_multiply_fusion
  49.5 2.1 convert_element_type.116
  51.6 2.6 %gather_fusion = f32[32,2,64,128]{3,2,1,0:T(8,128)S(1)} fusion(f32[48,2,64,128]{3,2,1,0:T(8,128)} %convert_element_type.116, s32[1024]{0:T(1024)S(1)} %pad_clamp_fusion), kind=kCustom, calls=%fused_computation | custom fusion | bytes 4194432 | tf_op jit(solution)/shard_map/jit(_take)/gather | solution.py:122
  54.2 48.6 %all-to-all-done = bf16[32,16,2560]{2,1,0:T(8,128)(2,1)} async-done(((bf16[32,16,2560]{2,1,0:T(8,128)(2,1)}), bf16[32,16,2560]{2,1,0:T(8,128)(2,1)}, u32[]{:S(2)}, u32[]{:S(2)}) %all-to-all-start) | async-done | bytes 2621472 | tf_op jit(solution)/shard_map/all_to_all | solution.py:52
  102.8 2.5 %fusion.10 = f32[512,2]{0,1:T(2,128)S(1)} fusion(bf16[512,2560]{1,0:T(8,128)(2,1)} %bitcast.2, bf16[2560,2]{0,1:T(2,128)(2,1)S(1)} %copy-done.11), kind=kOutput, calls=%fused_computation.17 | convolution fusion | flops 5244928 | bytes 2635776 | tf_op jit(solution)/shard_map/dot_general | solution.py:57
  105.6 0.9 copy.83
  106.5 1.7 fusion.56
  108.2 1.7 copy.97
  109.9 1.8 copy.84
  111.7 1.7 multiply_reduce_fusion
  113.4 0.7 copy.96
  114.1 0.6 exp.50
  114.7 0.7 copy.86
  115.4 2.7 %convolution_convert_fusion.3 = bf16[512,128]{1,0:T(8,128)(2,1)S(1)} fusion(bf16[512,2560]{1,0:T(8,128)(2,1)} %bitcast.2, bf16[2560,128]{1,0:T(8,128)(2,1)} %param.25), kind=kOutput, calls=%fused_computation.15 | convolution fusion | flops 335609856 | bytes 3407872 | tf_op jit(solution)/shard_map/dot_general | solution.py:57
  118.1 0.8 maximum_convert_fusion.1
  119.1 0.9 reshape.239
  120.0 1.3 copy.91
  121.3 1.3 select_multiply_fusion
  122.6 0.8 copy.98
  123.4 2.6 %convolution_convert_fusion.1 = bf16[512,256]{1,0:T(8,128)(2,1)S(1)} fusion(bf16[512,2560]{1,0:T(8,128)(2,1)} %bitcast.2, bf16[2560,256]{1,0:T(8,128)(2,1)S(1)} %copy-done), kind=kOutput, calls=%fused_computation.12 | convolution fusion | flops 671219712 | bytes 4194304 | tf_op jit(solution)/shard_map/dot_general | solution.py:57
  126.6 0.9 fusion.40
  127.5 3.6 %multiply_add_fusion = f32[32,2,64,128]{3,2,1,0:T(8,128)} fusion(f32[32,2,64,128]{3,2,1,0:T(8,128)S(1)} %gather_fusion, f32[32,2]{1,0:T(8,128)S(1)} %copy-done.6, pred[32]{0:T(512)(128)(4,1)S(1)} %copy-done.14, f32[32,16,2]{1,2,0:T(2,128)S(1)} %copy.98, bf16[32,16,2,64]{3,2,1,0:T(2,128)(2,1)S(1)} %copy-done.2, bf16[32,16,256]{2,1,0:T(8,128)(2,1)S(1)} %multiply_convert_fusion), kind=kOutput, calls=%fused_computation.5 | convolution fusion | flops 102367232 | bytes 4637184 | tf_op jit(solution)/shard_map/rsh,rshp,rsn->rhpn/dot_general | solution.py:126
  131.1 2.1 broadcast_in_dim.37
  133.1 6.2 %scatter_fusion = f32[48,2,64,128]{3,2,1,0:T(8,128)} fusion(f32[48,2,64,128]{3,2,1,0:T(8,128)} %broadcast_in_dim.37, s32[32]{0:T(128)S(1)} %bitcast.65, f32[32,2,64,128]{3,2,1,0:T(8,128)} %multiply_add_fusion), kind=kCustom, calls=%fused_computation.1 | custom fusion | bytes 6291584 | tf_op jit(solution)/shard_map/scatter | solution.py:129
  139.3 3.4 %convert_element_type.126 = bf16[48,2,64,128]{3,2,1,0:T(8,128)(2,1)} convert(f32[48,2,64,128]{3,2,1,0:T(8,128)} %scatter_fusion) | non-fusion elementwise | flops 786432 | bytes 4718592 | tf_op jit(solution)/shard_map/convert_element_type | solution.py:131
  142.8 8.7 %all-to-all-start.3 = ((bf16[48,2,64,128]{3,2,1,0:T(8,128)(2,1)}), bf16[48,2,64,128]{3,2,1,0:T(8,128)(2,1)}, u32[]{:S(2)}, u32[]{:S(2)}) async-start(bf16[48,2,64,128]{3,2,1,0:T(8,128)(2,1)} %convert_element_type.126), calls=%async_computation.3 | async-start | bytes 3145728 | tf_op jit(solution)/shard_map/all_to_all | solution.py:130
  151.5 1.7 fusion.8
  153.2 3.5 %fusion.5 = f32[32,16,2,64]{3,1,2,0:T(8,128)S(1)} fusion(f32[32,16,2,64]{3,1,2,0:T(8,128)S(1)} %fusion.8, f32[32,2,64,128]{3,2,1,0:T(8,128)S(1)} %gather_fusion, pred[32]{0:T(512)(128)(4,1)S(1)} %copy-done.14, f32[32,16,2]{1,2,0:T(2,128)S(1)} %copy.91, bf16[32,16,256]{2,1,0:T(8,128)(2,1)} %copy-done.1), kind=kOutput, calls=%fused_computation.9 | convolution fusion | flops 101318656 | bytes 2756640 | tf_op jit(solution)/shard_map/rhpn,rtn->rthp/dot_general | solution.py:123
  157.5 3.0 %multiply_reduce_fusion.1 = (f32[512]{0:T(512)S(1)}, f32[512,128]{0,1:T(8,128)S(1)}) fusion(f32[512,128]{0,1:T(8,128)S(1)} %copy.93, bf16[512,2560]{1,0:T(8,128)(2,1)} %bitcast.2, bf16[2560,128]{1,0:T(8,128)(2,1)} %param.24), kind=kOutput, calls=%fused_computation.47 | convolution fusion | flops 336133632 | bytes 3803136 | tf_op jit(solution)/shard_map/dot_general | solution.py:57
  160.7 1.3 fusion.35
  162.5 0.9 convolution_convert_fusion
  163.4 1.7 pad_maximum_fusion
  165.1 7.2 %all-to-all-done.3 = bf16[48,2,64,128]{3,2,1,0:T(8,128)(2,1)} async-done(((bf16[48,2,64,128]{3,2,1,0:T(8,128)(2,1)}), bf16[48,2,64,128]{3,2,1,0:T(8,128)(2,1)}, u32[]{:S(2)}, u32[]{:S(2)}) %all-to-all-start.3) | async-done | bytes 1572896 | tf_op jit(solution)/shard_map/all_to_all | solution.py:130
  172.3 4.8 %all-to-all-start.2 = ((bf16[32,16,2688]{2,1,0:T(8,128)(2,1)}), bf16[32,16,2688]{2,1,0:T(8,128)(2,1)}, u32[]{:S(2)}, u32[]{:S(2)}) async-start(bf16[32,16,2688]{2,1,0:T(8,128)(2,1)} %bitcast.60), calls=%async_computation.2 | async-start | bytes 5505024 | tf_op jit(solution)/shard_map/all_to_all | solution.py:144
  177.2 3.5 %convert_element_type.127 = f32[48,2,64,128]{3,2,1,0:T(8,128)} convert(bf16[48,2,64,128]{3,2,1,0:T(8,128)(2,1)} %all-to-all-done.3) | non-fusion elementwise | flops 786432 | bytes 4718592 | tf_op jit(solution)/shard_map/convert_element_type | solution.py:132
  180.6 59.3 %all-to-all-done.2 = bf16[32,16,2688]{2,1,0:T(8,128)(2,1)} async-done(((bf16[32,16,2688]{2,1,0:T(8,128)(2,1)}), bf16[32,16,2688]{2,1,0:T(8,128)(2,1)}, u32[]{:S(2)}, u32[]{:S(2)}) %all-to-all-start.2) | async-done | bytes 2752544 | tf_op jit(solution)/shard_map/all_to_all | solution.py:144
  240.0 2.2 convert_reduce_fusion
  242.4 0.7 fusion.44
  (97 shorter events, 4.6 us)
Async XLA Ops:
  0.6 122.8 %copy-start = (bf16[2560,256]{1,0:T(8,128)(2,1)S(1)}, bf16[2560,256]{1,0:T(8,128)(2,1)}, u32[]{:S(2)}) copy-start(bf16[2560,256]{1,0:T(8,128)(2,1)} %param.26) | copy-start | bytes 3932164
  3.0 26.6 %copy-start.5 = (bf16[1,16,2560]{2,1,0:T(8,128)(2,1)S(1)}, bf16[1,16,2560]{2,1,0:T(8,128)(2,1)}, u32[]{:S(2)}) copy-start(bf16[1,16,2560]{2,1,0:T(8,128)(2,1)} %param.23) | copy-start | bytes 245764
  31.4 11.5 %copy-start.27 = (s32[32]{0:T(128)S(1)}, s32[32]{0:T(128)}, u32[]{:S(2)}) copy-start(s32[32]{0:T(128)} %param.41) | copy-start | bytes 388
  31.4 11.7 %copy-start.10 = (bf16[32,3,128]{2,0,1:T(8,128)(2,1)S(1)}, bf16[32,3,128]{2,0,1:T(8,128)(2,1)}, u32[]{:S(2)}) copy-start(bf16[32,3,128]{2,0,1:T(8,128)(2,1)} %param.35) | copy-start | bytes 73732
  31.4 12.4 %copy-start.31 = (s32[4]{0:T(128)S(1)}, s32[4]{0:T(128)}, u32[]{:S(2)}) copy-start(s32[4]{0:T(128)} %param.38) | copy-start | bytes 52
  31.4 14.5 %copy-start.28 = (s32[32,1]{0,1:T(1,128)S(1)}, s32[32,1]{0,1:T(1,128)}, u32[]{:S(2)}) copy-start(s32[32,1]{0,1:T(1,128)} %param.39) | copy-start | bytes 388
  31.4 15.3 %copy-start.32 = (f32[2]{0:T(128)S(1)}, f32[2]{0:T(128)}, u32[]{:S(2)}) copy-start(f32[2]{0:T(128)} %param.31) | copy-start | bytes 28
  31.4 15.3 %copy-start.26 = (s32[32]{0:T(128)S(1)}, s32[32]{0:T(128)}, u32[]{:S(2)}) copy-start(s32[32]{0:T(128)} %param.40) | copy-start | bytes 388
  31.4 15.9 %copy-start.30 = (f32[4,2]{0,1:T(2,128)S(1)}, f32[4,2]{0,1:T(2,128)}, u32[]{:S(2)}) copy-start(f32[4,2]{0,1:T(2,128)} %param.30) | copy-start | bytes 100
  31.5 16.1 %copy-start.24 = (f32[4,128]{1,0:T(4,128)S(1)}, f32[4,128]{1,0:T(4,128)}, u32[]{:S(2)}) copy-start(f32[4,128]{1,0:T(4,128)} %param.28) | copy-start | bytes 6148
  31.5 16.7 %copy-start.19 = (f32[4,256]{1,0:T(4,128)S(1)}, f32[4,256]{1,0:T(4,128)}, u32[]{:S(2)}) copy-start(f32[4,256]{1,0:T(4,128)} %param.29) | copy-start | bytes 12292
  31.5 17.3 %copy-start.7 = (bf16[32,3,256]{2,0,1:T(8,128)(2,1)S(1)}, bf16[32,3,256]{2,0,1:T(8,128)(2,1)}, u32[]{:S(2)}) copy-start(bf16[32,3,256]{2,0,1:T(8,128)(2,1)} %param.36) | copy-start | bytes 147460
  31.5 71.3 %all-to-all-start = ((bf16[32,16,2560]{2,1,0:T(8,128)(2,1)}), bf16[32,16,2560]{2,1,0:T(8,128)(2,1)}, u32[]{:S(2)}, u32[]{:S(2)}) async-start(bf16[32,16,2560]{2,1,0:T(8,128)(2,1)} %broadcast_in_dim.32), calls=%async_computation | async-start | bytes 5242880 | tf_op jit(solution)/shard_map/all_to_all | solution.py:52
  46.7 2.9 %copy-start.12 = (s32[32,1]{0,1:T(1,128)}, s32[32,1]{0,1:T(1,128)S(1)}, u32[]{:S(2)}) copy-start(s32[32,1]{0,1:T(1,128)S(1)} %get-tuple-element.27) | copy-start | bytes 388
  51.6 51.2 %copy-start.11 = (bf16[2560,2]{0,1:T(2,128)(2,1)S(1)}, bf16[2560,2]{0,1:T(2,128)(2,1)}, u32[]{:S(2)}) copy-start(bf16[2560,2]{0,1:T(2,128)(2,1)} %param.27) | copy-start | bytes 30724
  115.4 3.5 %copy-start.20 = (f32[128]{0:T(128)S(1)}, f32[128]{0:T(128)}, u32[]{:S(2)}) copy-start(f32[128]{0:T(128)} %get-tuple-element.38) | copy-start | bytes 1540
  115.4 3.6 %copy-start.21 = (f32[128]{0:T(128)S(1)}, f32[128]{0:T(128)}, u32[]{:S(2)}) copy-start(f32[128]{0:T(128)} %get-tuple-element.39) | copy-start | bytes 1540
  115.4 3.6 %copy-start.22 = (f32[128]{0:T(128)S(1)}, f32[128]{0:T(128)}, u32[]{:S(2)}) copy-start(f32[128]{0:T(128)} %get-tuple-element.40) | copy-start | bytes 1540
  115.4 3.6 %copy-start.23 = (f32[128]{0:T(128)S(1)}, f32[128]{0:T(128)}, u32[]{:S(2)}) copy-start(f32[128]{0:T(128)} %get-tuple-element.41) | copy-start | bytes 1540
  120.0 6.1 %copy-start.4 = (bf16[32,3,256]{2,1,0:T(4,128)(2,1)S(1)}, bf16[32,3,256]{2,1,0:T(4,128)(2,1)}, u32[]{:S(2)}) copy-start(bf16[32,3,256]{2,1,0:T(4,128)(2,1)} %copy_multiply_fusion) | copy-start | bytes 147460
  123.4 2.8 %copy-start.15 = (f32[1,256]{1,0:T(1,128)S(1)}, f32[1,256]{1,0:T(1,128)}, u32[]{:S(2)}) copy-start(f32[1,256]{1,0:T(1,128)} %get-tuple-element.34) | copy-start | bytes 3076
  123.4 2.8 %copy-start.16 = (f32[1,256]{1,0:T(1,128)S(1)}, f32[1,256]{1,0:T(1,128)}, u32[]{:S(2)}) copy-start(f32[1,256]{1,0:T(1,128)} %get-tuple-element.35) | copy-start | bytes 3076
  123.4 2.8 %copy-start.17 = (f32[1,256]{1,0:T(1,128)S(1)}, f32[1,256]{1,0:T(1,128)}, u32[]{:S(2)}) copy-start(f32[1,256]{1,0:T(1,128)} %get-tuple-element.36) | copy-start | bytes 3076
  123.4 2.8 %copy-start.18 = (f32[1,256]{1,0:T(1,128)S(1)}, f32[1,256]{1,0:T(1,128)}, u32[]{:S(2)}) copy-start(f32[1,256]{1,0:T(1,128)} %get-tuple-element.37) | copy-start | bytes 3076
  126.0 1.5 copy-start.2
  126.0 1.5 copy-start.6
  126.0 1.4 copy-start.14
  126.5 0.9 copy-start.1
  131.1 2.1 copy-start.13
  142.8 8.7 %copy-start.8 = (f32[32,16,2]{1,2,0:T(2,128)S(1)}, f32[32,16,2]{1,2,0:T(2,128)}, u32[]{:S(2)}) copy-start(f32[32,16,2]{1,2,0:T(2,128)} %copy.84) | copy-start | bytes 12292
  142.8 8.7 %copy-start.9 = (f32[32,16,2]{1,2,0:T(2,128)S(1)}, f32[32,16,2]{1,2,0:T(2,128)}, u32[]{:S(2)}) copy-start(f32[32,16,2]{1,2,0:T(2,128)} %copy.86) | copy-start | bytes 12292
  142.8 8.7 %copy-start.25 = (pred[16,16]{1,0:T(8,128)(4,1)S(1)}, pred[16,16]{1,0:T(8,128)(4,1)}, u32[]{:S(2)}) copy-start(pred[16,16]{1,0:T(8,128)(4,1)} %iota_compare_fusion.5) | copy-start | bytes 772
  142.8 8.8 %copy-start.33 = (f32[2]{0:T(128)S(1)}, f32[2]{0:T(128)}, u32[]{:S(2)}) copy-start(f32[2]{0:T(128)} %param.32) | copy-start | bytes 28
  142.8 29.6 %all-to-all-start.3 = ((bf16[48,2,64,128]{3,2,1,0:T(8,128)(2,1)}), bf16[48,2,64,128]{3,2,1,0:T(8,128)(2,1)}, u32[]{:S(2)}, u32[]{:S(2)}) async-start(bf16[48,2,64,128]{3,2,1,0:T(8,128)(2,1)} %convert_element_type.126), calls=%async_computation.3 | async-start | bytes 3145728 | tf_op jit(solution)/shard_map/all_to_all | solution.py:130
  157.5 5.0 %copy-start.3 = (bf16[128,2560]{1,0:T(8,128)(2,1)S(1)}, bf16[128,2560]{1,0:T(8,128)(2,1)}, u32[]{:S(2)}) copy-start(bf16[128,2560]{1,0:T(8,128)(2,1)} %param.34) | copy-start | bytes 1966084
  157.5 5.0 %copy-start.29 = (f32[128]{0:T(128)S(1)}, f32[128]{0:T(128)}, u32[]{:S(2)}) copy-start(f32[128]{0:T(128)} %param.33) | copy-start | bytes 1540
  172.3 67.7 %all-to-all-start.2 = ((bf16[32,16,2688]{2,1,0:T(8,128)(2,1)}), bf16[32,16,2688]{2,1,0:T(8,128)(2,1)}, u32[]{:S(2)}, u32[]{:S(2)}) async-start(bf16[32,16,2688]{2,1,0:T(8,128)(2,1)} %bitcast.60), calls=%async_computation.2 | async-start | bytes 5505024 | tf_op jit(solution)/shard_map/all_to_all | solution.py:144

commit v2 on v1

--- a/solution.py
+++ b/solution.py
@@ -1,7 +1,63 @@
+import functools
+
 import jax
 import jax.numpy as jnp
 from jax import lax
+from jax.experimental import pallas as pl
+from jax.experimental.pallas import tpu as pltpu
 from jax.sharding import PartitionSpec as P
+
+MESH = pl.DeviceIdType.MESH
+AXES = ("blk", "rep")
+
+
+def exchange_kernel(n, axis, gather, src_ref, dst_ref, send_sem, recv_sem, local_sem):
+    me = lax.axis_index(axis)
+    coords = {name: lax.axis_index(name) for name in AXES}
+
+    def device_of(peer):
+        return tuple(peer if name == axis else coords[name] for name in AXES)
+
+    barrier = pltpu.get_barrier_semaphore()
+    for offset in range(1, n):
+        peer = lax.rem(me + offset, n)
+        pl.semaphore_signal(barrier, inc=1, device_id=device_of(peer), device_id_type=MESH)
+    pl.semaphore_wait(barrier, n - 1)
+    local = pltpu.make_async_copy(src_ref if gather else src_ref.at[me], dst_ref.at[me], local_sem)
+    local.start()
+    copies = []
+    for offset in range(1, n):
+        peer = lax.rem(me + offset, n)
+        copy = pltpu.make_async_remote_copy(
+            src_ref=src_ref if gather else src_ref.at[peer],
+            dst_ref=dst_ref.at[me],
+            send_sem=send_sem.at[offset],
+            recv_sem=recv_sem.at[offset],
+            device_id=device_of(peer),
+            device_id_type=MESH,
+        )
+        copy.start()
+        copies.append(copy)
+    local.wait()
+    for copy in copies:
+        copy.wait()
+
+
+def exchange(src, axis, gather, collective_id):
+    n = lax.axis_size(axis)
+    block = src.shape if gather else src.shape[1:]
+    return pl.pallas_call(
+        functools.partial(exchange_kernel, n, axis, gather),
+        out_shape=jax.ShapeDtypeStruct((n,) + tuple(block), src.dtype),
+        in_specs=[pl.BlockSpec(memory_space=pl.ANY)],
+        out_specs=pl.BlockSpec(memory_space=pl.ANY),
+        scratch_shapes=[
+            pltpu.SemaphoreType.DMA((n,)),
+            pltpu.SemaphoreType.DMA((n,)),
+            pltpu.SemaphoreType.DMA,
+        ],
+        compiler_params=pltpu.CompilerParams(collective_id=collective_id, has_side_effects=True),
+    )(src)
 
 
 def convolve(edge_cells, fresh_cells, kernel, edge_mask):
@@ -49,9 +105,7 @@
     cap_group = slots_here // lax.axis_size("rep")
     weights_in = (w_z, w_x, w_dt, w_bc)
     n_blk = lax.axis_size("blk")
-    block_rows = lax.all_to_all(
-        jnp.broadcast_to(rows_in[None], (n_blk,) + rows_in.shape), "blk", 0, 0, tiled=True
-    ).reshape(n_blk * local_rows, rows_in.shape[1])
+    block_rows = exchange(rows_in, "blk", True, 0).reshape(n_blk * local_rows, rows_in.shape[1])
     projected = jnp.concatenate(
         [
             jnp.dot(block_rows, weight_cols, preferred_element_type=jnp.float32)
@@ -141,7 +195,7 @@
     extra = jnp.zeros((partial.shape[0], 128), jnp.bfloat16)
     extra = extra.at[:, 0].set(sq_hi).at[:, 1].set(sq_lo)
     packed = jnp.concatenate([partial, extra], 1).reshape(n_blk, local_rows, width + 128)
-    arrived = lax.all_to_all(packed, "blk", 0, 0, tiled=True).astype(jnp.float32)
+    arrived = exchange(packed, "blk", False, 1).astype(jnp.float32)
     summed = jnp.sum(arrived, axis=0)
     inner_all = inner_here * n_blk
     mean_sq = (summed[:, width] + summed[:, width + 1]) / inner_all

time: 246 us -> 223 us (0.907)
  Pallas kernels: 0 us -> 139 us
  waiting for transfers between devices: 115 us -> 0.01 us
  blocking collectives: 26.6 us -> 0 us
  starting transfers between devices: 24.9 us -> 11.3 us
  local copies, waits for them, and re-layouts: 25.5 us -> 22.1 us
  other arithmetic: 28.1 us -> 24.8 us
    pallas_call x0 -> x2, Pallas kernels: none -> 139 us  [exchange(): pl.pallas_call(functools.partial(exchange_kernel, n, axis, gather), out_s...]
    all_to_all x2 -> x1, waiting for transfers between devices: 108 us -> 0.01 us  [shards(): lax.all_to_all(pool.astype(jnp.bfloat16), 'rep', split_axis=0, concat_axi...]
    all_to_all x1 -> x0, blocking collectives: 26.6 us -> none  [shards(): lax.all_to_all(pool.astype(jnp.bfloat16), 'rep', split_axis=0, concat_axi...]
    all_to_all x2 -> x1, starting transfers between devices: 16.2 us -> 6.87 us  [shards(): lax.all_to_all(pool.astype(jnp.bfloat16), 'rep', split_axis=0, concat_axi...]
    all_to_all x1, waiting for transfers between devices: 7.18 us -> 0.01 us  [shards(): lax.all_to_all(buffer.astype(jnp.bfloat16), 'rep', split_axis=0, concat_a...]
    all_to_all x1, starting transfers between devices: 8.73 us -> 4.4 us  [shards(): lax.all_to_all(buffer.astype(jnp.bfloat16), 'rep', split_axis=0, concat_a...]
    reshape x2, local copies, waits for them, and re-layouts: 0.43 us -> 3.83 us  [shards(): y_total = (y_local + y_prior).reshape(n_req * drafts, inner_here)]
  transfers between devices with their start and end apart: 3 -> 2, of which waited for: 3 -> 0; matrix products, arithmetic and copies ran while one was open for 12% -> 14% of each run, Pallas kernels for 0% -> 63%
where the time goes in v2:
time: 223 us; the launch traced here: 222 us
  Pallas kernels  139 us (62%)
  other arithmetic  24.8 us (11%)
  matrix products  23.6 us (11%)
  local copies, waits for them, and re-layouts  22.1 us (10%)
  starting transfers between devices  11.3 us (5%)
    pallas_call x2, Pallas kernels, exchange(): pl.pallas_call(functools.partial(exchange_kernel, n, axis, gather), out_s...  139 us
    dot_general x4, matrix products, shards(): jnp.dot(block_rows, weight_cols, preferred_element_type=jnp.float32)  11.5 us
    all_to_all x1, starting transfers between devices, shards(): lax.all_to_all(pool.astype(jnp.bfloat16), 'rep', split_axis=0, concat_axi...  6.87 us
    scatter x1, local copies, waits for them, and re-layouts, shards(): jnp.zeros(pool.shape, jnp.float32).at[slot_index].set(accepted_state)  5.34 us
    dot_general x1, matrix products, shards(): jnp.einsum('rsh,rshp,rsn->rhpn', coef, x_heads, b_float, precision=highest)  4.53 us
  transfers between devices with their start and end apart: 2, of which 0 were waited for; matrix products, arithmetic and copies ran while one was open for 14% of the time, Pallas kernels for 63%

profile of v2, /device:TPU:1, one launch (start us, length us, event | category | flops | bytes accessed | tf_op | source)
XLA Modules:
  0.0 222.2 jit_solution(3413623393199449188)
XLA Ops:
  0.6 3.5 %convert_element_type.115 = bf16[48,2,64,128]{3,2,1,0:T(8,128)(2,1)} convert(f32[48,2,64,128]{3,2,1,0:T(8,128)} %param.37) | non-fusion elementwise | flops 786432 | bytes 4718592 | tf_op jit(solution)/shard_map/convert_element_type | solution.py:174
  4.2 6.9 %all-to-all-start = ((bf16[48,2,64,128]{3,2,1,0:T(8,128)(2,1)}), bf16[48,2,64,128]{3,2,1,0:T(8,128)(2,1)S(1)}, u32[]{:S(2)}, u32[]{:S(2)}) async-start(bf16[48,2,64,128]{3,2,1,0:T(8,128)(2,1)} %convert_element_type.115), calls=%async_computation | async-start | bytes 3145728 | tf_op jit(solution)/shard_map/all_to_all | solution.py:173
  11.1 0.7 compare_reduce_fusion.1
  11.8 0.7 compare_reduce_fusion
  12.4 0.6 iota_compare_fusion.3
  13.0 0.6 iota_compare_fusion.5
  13.8 71.7 %shard_map.194 = bf16[32,16,2560]{2,1,0:T(8,128)(2,1)} custom-call(bf16[16,2560]{1,0:T(8,128)(2,1)} %bitcast.67), custom_call_target="tpu_custom_call" | custom-call | tf_op jit(solution)/shard_map/pallas_call | solution.py:49
  85.6 2.5 %fusion.10 = f32[512,2]{0,1:T(2,128)S(1)} fusion(bf16[512,2560]{1,0:T(8,128)(2,1)} %bitcast.61, bf16[2560,2]{0,1:T(2,128)(2,1)S(1)} %copy-done.10), kind=kOutput, calls=%fused_computation.17 | convolution fusion | flops 5244928 | bytes 2635776 | tf_op jit(solution)/shard_map/dot_general | solution.py:111
  88.8 0.7 fusion.56
  89.6 0.8 copy.97
  90.3 0.9 copy.84
  91.4 0.6 copy.96
  91.9 0.6 exp.50
  92.7 0.6 and_bitcast_fusion
  93.3 0.6 pad_clamp_fusion
  94.0 0.7 copy.87
  94.8 0.7 copy.86
  95.5 2.7 %convolution_convert_fusion.3 = bf16[512,128]{1,0:T(8,128)(2,1)S(1)} fusion(bf16[512,2560]{1,0:T(8,128)(2,1)} %bitcast.62, bf16[2560,128]{1,0:T(8,128)(2,1)} %param.25), kind=kOutput, calls=%fused_computation.15 | convolution fusion | flops 335609856 | bytes 3407872 | tf_op jit(solution)/shard_map/dot_general | solution.py:111
  98.6 0.3 copy.91
  98.9 0.7 select_multiply_fusion
  99.7 0.9 copy_multiply_fusion
  100.6 2.6 %convolution_convert_fusion.1 = bf16[512,256]{1,0:T(8,128)(2,1)S(1)} fusion(bf16[512,2560]{1,0:T(8,128)(2,1)} %bitcast.63, bf16[2560,256]{1,0:T(8,128)(2,1)S(1)} %copy-done), kind=kOutput, calls=%fused_computation.12 | convolution fusion | flops 671219712 | bytes 4194304 | tf_op jit(solution)/shard_map/dot_general | solution.py:111
  103.4 0.3 multiply_convert_fusion
  103.7 0.2 fusion.40
  104.0 0.5 copy-done.2
  104.5 1.4 fusion.8
  105.9 2.1 convert_element_type.116
  107.9 2.7 %gather_fusion = f32[32,2,64,128]{3,2,1,0:T(8,128)S(1)} fusion(f32[48,2,64,128]{3,2,1,0:T(8,128)} %convert_element_type.116, s32[1024]{0:T(1024)} %pad_clamp_fusion), kind=kCustom, calls=%fused_computation | custom fusion | bytes 4194432 | tf_op jit(solution)/shard_map/jit(_take)/gather | solution.py:176
  110.6 3.8 %fusion.5 = f32[32,16,2,64]{3,1,2,0:T(8,128)S(1)} fusion(f32[32,16,2,64]{3,1,2,0:T(8,128)} %fusion.8, f32[32,2,64,128]{3,2,1,0:T(8,128)S(1)} %gather_fusion, pred[32]{0:T(512)(128)(4,1)S(1)} %copy-done.13, f32[32,16,2]{1,2,0:T(2,128)S(1)} %copy.91, bf16[32,16,256]{2,1,0:T(8,128)(2,1)} %copy-done.2), kind=kOutput, calls=%fused_computation.9 | convolution fusion | flops 101318656 | bytes 3018784 | tf_op jit(solution)/shard_map/rhpn,rtn->rthp/dot_general | solution.py:177
  114.4 1.1 copy.92
  115.5 2.0 reshape.242
  117.5 1.8 copy.93
  119.3 3.7 %multiply_reduce_fusion.1 = (f32[512]{0:T(512)S(1)}, f32[512,128]{0,1:T(8,128)}) fusion(f32[512,128]{0,1:T(8,128)} %copy.93, bf16[512,2560]{1,0:T(8,128)(2,1)} %bitcast.64, bf16[2560,128]{1,0:T(8,128)(2,1)} %param.24), kind=kOutput, calls=%fused_computation.47 | convolution fusion | flops 336133632 | bytes 3803136 | tf_op jit(solution)/shard_map/dot_general | solution.py:111
  123.0 0.9 copy.94
  123.9 4.5 %multiply_add_fusion = f32[32,2,64,128]{3,2,1,0:T(8,128)} fusion(f32[32,2,64,128]{3,2,1,0:T(8,128)S(1)} %gather_fusion, f32[32,2]{1,0:T(8,128)S(1)} %copy-done.6, pred[32]{0:T(512)(128)(4,1)S(1)} %copy-done.13, f32[32,16,2]{1,2,0:T(2,128)S(1)} %copy.98, bf16[32,16,2,64]{3,2,1,0:T(2,128)(2,1)} %copy-done.3, bf16[32,16,256]{2,1,0:T(8,128)(2,1)} %copy-done.2), kind=kOutput, calls=%fused_computation.5 | convolution fusion | flops 102367232 | bytes 4591904 | tf_op jit(solution)/shard_map/rsh,rshp,rsn->rhpn/dot_general | solution.py:180
  128.4 2.1 broadcast_in_dim.31
  130.5 5.3 %scatter_fusion = f32[48,2,64,128]{3,2,1,0:T(8,128)} fusion(f32[48,2,64,128]{3,2,1,0:T(8,128)} %broadcast_in_dim.31, s32[32]{0:T(128)S(1)} %bitcast.69, f32[32,2,64,128]{3,2,1,0:T(8,128)S(1)} %copy-done.1), kind=kCustom, calls=%fused_computation.1 | custom fusion | bytes 6291584 | tf_op jit(solution)/shard_map/scatter | solution.py:183
  135.9 3.4 %convert_element_type.126 = bf16[48,2,64,128]{3,2,1,0:T(8,128)(2,1)} convert(f32[48,2,64,128]{3,2,1,0:T(8,128)} %scatter_fusion) | non-fusion elementwise | flops 786432 | bytes 4718592 | tf_op jit(solution)/shard_map/convert_element_type | solution.py:185
  139.3 4.4 %all-to-all-start.1 = ((bf16[48,2,64,128]{3,2,1,0:T(8,128)(2,1)}), bf16[48,2,64,128]{3,2,1,0:T(8,128)(2,1)S(1)}, u32[]{:S(2)}, u32[]{:S(2)}) async-start(bf16[48,2,64,128]{3,2,1,0:T(8,128)(2,1)} %convert_element_type.126), calls=%async_computation.1 | async-start | bytes 3145728 | tf_op jit(solution)/shard_map/all_to_all | solution.py:184
  143.7 1.4 fusion.35
  145.1 0.4 scatter.18
  145.6 2.0 convolution_convert_fusion
  147.6 1.7 pad_maximum_fusion
  149.3 67.8 %shard_map.195 = bf16[32,16,2688]{2,1,0:T(8,128)(2,1)} custom-call(bf16[32,16,2688]{2,1,0:T(8,128)(2,1)} %bitcast.60), custom_call_target="tpu_custom_call" | custom-call | tf_op jit(solution)/shard_map/pallas_call | solution.py:49
  217.1 2.2 convert_reduce_fusion
  219.3 0.2 fusion.50
  219.5 0.7 fusion.44
  220.2 2.1 convert_element_type.127
  (77 shorter events, 2.2 us)
Async XLA Ops:
  0.6 100.0 %copy-start = (bf16[2560,256]{1,0:T(8,128)(2,1)S(1)}, bf16[2560,256]{1,0:T(8,128)(2,1)}, u32[]{:S(2)}) copy-start(bf16[2560,256]{1,0:T(8,128)(2,1)} %param.26) | copy-start | bytes 3932164
  4.2 8.3 %copy-start.17 = (s32[32]{0:T(128)S(1)}, s32[32]{0:T(128)}, u32[]{:S(2)}) copy-start(s32[32]{0:T(128)} %param.40) | copy-start | bytes 388
  4.2 9.4 %copy-start.22 = (f32[2]{0:T(128)S(1)}, f32[2]{0:T(128)}, u32[]{:S(2)}) copy-start(f32[2]{0:T(128)} %param.31) | copy-start | bytes 28
  4.2 9.4 %copy-start.23 = (s32[4]{0:T(128)S(1)}, s32[4]{0:T(128)}, u32[]{:S(2)}) copy-start(s32[4]{0:T(128)} %param.38) | copy-start | bytes 52
  4.2 81.4 %copy-start.10 = (bf16[2560,2]{0,1:T(2,128)(2,1)S(1)}, bf16[2560,2]{0,1:T(2,128)(2,1)}, u32[]{:S(2)}) copy-start(bf16[2560,2]{0,1:T(2,128)(2,1)} %param.27) | copy-start | bytes 30724
  4.2 101.7 %all-to-all-start = ((bf16[48,2,64,128]{3,2,1,0:T(8,128)(2,1)}), bf16[48,2,64,128]{3,2,1,0:T(8,128)(2,1)S(1)}, u32[]{:S(2)}, u32[]{:S(2)}) async-start(bf16[48,2,64,128]{3,2,1,0:T(8,128)(2,1)} %convert_element_type.115), calls=%async_computation | async-start | bytes 3145728 | tf_op jit(solution)/shard_map/all_to_all | solution.py:173
  13.8 74.6 %copy-start.21 = (f32[4,2]{0,1:T(2,128)S(1)}, f32[4,2]{0,1:T(2,128)}, u32[]{:S(2)}) copy-start(f32[4,2]{0,1:T(2,128)} %param.30) | copy-start | bytes 100
  85.5 7.0 %copy-start.18 = (s32[32,1]{0,1:T(1,128)S(1)}, s32[32,1]{0,1:T(1,128)}, u32[]{:S(2)}) copy-start(s32[32,1]{0,1:T(1,128)} %param.39) | copy-start | bytes 388
  85.5 7.8 %copy-start.15 = (f32[4,128]{1,0:T(4,128)S(1)}, f32[4,128]{1,0:T(4,128)}, u32[]{:S(2)}) copy-start(f32[4,128]{1,0:T(4,128)} %param.28) | copy-start | bytes 6148
  85.6 8.4 %copy-start.19 = (s32[32]{0:T(128)S(1)}, s32[32]{0:T(128)}, u32[]{:S(2)}) copy-start(s32[32]{0:T(128)} %param.41) | copy-start | bytes 388
  85.6 9.1 %copy-start.9 = (bf16[32,3,128]{2,0,1:T(8,128)(2,1)S(1)}, bf16[32,3,128]{2,0,1:T(8,128)(2,1)}, u32[]{:S(2)}) copy-start(bf16[32,3,128]{2,0,1:T(8,128)(2,1)} %param.35) | copy-start | bytes 73732
  93.3 0.7 copy-start.11
  98.6 5.4 %copy-start.3 = (bf16[32,16,2,64]{3,2,1,0:T(2,128)(2,1)}, bf16[32,16,2,64]{3,2,1,0:T(2,128)(2,1)S(1)}, u32[]{:S(2)}) copy-start(bf16[32,16,2,64]{3,2,1,0:T(2,128)(2,1)S(1)} %reshape.239) | copy-start | bytes 393220
  100.6 2.8 %copy-start.14 = (f32[4,256]{1,0:T(4,128)S(1)}, f32[4,256]{1,0:T(4,128)}, u32[]{:S(2)}) copy-start(f32[4,256]{1,0:T(4,128)} %param.29) | copy-start | bytes 12292
  103.2 1.2 copy-start.7
  103.2 1.2 copy-start.8
  103.2 1.2 copy-start.16
  103.3 1.2 copy-start.24
  103.7 0.7 copy-start.2
  107.9 2.7 %copy-start.13 = (pred[32]{0:T(512)(128)(4,1)S(1)}, pred[32]{0:T(512)(128)(4,1)}, u32[]{:S(2)}) copy-start(pred[32]{0:T(512)(128)(4,1)} %get-tuple-element.26) | copy-start | bytes 100
  115.5 8.4 %copy-start.6 = (f32[32,2]{1,0:T(8,128)S(1)}, f32[32,2]{1,0:T(8,128)}, u32[]{:S(2)}) copy-start(f32[32,2]{1,0:T(8,128)} %exp.50) | copy-start | bytes 772
  128.4 2.1 copy-start.1
  128.4 2.1 copy-start.12
  139.3 4.4 %copy-start.4 = (f32[512,1]{1,0:T(8,128)S(1)}, f32[512,1]{1,0:T(8,128)}, u32[]{:S(2)}) copy-start(f32[512,1]{1,0:T(8,128)} %copy.94) | copy-start | bytes 6148
  139.3 6.2 %copy-start.5 = (f32[512,128]{0,1:T(8,128)S(1)}, f32[512,128]{0,1:T(8,128)}, u32[]{:S(2)}) copy-start(f32[512,128]{0,1:T(8,128)} %get-tuple-element.43) | copy-start | bytes 786436
  139.3 6.2 %copy-start.20 = (f32[128]{0:T(128)S(1)}, f32[128]{0:T(128)}, u32[]{:S(2)}) copy-start(f32[128]{0:T(128)} %param.33) | copy-start | bytes 1540
  139.3 80.9 %all-to-all-start.1 = ((bf16[48,2,64,128]{3,2,1,0:T(8,128)(2,1)}), bf16[48,2,64,128]{3,2,1,0:T(8,128)(2,1)S(1)}, u32[]{:S(2)}, u32[]{:S(2)}) async-start(bf16[48,2,64,128]{3,2,1,0:T(8,128)(2,1)} %convert_element_type.126), calls=%async_computation.1 | async-start | bytes 3145728 | tf_op jit(solution)/shard_map/all_to_all | solution.py:184

commit v3 on v2

--- a/solution.py
+++ b/solution.py
@@ -8,7 +8,9 @@
 from jax.sharding import PartitionSpec as P
 
 MESH = pl.DeviceIdType.MESH
-AXES = ("blk", "rep")
+AXES = ("by", "bz", "rep")
+BLK = ("by", "bz")
+Y_CHIPS = 4
 
 
 def exchange_kernel(n, axis, gather, src_ref, dst_ref, send_sem, recv_sem, local_sem):
@@ -96,7 +98,7 @@
     rows_in = hidden_in[0]
     local_rows = rows_in.shape[0]
     n_req = edge_x.shape[0]
-    drafts = local_rows * lax.axis_size("blk") // n_req
+    drafts = local_rows * lax.axis_size(BLK) // n_req
     state_dim = w_bc.shape[1] // 2
     heads_here = w_dt.shape[1]
     inner_here = w_z.shape[1]
@@ -104,8 +106,9 @@
     slots_here = pool.shape[0]
     cap_group = slots_here // lax.axis_size("rep")
     weights_in = (w_z, w_x, w_dt, w_bc)
-    n_blk = lax.axis_size("blk")
-    block_rows = exchange(rows_in, "blk", True, 0).reshape(n_blk * local_rows, rows_in.shape[1])
+    n_blk = lax.axis_size(BLK)
+    along_z = exchange(rows_in, "bz", True, 0)
+    block_rows = exchange(along_z, "by", True, 1).reshape(n_blk * local_rows, rows_in.shape[1])
     projected = jnp.concatenate(
         [
             jnp.dot(block_rows, weight_cols, preferred_element_type=jnp.float32)
@@ -194,9 +197,16 @@
     width = partial.shape[1]
     extra = jnp.zeros((partial.shape[0], 128), jnp.bfloat16)
     extra = extra.at[:, 0].set(sq_hi).at[:, 1].set(sq_lo)
-    packed = jnp.concatenate([partial, extra], 1).reshape(n_blk, local_rows, width + 128)
-    arrived = exchange(packed, "blk", False, 1).astype(jnp.float32)
-    summed = jnp.sum(arrived, axis=0)
+    n_y = lax.axis_size("by")
+    packed = jnp.concatenate([partial, extra], 1).reshape(n_y, n_blk // n_y, local_rows, width + 128)
+    half_sum = jnp.sum(exchange(packed, "by", False, 2).astype(jnp.float32), axis=0)
+    sq_mid = half_sum[:, :, width] + half_sum[:, :, width + 1]
+    sq_mid_hi = sq_mid.astype(jnp.bfloat16)
+    sq_mid_lo = (sq_mid - sq_mid_hi.astype(jnp.float32)).astype(jnp.bfloat16)
+    half_packed = (
+        half_sum.astype(jnp.bfloat16).at[:, :, width].set(sq_mid_hi).at[:, :, width + 1].set(sq_mid_lo)
+    )
+    summed = jnp.sum(exchange(half_packed, "bz", False, 3).astype(jnp.float32), axis=0)
     inner_all = inner_here * n_blk
     mean_sq = (summed[:, width] + summed[:, width + 1]) / inner_all
     mixed = (summed[:, :width] * lax.rsqrt(mean_sq + 1e-05)[:, None]).astype(jnp.bfloat16)
@@ -225,10 +235,15 @@
         P("rep"),
         P("rep"),
     )
+    n_blk, n_rep = mesh.shape["blk"], mesh.shape["rep"]
+    split_mesh = jax.sharding.Mesh(
+        mesh.devices.reshape(Y_CHIPS, n_blk // Y_CHIPS, n_rep), AXES
+    )
+    placed = tuple(P(*[BLK if part == "blk" else part for part in spec]) for spec in placed)
     return jax.shard_map(
         shards,
-        mesh=mesh,
+        mesh=split_mesh,
         in_specs=placed,
-        out_specs=(P("rep", "blk", None), P("rep", "blk", None, None)),
+        out_specs=(P("rep", BLK, None), P("rep", BLK, None, None)),
         check_vma=False,
     )

time: 223 us -> 204 us (0.915)
  Pallas kernels: 139 us -> 109 us
  local copies, waits for them, and re-layouts: 22.1 us -> 27.2 us
  other arithmetic: 24.8 us -> 28.8 us
    pallas_call x2 -> x4, Pallas kernels: 139 us -> 109 us  [exchange(): pl.pallas_call(functools.partial(exchange_kernel, n, axis, gather), out_s...]
    scatter x0 -> x2, local copies, waits for them, and re-layouts: none -> 3.41 us  [shards(): half_sum.astype(jnp.bfloat16).at[:, :, width].set(sq_mid_hi)]
  transfers between devices with their start and end apart: 2 -> 2, of which waited for: 0 -> 0; matrix products, arithmetic and copies ran while one was open for 14% -> 16% of each run, Pallas kernels for 63% -> 37%
where the time goes in v3:
time: 204 us; the launch traced here: 203 us
  Pallas kernels  109 us (53%)
  other arithmetic  28.8 us (14%)
  local copies, waits for them, and re-layouts  27.2 us (13%)
  matrix products  23.7 us (12%)
  starting transfers between devices  12.6 us (6%)
    pallas_call x4, Pallas kernels, exchange(): pl.pallas_call(functools.partial(exchange_kernel, n, axis, gather), out_s...  109 us
    dot_general x4, matrix products, shards(): jnp.dot(block_rows, weight_cols, preferred_element_type=jnp.float32)  11.5 us
    all_to_all x1, starting transfers between devices, shards(): lax.all_to_all(pool.astype(jnp.bfloat16), 'rep', split_axis=0, concat_axi...  6.86 us
    all_to_all x1, starting transfers between devices, shards(): lax.all_to_all(buffer.astype(jnp.bfloat16), 'rep', split_axis=0, concat_a...  5.77 us
    scatter x1, local copies, waits for them, and re-layouts, shards(): jnp.zeros(pool.shape, jnp.float32).at[slot_index].set(accepted_state)  5.34 us
    dot_general x1, matrix products, shards(): jnp.einsum('rsh,rshp,rsn->rhpn', coef, x_heads, b_float, precision=highest)  4.54 us
    another operation x4, other arithmetic  4.54 us
  transfers between devices with their start and end apart: 2, of which 0 were waited for; matrix products, arithmetic and copies ran while one was open for 16% of the time, Pallas kernels for 37%

profile of v3, /device:TPU:1, one launch (start us, length us, event | category | flops | bytes accessed | tf_op | source)
XLA Modules:
  0.0 202.6 jit_solution(1337493782242552897)
XLA Ops:
  0.6 3.5 %convert_element_type.134 = bf16[48,2,64,128]{3,2,1,0:T(8,128)(2,1)} convert(f32[48,2,64,128]{3,2,1,0:T(8,128)} %param.41) | non-fusion elementwise | flops 786432 | bytes 4718592 | tf_op jit(solution)/shard_map/convert_element_type | solution.py:177
  4.2 6.9 %all-to-all-start = ((bf16[48,2,64,128]{3,2,1,0:T(8,128)(2,1)}), bf16[48,2,64,128]{3,2,1,0:T(8,128)(2,1)S(1)}, u32[]{:S(2)}, u32[]{:S(2)}) async-start(bf16[48,2,64,128]{3,2,1,0:T(8,128)(2,1)} %convert_element_type.134), calls=%async_computation | async-start | bytes 3145728 | tf_op jit(solution)/shard_map/all_to_all | solution.py:176
  11.0 0.7 compare_reduce_fusion.1
  11.7 0.7 compare_reduce_fusion
  12.4 0.6 iota_compare_fusion.3
  13.8 22.3 %shard_map.194.src_ref = bf16[8,16,2560]{2,1,0:T(8,128)(2,1)} custom-call(bf16[16,2560]{1,0:T(8,128)(2,1)} %bitcast.67), custom_call_target="tpu_custom_call" | custom-call | tf_op jit(solution)/shard_map/pallas_call | solution.py:51
  36.1 32.5 %shard_map.195 = bf16[4,8,16,2560]{3,2,1,0:T(8,128)(2,1)} custom-call(bf16[8,16,2560]{2,1,0:T(8,128)(2,1)} %shard_map.194.src_ref), custom_call_target="tpu_custom_call" | custom-call | tf_op jit(solution)/shard_map/pallas_call | solution.py:51
  68.7 2.5 %fusion.10 = f32[512,2]{0,1:T(2,128)S(1)} fusion(bf16[512,2560]{1,0:T(8,128)(2,1)} %bitcast.61, bf16[2560,2]{0,1:T(2,128)(2,1)S(1)} %copy-done.9), kind=kOutput, calls=%fused_computation.18 | convolution fusion | flops 5244928 | bytes 2635776 | tf_op jit(solution)/shard_map/dot_general | solution.py:114
  72.0 0.7 fusion.58
  72.7 0.8 copy.97
  73.5 0.9 copy.84
  74.5 0.7 copy.96
  75.2 0.6 exp.50
  76.5 0.6 pad_clamp_fusion
  77.1 0.7 copy.87
  77.9 0.7 copy.86
  78.6 2.7 %convolution_convert_fusion.3 = bf16[512,128]{1,0:T(8,128)(2,1)S(1)} fusion(bf16[512,2560]{1,0:T(8,128)(2,1)} %bitcast.62, bf16[2560,128]{1,0:T(8,128)(2,1)} %param.29), kind=kOutput, calls=%fused_computation.16 | convolution fusion | flops 335609856 | bytes 3407872 | tf_op jit(solution)/shard_map/dot_general | solution.py:114
  82.0 0.7 select_multiply_fusion
  82.8 0.7 copy.98
  83.5 0.9 copy_multiply_fusion
  84.4 2.6 %convolution_convert_fusion.1 = bf16[512,256]{1,0:T(8,128)(2,1)S(1)} fusion(bf16[512,2560]{1,0:T(8,128)(2,1)} %bitcast.63, bf16[2560,256]{1,0:T(8,128)(2,1)S(1)} %copy-done), kind=kOutput, calls=%fused_computation.13 | convolution fusion | flops 671219712 | bytes 4194304 | tf_op jit(solution)/shard_map/dot_general | solution.py:114
  88.2 1.4 fusion.8
  89.6 2.1 %convert_element_type.135 = f32[48,2,64,128]{3,2,1,0:T(8,128)} convert(bf16[48,2,64,128]{3,2,1,0:T(8,128)(2,1)S(1)} %all-to-all-done) | non-fusion elementwise | flops 786432 | bytes 4718592 | tf_op jit(solution)/shard_map/convert_element_type | solution.py:178
  91.7 2.7 %gather_fusion = f32[32,2,64,128]{3,2,1,0:T(8,128)S(1)} fusion(f32[48,2,64,128]{3,2,1,0:T(8,128)} %convert_element_type.135, s32[1024]{0:T(1024)} %pad_clamp_fusion), kind=kCustom, calls=%fused_computation | custom fusion | bytes 4194432 | tf_op jit(solution)/shard_map/jit(_take)/gather | solution.py:179
  94.4 3.8 %fusion.5 = f32[32,16,2,64]{3,1,2,0:T(8,128)S(1)} fusion(f32[32,16,2,64]{3,1,2,0:T(8,128)} %fusion.8, f32[32,2,64,128]{3,2,1,0:T(8,128)S(1)} %gather_fusion, pred[32]{0:T(512)(128)(4,1)S(1)} %copy-done.12, f32[32,16,2]{1,2,0:T(2,128)S(1)} %copy.91, bf16[32,16,256]{2,1,0:T(8,128)(2,1)} %copy-done.2), kind=kOutput, calls=%fused_computation.10 | convolution fusion | flops 101318656 | bytes 3018784 | tf_op jit(solution)/shard_map/rhpn,rtn->rthp/dot_general | solution.py:180
  98.1 1.1 copy.92
  99.2 2.1 %reshape.297 = f32[512,128]{1,0:T(8,128)} reshape(f32[32,16,2,64]{3,2,1,0:T(2,128)} %copy.92) | data formatting | bytes 524288 | tf_op jit(solution)/shard_map/reshape | solution.py:190
  101.2 1.8 copy.93
  103.0 3.7 %multiply_reduce_fusion.1 = (f32[512]{0:T(512)S(1)}, f32[512,128]{0,1:T(8,128)}) fusion(f32[512,128]{0,1:T(8,128)} %copy.93, bf16[512,2560]{1,0:T(8,128)(2,1)} %bitcast.64, bf16[2560,128]{1,0:T(8,128)(2,1)} %param.28), kind=kOutput, calls=%fused_computation.48 | convolution fusion | flops 336133632 | bytes 3803136 | tf_op jit(solution)/shard_map/dot_general | solution.py:114
  106.8 0.8 copy.94
  107.6 3.0 %fusion.35 = (bf16[512,1]{1,0:T(8,128)(2,1)}, bf16[512,1]{1,0:T(8,128)(2,1)S(1)}) fusion(f32[512,1]{1,0:T(8,128)} %copy.94, pred[]{:T(512)} %compare_reduce_fusion, pred[]{:T(512)} %compare_reduce_fusion.1), kind=kLoop, calls=%fused_computation.63 | loop fusion | flops 3072 | bytes 4098 | tf_op jit(solution)/shard_map/select.17
  110.6 1.5 scatter.21
  112.1 2.1 %convolution_convert_fusion = bf16[512,2560]{1,0:T(8,128)(2,1)S(1)} fusion(bf16[128,2560]{1,0:T(8,128)(2,1)} %param.38, f32[512,128]{0,1:T(8,128)} %get-tuple-element.69, f32[128]{0:T(128)S(1)} %copy-done.19), kind=kOutput, calls=%fused_computation.3 | convolution fusion | flops 336986112 | bytes 3539456 | tf_op jit(solution)/shard_map/dot_general | solution.py:196
  114.2 1.7 pad_maximum_fusion
  115.9 34.1 %shard_map.196 = bf16[4,8,16,2688]{3,2,1,0:T(8,128)(2,1)} custom-call(bf16[4,8,16,2688]{3,2,1,0:T(8,128)(2,1)} %bitcast.60), custom_call_target="tpu_custom_call" | custom-call | tf_op jit(solution)/shard_map/pallas_call | solution.py:51
  150.0 4.5 %multiply_add_fusion = f32[32,2,64,128]{3,2,1,0:T(8,128)} fusion(f32[32,2,64,128]{3,2,1,0:T(8,128)S(1)} %gather_fusion, f32[32,2]{1,0:T(8,128)S(1)} %copy-done.5, pred[32]{0:T(512)(128)(4,1)S(1)} %copy-done.12, f32[32,16,2]{1,2,0:T(2,128)S(1)} %copy-done.4, bf16[32,16,2,64]{3,2,1,0:T(2,128)(2,1)} %copy-done.3, bf16[32,16,256]{2,1,0:T(8,128)(2,1)} %copy-done.2), kind=kOutput, calls=%fused_computation.5 | convolution fusion | flops 102367232 | bytes 4591904 | tf_op jit(solution)/shard_map/rsh,rshp,rsn->rhpn/dot_general | solution.py:183
  154.6 2.1 %broadcast_in_dim.31 = f32[48,2,64,128]{3,2,1,0:T(8,128)} broadcast(f32[]{:T(128)} %constant.154.clone.1), dimensions={} | broadcast | bytes 3145732 | tf_op jit(solution)/shard_map/broadcast_in_dim | solution.py:186
  156.7 5.3 %scatter_fusion = f32[48,2,64,128]{3,2,1,0:T(8,128)} fusion(f32[48,2,64,128]{3,2,1,0:T(8,128)} %broadcast_in_dim.31, s32[32]{0:T(128)S(1)} %bitcast.69, f32[32,2,64,128]{3,2,1,0:T(8,128)S(1)} %copy-done.1), kind=kCustom, calls=%fused_computation.1 | custom fusion | bytes 6291584 | tf_op jit(solution)/shard_map/scatter | solution.py:186
  162.0 3.4 %convert_element_type.150 = bf16[48,2,64,128]{3,2,1,0:T(8,128)(2,1)} convert(f32[48,2,64,128]{3,2,1,0:T(8,128)} %scatter_fusion) | non-fusion elementwise | flops 786432 | bytes 4718592 | tf_op jit(solution)/shard_map/convert_element_type | solution.py:188
  165.5 5.8 %all-to-all-start.1 = ((bf16[48,2,64,128]{3,2,1,0:T(8,128)(2,1)}), bf16[48,2,64,128]{3,2,1,0:T(8,128)(2,1)S(1)}, u32[]{:S(2)}, u32[]{:S(2)}) async-start(bf16[48,2,64,128]{3,2,1,0:T(8,128)(2,1)} %convert_element_type.150), calls=%async_computation.1 | async-start | bytes 3145728 | tf_op jit(solution)/shard_map/all_to_all | solution.py:187
  171.3 2.4 %convert_reduce_fusion = f32[8,16,2688]{2,1,0:T(8,128)S(1)} fusion(bf16[4,8,16,2688]{3,2,1,0:T(8,128)(2,1)} %shard_map.196), kind=kLoop, calls=%fused_computation.2 | loop fusion | flops 2408448 | bytes 4128768 | tf_op jit(solution)/shard_map/reduce_sum | solution.py:202
  173.6 0.9 convert_element_type.143
  174.6 1.4 scatter.24
  176.1 2.0 scatter.30.src_ref
  178.0 20.4 %shard_map.197 = bf16[8,16,2688]{2,1,0:T(8,128)(2,1)} custom-call(bf16[8,16,2688]{2,1,0:T(8,128)(2,1)} %scatter.30.src_ref), custom_call_target="tpu_custom_call" | custom-call | tf_op jit(solution)/shard_map/pallas_call | solution.py:51
  198.4 1.2 convert_reduce_fusion.1
  199.8 0.7 fusion.44
  200.6 2.1 %convert_element_type.151 = f32[48,2,64,128]{3,2,1,0:T(8,128)} convert(bf16[48,2,64,128]{3,2,1,0:T(8,128)(2,1)S(1)} %all-to-all-done.1) | non-fusion elementwise | flops 786432 | bytes 4718592 | tf_op jit(solution)/shard_map/convert_element_type | solution.py:189
  (82 shorter events, 4.7 us)
Async XLA Ops:
  0.6 83.7 %copy-start = (bf16[2560,256]{1,0:T(8,128)(2,1)S(1)}, bf16[2560,256]{1,0:T(8,128)(2,1)}, u32[]{:S(2)}) copy-start(bf16[2560,256]{1,0:T(8,128)(2,1)} %param.30) | copy-start | bytes 3932164
  4.2 8.2 %copy-start.16 = (s32[32]{0:T(128)S(1)}, s32[32]{0:T(128)}, u32[]{:S(2)}) copy-start(s32[32]{0:T(128)} %param.44) | copy-start | bytes 388
  4.2 9.4 %copy-start.21 = (f32[2]{0:T(128)S(1)}, f32[2]{0:T(128)}, u32[]{:S(2)}) copy-start(f32[2]{0:T(128)} %param.35) | copy-start | bytes 28
  4.2 9.4 %copy-start.22 = (s32[4]{0:T(128)S(1)}, s32[4]{0:T(128)}, u32[]{:S(2)}) copy-start(s32[4]{0:T(128)} %param.42) | copy-start | bytes 52
  4.2 85.4 %all-to-all-start = ((bf16[48,2,64,128]{3,2,1,0:T(8,128)(2,1)}), bf16[48,2,64,128]{3,2,1,0:T(8,128)(2,1)S(1)}, u32[]{:S(2)}, u32[]{:S(2)}) async-start(bf16[48,2,64,128]{3,2,1,0:T(8,128)(2,1)} %convert_element_type.134), calls=%async_computation | async-start | bytes 3145728 | tf_op jit(solution)/shard_map/all_to_all | solution.py:176
  11.0 57.7 %copy-start.9 = (bf16[2560,2]{0,1:T(2,128)(2,1)S(1)}, bf16[2560,2]{0,1:T(2,128)(2,1)}, u32[]{:S(2)}) copy-start(bf16[2560,2]{0,1:T(2,128)(2,1)} %param.31) | copy-start | bytes 30724
  36.1 35.4 %copy-start.20 = (f32[4,2]{0,1:T(2,128)S(1)}, f32[4,2]{0,1:T(2,128)}, u32[]{:S(2)}) copy-start(f32[4,2]{0,1:T(2,128)} %param.34) | copy-start | bytes 100
  68.7 7.1 %copy-start.17 = (s32[32,1]{0,1:T(1,128)S(1)}, s32[32,1]{0,1:T(1,128)}, u32[]{:S(2)}) copy-start(s32[32,1]{0,1:T(1,128)} %param.43) | copy-start | bytes 388
  68.7 7.8 %copy-start.14 = (f32[4,128]{1,0:T(4,128)S(1)}, f32[4,128]{1,0:T(4,128)}, u32[]{:S(2)}) copy-start(f32[4,128]{1,0:T(4,128)} %param.32) | copy-start | bytes 6148
  68.7 8.4 %copy-start.18 = (s32[32]{0:T(128)S(1)}, s32[32]{0:T(128)}, u32[]{:S(2)}) copy-start(s32[32]{0:T(128)} %param.45) | copy-start | bytes 388
  68.7 9.1 %copy-start.8 = (bf16[32,3,128]{2,0,1:T(8,128)(2,1)S(1)}, bf16[32,3,128]{2,0,1:T(8,128)(2,1)}, u32[]{:S(2)}) copy-start(bf16[32,3,128]{2,0,1:T(8,128)(2,1)} %param.39) | copy-start | bytes 73732
  76.5 0.7 copy-start.10
  81.7 6.0 %copy-start.3 = (bf16[32,16,2,64]{3,2,1,0:T(2,128)(2,1)}, bf16[32,16,2,64]{3,2,1,0:T(2,128)(2,1)S(1)}, u32[]{:S(2)}) copy-start(bf16[32,16,2,64]{3,2,1,0:T(2,128)(2,1)S(1)} %reshape.294) | copy-start | bytes 393220
  84.4 2.8 %copy-start.13 = (f32[4,256]{1,0:T(4,128)S(1)}, f32[4,256]{1,0:T(4,128)}, u32[]{:S(2)}) copy-start(f32[4,256]{1,0:T(4,128)} %param.33) | copy-start | bytes 12292
  87.0 1.2 copy-start.6
  87.0 1.2 copy-start.7
  87.0 1.2 copy-start.15
  87.0 1.2 copy-start.23
  87.5 0.7 copy-start.2
  91.7 2.7 %copy-start.12 = (pred[32]{0:T(512)(128)(4,1)S(1)}, pred[32]{0:T(512)(128)(4,1)}, u32[]{:S(2)}) copy-start(pred[32]{0:T(512)(128)(4,1)} %get-tuple-element.52) | copy-start | bytes 100
  103.0 9.1 %copy-start.19 = (f32[128]{0:T(128)S(1)}, f32[128]{0:T(128)}, u32[]{:S(2)}) copy-start(f32[128]{0:T(128)} %param.37) | copy-start | bytes 1540
  115.9 34.1 %copy-start.4 = (f32[32,16,2]{1,2,0:T(2,128)S(1)}, f32[32,16,2]{1,2,0:T(2,128)}, u32[]{:S(2)}) copy-start(f32[32,16,2]{1,2,0:T(2,128)} %copy.98) | copy-start | bytes 12292
  115.9 34.1 %copy-start.5 = (f32[32,2]{1,0:T(8,128)S(1)}, f32[32,2]{1,0:T(8,128)}, u32[]{:S(2)}) copy-start(f32[32,2]{1,0:T(8,128)} %exp.50) | copy-start | bytes 772
  154.6 2.1 %copy-start.1 = (f32[32,2,64,128]{3,2,1,0:T(8,128)S(1)}, f32[32,2,64,128]{3,2,1,0:T(8,128)}, u32[]{:S(2)}) copy-start(f32[32,2,64,128]{3,2,1,0:T(8,128)} %multiply_add_fusion) | copy-start | bytes 6291460
  154.6 2.1 %copy-start.11 = (s32[32,1]{0,1:T(1,128)S(1)}, s32[32,1]{0,1:T(1,128)}, u32[]{:S(2)}) copy-start(s32[32,1]{0,1:T(1,128)} %copy-done.10) | copy-start | bytes 388
  165.5 35.1 %all-to-all-start.1 = ((bf16[48,2,64,128]{3,2,1,0:T(8,128)(2,1)}), bf16[48,2,64,128]{3,2,1,0:T(8,128)(2,1)S(1)}, u32[]{:S(2)}, u32[]{:S(2)}) async-start(bf16[48,2,64,128]{3,2,1,0:T(8,128)(2,1)} %convert_element_type.150), calls=%async_computation.1 | async-start | bytes 3145728 | tf_op jit(solution)/shard_map/all_to_all | solution.py:187

commit v4 on v3

--- a/solution.py
+++ b/solution.py
@@ -176,14 +176,22 @@
     fetched = lax.all_to_all(
         pool.astype(jnp.bfloat16), "rep", split_axis=0, concat_axis=0, tiled=True
     ).astype(pool.dtype)
-    start_state = jnp.take(fetched, slot_index, axis=0)
-    y_prior = decay_now[:, :, :, None] * jnp.einsum(
-        "rhpn,rtn->rthp", start_state, c_float, precision=highest
-    )
-    accepted_state = carry_decay[:, :, None, None] * start_state + jnp.einsum(
-        "rsh,rshp,rsn->rhpn", coef, x_heads, b_float, precision=highest
-    )
-    buffer = jnp.zeros(pool.shape, jnp.float32).at[slot_index].set(accepted_state)
+    slots = jnp.arange(slots_here, dtype=jnp.int32)
+    slot_pick = (slots[:, None] == slot_index[None, :]).astype(jnp.int32)
+    slot_used = jnp.sum(slot_pick, axis=1) > 0
+    slot_req = jnp.sum(slot_pick * local_index[None, :], axis=1)
+
+    def to_slots(per_req):
+        taken = jnp.take(per_req, slot_req, axis=0)
+        return jnp.where(slot_used.reshape((-1,) + (1,) * (per_req.ndim - 1)), taken, 0.0)
+
+    prior_slot = to_slots(decay_now)[:, :, :, None] * jnp.einsum(
+        "jhpn,jtn->jthp", fetched, to_slots(c_float), precision=highest
+    )
+    y_prior = jnp.take(prior_slot, slot_index, axis=0)
+    buffer = to_slots(carry_decay)[:, :, None, None] * fetched + jnp.einsum(
+        "jsh,jshp,jsn->jhpn", to_slots(coef), to_slots(x_heads), to_slots(b_float), precision=highest
+    )
     new_pool = lax.all_to_all(
         buffer.astype(jnp.bfloat16), "rep", split_axis=0, concat_axis=0, tiled=True
     ).astype(buffer.dtype)

time: 204 us -> 186 us (0.912)
  local copies, waits for them, and re-layouts: 27.2 us -> 15.4 us
  other arithmetic: 28.8 us -> 20.8 us
  matrix products: 23.7 us -> 26.2 us
    convert_element_type x2, other arithmetic: 5.49 us -> 0.09 us  [the longest x1 0.05 us: shards(): x_conv.reshape(n_req, drafts, heads_here, head_dim).astype(jnp.float32)]
    scatter x1 -> x0, local copies, waits for them, and re-layouts: 5.34 us -> none  [shards(): jnp.zeros(pool.shape, jnp.float32).at[slot_index].set(accepted_state)]
    dot_general x2, matrix products: 8.29 us -> 13.3 us  [the longest x1 8 us: shards(): jnp.einsum('jsh,jshp,jsn->jhpn', to_slots(coef), to_slots(x_heads), to_sl...]
    reshape x2, local copies, waits for them, and re-layouts: 3.84 us -> 0.43 us  [shards(): y_total = (y_local + y_prior).reshape(n_req * drafts, inner_here)]
    gather x1 -> x7, local copies, waits for them, and re-layouts: 2.69 us -> 5.91 us  [the longest x6 5.32 us: to_slots(): taken = jnp.take(per_req, slot_req, axis=0)]
    broadcast_in_dim x1 -> x0, local copies, waits for them, and re-layouts: 2.06 us -> none  [shards(): jnp.zeros(pool.shape, jnp.float32).at[slot_index].set(accepted_state)]
  transfers between devices with their start and end apart: 2 -> 2, of which waited for: 0 -> 0; matrix products, arithmetic and copies ran while one was open for 16% -> 17% of each run, Pallas kernels for 37% -> 40%
where the time goes in v4:
time: 186 us; the launch traced here: 185 us
  Pallas kernels  109 us (59%)
  matrix products  26.2 us (14%)
  other arithmetic  20.8 us (11%)
  local copies, waits for them, and re-layouts  15.4 us (8%)
  starting transfers between devices  13.3 us (7%)
    pallas_call x4, Pallas kernels, exchange(): pl.pallas_call(functools.partial(exchange_kernel, n, axis, gather), out_s...  109 us
    dot_general x4, matrix products, shards(): jnp.dot(block_rows, weight_cols, preferred_element_type=jnp.float32)  10 us
    dot_general x1, matrix products, shards(): jnp.einsum('jsh,jshp,jsn->jhpn', to_slots(coef), to_slots(x_heads), to_sl...  8 us
    all_to_all x1, starting transfers between devices, shards(): lax.all_to_all(pool.astype(jnp.bfloat16), 'rep', split_axis=0, concat_axi...  7.53 us
    all_to_all x1, starting transfers between devices, shards(): lax.all_to_all(buffer.astype(jnp.bfloat16), 'rep', split_axis=0, concat_a...  5.78 us
    dot_general x1, matrix products, shards(): jnp.einsum('jhpn,jtn->jthp', fetched, to_slots(c_float), precision=highest)  5.33 us
    gather x6, local copies, waits for them, and re-layouts, to_slots(): taken = jnp.take(per_req, slot_req, axis=0)  5.32 us
  transfers between devices with their start and end apart: 2, of which 0 were waited for; matrix products, arithmetic and copies ran while one was open for 17% of the time, Pallas kernels for 40%

profile of v4, /device:TPU:1, one launch (start us, length us, event | category | flops | bytes accessed | tf_op | source)
XLA Modules:
  0.0 185.5 jit_solution(10514961881193583528)
XLA Ops:
  0.6 3.5 %convert_element_type.143 = bf16[48,2,64,128]{3,2,1,0:T(8,128)(2,1)} convert(f32[48,2,64,128]{3,2,1,0:T(8,128)} %param.45) | non-fusion elementwise | flops 786432 | bytes 4718592 | tf_op jit(solution)/shard_map/convert_element_type | solution.py:177
  4.2 7.5 %all-to-all-start = ((bf16[48,2,64,128]{3,2,1,0:T(8,128)(2,1)}), bf16[48,2,64,128]{3,2,1,0:T(8,128)(2,1)}, u32[]{:S(2)}, u32[]{:S(2)}) async-start(bf16[48,2,64,128]{3,2,1,0:T(8,128)(2,1)} %convert_element_type.143), calls=%async_computation | async-start | bytes 3145728 | tf_op jit(solution)/shard_map/all_to_all | solution.py:176
  11.9 0.6 copy-done.17
  12.5 0.6 convert_reduce_fusion.2
  13.1 21.7 %shard_map.194.src_ref = bf16[8,16,2560]{2,1,0:T(8,128)(2,1)} custom-call(bf16[16,2560]{1,0:T(8,128)(2,1)} %bitcast.74), custom_call_target="tpu_custom_call" | custom-call | tf_op jit(solution)/shard_map/pallas_call | solution.py:51
  34.9 32.5 %shard_map.195 = bf16[4,8,16,2560]{3,2,1,0:T(8,128)(2,1)} custom-call(bf16[8,16,2560]{2,1,0:T(8,128)(2,1)} %shard_map.194.src_ref), custom_call_target="tpu_custom_call" | custom-call | tf_op jit(solution)/shard_map/pallas_call | solution.py:51
  67.4 2.5 %fusion.3 = f32[512,2]{0,1:T(2,128)S(1)} fusion(bf16[512,2560]{1,0:T(8,128)(2,1)} %bitcast.68, bf16[2560,2]{0,1:T(2,128)(2,1)S(1)} %copy-done.8), kind=kOutput, calls=%fused_computation.21 | convolution fusion | flops 5244928 | bytes 2635776 | tf_op jit(solution)/shard_map/dot_general | solution.py:114
  70.9 0.7 fusion.65
  72.0 2.6 %convolution_convert_fusion.1 = bf16[512,256]{1,0:T(8,128)(2,1)S(1)} fusion(bf16[512,2560]{1,0:T(8,128)(2,1)} %bitcast.69, bf16[2560,256]{1,0:T(8,128)(2,1)S(1)} %copy-done), kind=kOutput, calls=%fused_computation.16 | convolution fusion | flops 671219712 | bytes 4194304 | tf_op jit(solution)/shard_map/dot_general | solution.py:114
  75.1 0.3 multiply_convert_fusion
  75.4 1.1 copy-done.1
  76.6 1.9 %convolution_convert_fusion.3 = bf16[512,128]{1,0:T(8,128)(2,1)S(1)} fusion(bf16[512,2560]{1,0:T(8,128)(2,1)S(1)} %bitcast.71, bf16[2560,128]{1,0:T(8,128)(2,1)} %param.33), kind=kOutput, calls=%fused_computation.19 | convolution fusion | flops 335609856 | bytes 3407872 | tf_op jit(solution)/shard_map/dot_general | solution.py:114
  79.1 0.9 copy.64
  80.0 0.7 copy.66
  80.8 0.3 copy.71
  81.1 0.6 gather_fusion.5
  81.7 0.6 gather_fusion.3
  82.4 1.4 gather_fusion.4
  83.7 0.6 gather_fusion.6
  84.3 0.6 gather_fusion.1
  84.9 1.5 gather_fusion.2
  86.4 0.7 compare_reduce_fusion
  87.1 0.7 compare_reduce_fusion.1
  87.9 0.6 and_bitcast_fusion
  88.5 0.7 select_select_fusion.6
  89.2 0.8 select_select_fusion.4
  89.9 0.2 fusion.44
  90.2 5.3 %convolution_multiply_fusion = f32[48,16,2,64]{3,1,2,0:T(8,128)S(1)} fusion(bf16[48,2,64,128]{3,2,1,0:T(8,128)(2,1)} %all-to-all-done, f32[48,16,128]{2,1,0:T(8,128)} %gather_fusion.4, f32[48,16,2]{1,2,0:T(2,128)S(1)} %get-tuple-element.75, pred[48]{0:T(512)(128)(4,1)S(1)} %get-tuple-element.78, pred[48]{0:T(512)(128)(4,1)S(1)} %get-tuple-element.79), kind=kOutput, calls=%fused_computation.12 | convolution fusion | flops 151289856 | bytes 2365536 | tf_op jit(solution)/shard_map/jhpn,jtn->jthp/dot_general | solution.py:188
  95.5 0.6 gather_fusion
  96.1 1.5 fusion.1
  97.6 0.3 copy.72
  97.9 0.3 reshape.374
  98.3 3.0 %multiply_reduce_fusion.1 = (f32[512]{0:T(512)S(1)}, f32[512,128]{0,1:T(8,128)S(1)}) fusion(f32[512,128]{0,1:T(8,128)S(1)} %copy.73, bf16[512,2560]{1,0:T(8,128)(2,1)} %bitcast.70, bf16[2560,128]{1,0:T(8,128)(2,1)} %param.32), kind=kOutput, calls=%fused_computation.58 | convolution fusion | flops 336133632 | bytes 3803136 | tf_op jit(solution)/shard_map/dot_general | solution.py:114
  101.5 1.4 fusion.42
  102.9 0.6 scatter.15
  103.6 0.9 convolution_convert_fusion
  104.5 1.7 pad_maximum_fusion
  106.2 34.1 %shard_map.196 = bf16[4,8,16,2688]{3,2,1,0:T(8,128)(2,1)} custom-call(bf16[4,8,16,2688]{3,2,1,0:T(8,128)(2,1)} %bitcast.67), custom_call_target="tpu_custom_call" | custom-call | tf_op jit(solution)/shard_map/pallas_call | solution.py:51
  140.3 8.0 %add_convert_fusion = bf16[48,2,64,128]{3,2,1,0:T(8,128)(2,1)} fusion(bf16[48,2,64,128]{3,2,1,0:T(8,128)(2,1)} %all-to-all-done, f32[48,2]{1,0:T(8,128)S(1)} %copy-done.7, f32[48,16,2,64]{3,1,2,0:T(8,128)S(1)} %copy-done.2, f32[48,16,128]{2,1,0:T(8,128)S(1)} %gather_fusion.6, f32[48,16,2]{1,2,0:T(2,128)S(1)} %copy-done.5, ...), kind=kOutput, calls=%fused_computation.9 | convolution fusion | flops 154632192 | bytes 3938784 | tf_op jit(solution)/shard_map/jsh,jshp,jsn->jhpn/dot_general | solution.py:192
  148.3 5.8 %all-to-all-start.1 = ((bf16[48,2,64,128]{3,2,1,0:T(8,128)(2,1)}), bf16[48,2,64,128]{3,2,1,0:T(8,128)(2,1)S(1)}, u32[]{:S(2)}, u32[]{:S(2)}) async-start(bf16[48,2,64,128]{3,2,1,0:T(8,128)(2,1)} %add_convert_fusion), calls=%async_computation.1 | async-start | bytes 3145728 | tf_op jit(solution)/shard_map/all_to_all | solution.py:195
  154.1 2.4 %convert_reduce_fusion = f32[8,16,2688]{2,1,0:T(8,128)S(1)} fusion(bf16[4,8,16,2688]{3,2,1,0:T(8,128)(2,1)} %shard_map.196), kind=kLoop, calls=%fused_computation.7 | loop fusion | flops 2408448 | bytes 4128768 | tf_op jit(solution)/shard_map/reduce_sum | solution.py:210
  156.5 0.9 convert_element_type.151
  157.5 1.4 scatter.16
  158.9 2.0 %scatter.19.src_ref = bf16[8,16,2688]{2,1,0:T(8,128)(2,1)} dynamic-update-slice(bf16[8,16,2688]{2,1,0:T(8,128)(2,1)} %scatter.16, bf16[8,16,1]{2,1,0:T(8,128)(2,1)S(1)} %get-tuple-element.54, s32[]{:T(128)} %constant.196.clone.1, s32[]{:T(128)} %constant.196.clone.1, s32[]{:T(128)} %constant.207.clone.1) | dynamic-update-slice | bytes 516 | tf_op jit(solution)/shard_map/scatter | solution.py:215
  160.9 20.4 %shard_map.197 = bf16[8,16,2688]{2,1,0:T(8,128)(2,1)} custom-call(bf16[8,16,2688]{2,1,0:T(8,128)(2,1)} %scatter.19.src_ref), custom_call_target="tpu_custom_call" | custom-call | tf_op jit(solution)/shard_map/pallas_call | solution.py:51
  181.3 1.2 convert_reduce_fusion.1
  182.7 0.7 fusion.47
  183.4 2.1 %convert_element_type.161 = f32[48,2,64,128]{3,2,1,0:T(8,128)} convert(bf16[48,2,64,128]{3,2,1,0:T(8,128)(2,1)S(1)} %all-to-all-done.1) | non-fusion elementwise | flops 786432 | bytes 4718592 | tf_op jit(solution)/shard_map/convert_element_type | solution.py:197
  (93 shorter events, 3.3 us)
Async XLA Ops:
  0.6 71.4 %copy-start = (bf16[2560,256]{1,0:T(8,128)(2,1)S(1)}, bf16[2560,256]{1,0:T(8,128)(2,1)}, u32[]{:S(2)}) copy-start(bf16[2560,256]{1,0:T(8,128)(2,1)} %param.34) | copy-start | bytes 3932164
  4.2 7.5 %copy-start.11 = (s32[32]{0:T(128)S(1)}, s32[32]{0:T(128)}, u32[]{:S(2)}) copy-start(s32[32]{0:T(128)} %param.48) | copy-start | bytes 388
  4.2 7.6 %copy-start.13 = (s32[32,1]{0,1:T(1,128)S(1)}, s32[32,1]{0,1:T(1,128)}, u32[]{:S(2)}) copy-start(s32[32,1]{0,1:T(1,128)} %param.47) | copy-start | bytes 388
  4.2 86.0 %all-to-all-start = ((bf16[48,2,64,128]{3,2,1,0:T(8,128)(2,1)}), bf16[48,2,64,128]{3,2,1,0:T(8,128)(2,1)}, u32[]{:S(2)}, u32[]{:S(2)}) async-start(bf16[48,2,64,128]{3,2,1,0:T(8,128)(2,1)} %convert_element_type.143), calls=%async_computation | async-start | bytes 3145728 | tf_op jit(solution)/shard_map/all_to_all | solution.py:176
  11.7 55.7 %copy-start.8 = (bf16[2560,2]{0,1:T(2,128)(2,1)S(1)}, bf16[2560,2]{0,1:T(2,128)(2,1)}, u32[]{:S(2)}) copy-start(bf16[2560,2]{0,1:T(2,128)(2,1)} %param.35) | copy-start | bytes 30724
  11.9 0.6 copy-start.17
  13.1 56.8 %copy-start.15 = (s32[48]{0:T(128)}, s32[48]{0:T(128)S(1)}, u32[]{:S(2)}) copy-start(s32[48]{0:T(128)S(1)} %get-tuple-element.53) | copy-start | bytes 580
  34.9 35.3 %copy-start.21 = (s32[4]{0:T(128)S(1)}, s32[4]{0:T(128)}, u32[]{:S(2)}) copy-start(s32[4]{0:T(128)} %param.46) | copy-start | bytes 52
  34.9 35.4 %copy-start.22 = (f32[2]{0:T(128)S(1)}, f32[2]{0:T(128)}, u32[]{:S(2)}) copy-start(f32[2]{0:T(128)} %param.39) | copy-start | bytes 28
  34.9 35.5 %copy-start.20 = (f32[4,2]{0,1:T(2,128)S(1)}, f32[4,2]{0,1:T(2,128)}, u32[]{:S(2)}) copy-start(f32[4,2]{0,1:T(2,128)} %param.38) | copy-start | bytes 100
  71.8 2.8 %copy-start.12 = (s32[32]{0:T(128)S(1)}, s32[32]{0:T(128)}, u32[]{:S(2)}) copy-start(s32[32]{0:T(128)} %param.49) | copy-start | bytes 388
  71.8 3.0 %copy-start.9 = (f32[4,256]{1,0:T(4,128)S(1)}, f32[4,256]{1,0:T(4,128)}, u32[]{:S(2)}) copy-start(f32[4,256]{1,0:T(4,128)} %param.37) | copy-start | bytes 12292
  71.8 3.0 %copy-start.4 = (bf16[32,3,256]{2,0,1:T(8,128)(2,1)S(1)}, bf16[32,3,256]{2,0,1:T(8,128)(2,1)}, u32[]{:S(2)}) copy-start(bf16[32,3,256]{2,0,1:T(8,128)(2,1)} %param.44) | copy-start | bytes 147460
  74.8 1.7 copy-start.1
  76.6 2.0 %copy-start.6 = (bf16[32,3,128]{2,0,1:T(8,128)(2,1)S(1)}, bf16[32,3,128]{2,0,1:T(8,128)(2,1)}, u32[]{:S(2)}) copy-start(bf16[32,3,128]{2,0,1:T(8,128)(2,1)} %param.43) | copy-start | bytes 73732
  76.6 2.1 %copy-start.10 = (f32[4,128]{1,0:T(4,128)S(1)}, f32[4,128]{1,0:T(4,128)}, u32[]{:S(2)}) copy-start(f32[4,128]{1,0:T(4,128)} %param.36) | copy-start | bytes 6148
  80.8 7.1 %copy-start.18 = (s32[32]{0:T(128)S(1)}, s32[32]{0:T(128)}, u32[]{:S(2)}) copy-start(s32[32]{0:T(128)} %copy-done.17) | copy-start | bytes 388
  80.8 7.7 %copy-start.14 = (s32[48]{0:T(128)S(1)}, s32[48]{0:T(128)}, u32[]{:S(2)}) copy-start(s32[48]{0:T(128)} %get-tuple-element.52) | copy-start | bytes 580
  80.8 7.7 %copy-start.16 = (s32[48]{0:T(128)S(1)}, s32[48]{0:T(128)}, u32[]{:S(2)}) copy-start(s32[48]{0:T(128)} %copy-done.15) | copy-start | bytes 580
  98.3 5.2 %copy-start.3 = (bf16[128,2560]{1,0:T(8,128)(2,1)S(1)}, bf16[128,2560]{1,0:T(8,128)(2,1)}, u32[]{:S(2)}) copy-start(bf16[128,2560]{1,0:T(8,128)(2,1)} %param.42) | copy-start | bytes 1966084
  98.3 5.2 %copy-start.19 = (f32[128]{0:T(128)S(1)}, f32[128]{0:T(128)}, u32[]{:S(2)}) copy-start(f32[128]{0:T(128)} %param.41) | copy-start | bytes 1540
  106.2 34.1 %copy-start.2 = (f32[48,16,2,64]{3,1,2,0:T(8,128)S(1)}, f32[48,16,2,64]{3,1,2,0:T(8,128)}, u32[]{:S(2)}) copy-start(f32[48,16,2,64]{3,1,2,0:T(8,128)} %gather_fusion.2) | copy-start | bytes 1179652
  106.2 34.1 %copy-start.5 = (f32[48,16,2]{1,2,0:T(2,128)S(1)}, f32[48,16,2]{1,2,0:T(2,128)}, u32[]{:S(2)}) copy-start(f32[48,16,2]{1,2,0:T(2,128)} %get-tuple-element.74) | copy-start | bytes 18436
  106.2 34.1 %copy-start.7 = (f32[48,2]{1,0:T(8,128)S(1)}, f32[48,2]{1,0:T(8,128)}, u32[]{:S(2)}) copy-start(f32[48,2]{1,0:T(8,128)} %select_select_fusion.6) | copy-start | bytes 1156
  148.3 35.1 %all-to-all-start.1 = ((bf16[48,2,64,128]{3,2,1,0:T(8,128)(2,1)}), bf16[48,2,64,128]{3,2,1,0:T(8,128)(2,1)S(1)}, u32[]{:S(2)}, u32[]{:S(2)}) async-start(bf16[48,2,64,128]{3,2,1,0:T(8,128)(2,1)} %add_convert_fusion), calls=%async_computation.1 | async-start | bytes 3145728 | tf_op jit(solution)/shard_map/all_to_all | solution.py:195

commit v5 on v4

--- a/solution.py
+++ b/solution.py
@@ -43,6 +43,79 @@
     local.wait()
     for copy in copies:
         copy.wait()
+
+
+def ring4_kernel(axis, gather, src_ref, dst_ref, stage_ref, send_sem, recv_sem, local_sem):
+    me = lax.axis_index(axis)
+    coords = {name: lax.axis_index(name) for name in AXES}
+
+    def device_of(peer):
+        return tuple(peer if name == axis else coords[name] for name in AXES)
+
+    right, left = lax.rem(me + 1, 4), lax.rem(me + 3, 4)
+    opposite = lax.rem(me + 2, 4)
+    half = dst_ref.shape[1] // 2
+    first, second = pl.ds(0, half), pl.ds(half, half)
+
+    def remote(src, dst, index, peer):
+        copy = pltpu.make_async_remote_copy(
+            src_ref=src,
+            dst_ref=dst,
+            send_sem=send_sem.at[index],
+            recv_sem=recv_sem.at[index],
+            device_id=device_of(peer),
+            device_id_type=MESH,
+        )
+        copy.start()
+        return copy
+
+    barrier = pltpu.get_barrier_semaphore()
+    for peer in (left, right):
+        pl.semaphore_signal(barrier, inc=1, device_id=device_of(peer), device_id_type=MESH)
+    pl.semaphore_wait(barrier, 2)
+    local = pltpu.make_async_copy(src_ref if gather else src_ref.at[me], dst_ref.at[me], local_sem)
+    local.start()
+    to_right = remote(src_ref if gather else src_ref.at[right], dst_ref.at[me], 0, right)
+    to_left = remote(src_ref if gather else src_ref.at[left], dst_ref.at[me], 1, left)
+    if gather:
+        to_right.wait_recv()
+        pass_right = remote(dst_ref.at[left, first], dst_ref.at[left, first], 2, right)
+        to_left.wait_recv()
+        pass_left = remote(dst_ref.at[right, second], dst_ref.at[right, second], 3, left)
+        to_right.wait_send()
+        to_left.wait_send()
+    else:
+        stage_right = remote(src_ref.at[opposite, first], stage_ref.at[0], 2, right)
+        stage_left = remote(src_ref.at[opposite, second], stage_ref.at[1], 3, left)
+        stage_right.wait_recv()
+        pass_right = remote(stage_ref.at[0], dst_ref.at[left, first], 4, right)
+        stage_left.wait_recv()
+        pass_left = remote(stage_ref.at[1], dst_ref.at[right, second], 5, left)
+        stage_right.wait_send()
+        stage_left.wait_send()
+        to_right.wait()
+        to_left.wait()
+    local.wait()
+    pass_right.wait()
+    pass_left.wait()
+
+
+def exchange4(src, axis, gather, collective_id):
+    block = src.shape if gather else src.shape[1:]
+    out = jax.ShapeDtypeStruct((4,) + tuple(block), src.dtype)
+    stage = jax.ShapeDtypeStruct((2, block[0] // 2) + tuple(block[1:]), src.dtype)
+    return pl.pallas_call(
+        functools.partial(ring4_kernel, axis, gather),
+        out_shape=(out, stage),
+        in_specs=[pl.BlockSpec(memory_space=pl.ANY)],
+        out_specs=(pl.BlockSpec(memory_space=pl.ANY), pl.BlockSpec(memory_space=pl.ANY)),
+        scratch_shapes=[
+            pltpu.SemaphoreType.DMA((6,)),
+            pltpu.SemaphoreType.DMA((6,)),
+            pltpu.SemaphoreType.DMA,
+        ],
+        compiler_params=pltpu.CompilerParams(collective_id=collective_id, has_side_effects=True),
+    )(src)[0]
 
 
 def exchange(src, axis, gather, collective_id):
@@ -108,7 +181,7 @@
     weights_in = (w_z, w_x, w_dt, w_bc)
     n_blk = lax.axis_size(BLK)
     along_z = exchange(rows_in, "bz", True, 0)
-    block_rows = exchange(along_z, "by", True, 1).reshape(n_blk * local_rows, rows_in.shape[1])
+    block_rows = exchange4(along_z, "by", True, 1).reshape(n_blk * local_rows, rows_in.shape[1])
     projected = jnp.concatenate(
         [
             jnp.dot(block_rows, weight_cols, preferred_element_type=jnp.float32)
@@ -207,7 +280,7 @@
     extra = extra.at[:, 0].set(sq_hi).at[:, 1].set(sq_lo)
     n_y = lax.axis_size("by")
     packed = jnp.concatenate([partial, extra], 1).reshape(n_y, n_blk // n_y, local_rows, width + 128)
-    half_sum = jnp.sum(exchange(packed, "by", False, 2).astype(jnp.float32), axis=0)
+    half_sum = jnp.sum(exchange4(packed, "by", False, 2).astype(jnp.float32), axis=0)
     sq_mid = half_sum[:, :, width] + half_sum[:, :, width + 1]
     sq_mid_hi = sq_mid.astype(jnp.bfloat16)
     sq_mid_lo = (sq_mid - sq_mid_hi.astype(jnp.float32)).astype(jnp.bfloat16)

time: 186 us -> 177 us (0.952)
  Pallas kernels: 109 us -> 98 us
    pallas_call x4 -> x2, Pallas kernels: 109 us -> 41.6 us  [exchange(): pl.pallas_call(functools.partial(exchange_kernel, n, axis, gather), out_s...]
    pallas_call x0 -> x2, Pallas kernels: none -> 56.4 us  [exchange4(): pl.pallas_call(functools.partial(ring4_kernel, axis, gather), out_shape=(...]
  transfers between devices with their start and end apart: 2 -> 2, of which waited for: 0 -> 0; matrix products, arithmetic and copies ran while one was open for 17% -> 18% of each run, Pallas kernels for 40% -> 38%
where the time goes in v5:
time: 177 us; the launch traced here: 176 us
  Pallas kernels  98 us (55%)
  matrix products  26.2 us (15%)
  other arithmetic  20.6 us (12%)
  local copies, waits for them, and re-layouts  15.3 us (9%)
  starting transfers between devices  14.8 us (8%)
    pallas_call x2, Pallas kernels, exchange4(): pl.pallas_call(functools.partial(ring4_kernel, axis, gather), out_shape=(...  56.4 us
    pallas_call x2, Pallas kernels, exchange(): pl.pallas_call(functools.partial(exchange_kernel, n, axis, gather), out_s...  41.6 us
    dot_general x4, matrix products, shards(): jnp.dot(block_rows, weight_cols, preferred_element_type=jnp.float32)  10 us
    dot_general x1, matrix products, shards(): jnp.einsum('jsh,jshp,jsn->jhpn', to_slots(coef), to_slots(x_heads), to_sl...  8 us
    all_to_all x1, starting transfers between devices, shards(): lax.all_to_all(pool.astype(jnp.bfloat16), 'rep', split_axis=0, concat_axi...  7.54 us
    all_to_all x1, starting transfers between devices, shards(): lax.all_to_all(buffer.astype(jnp.bfloat16), 'rep', split_axis=0, concat_a...  7.22 us
    dot_general x1, matrix products, shards(): jnp.einsum('jhpn,jtn->jthp', fetched, to_slots(c_float), precision=highest)  5.33 us
    gather x6, local copies, waits for them, and re-layouts, to_slots(): taken = jnp.take(per_req, slot_req, axis=0)  5.31 us
  transfers between devices with their start and end apart: 2, of which 0 were waited for; matrix products, arithmetic and copies ran while one was open for 18% of the time, Pallas kernels for 38%

profile of v5, /device:TPU:1, one launch (start us, length us, event | category | flops | bytes accessed | tf_op | source)
XLA Modules:
  0.0 176.1 jit_solution(9489849684902541597)
XLA Ops:
  0.6 3.5 %convert_element_type.143 = bf16[48,2,64,128]{3,2,1,0:T(8,128)(2,1)} convert(f32[48,2,64,128]{3,2,1,0:T(8,128)} %param.45) | non-fusion elementwise | flops 786432 | bytes 4718592 | tf_op jit(solution)/shard_map/convert_element_type | solution.py:250
  4.2 7.5 %all-to-all-start = ((bf16[48,2,64,128]{3,2,1,0:T(8,128)(2,1)}), bf16[48,2,64,128]{3,2,1,0:T(8,128)(2,1)}, u32[]{:S(2)}, u32[]{:S(2)}) async-start(bf16[48,2,64,128]{3,2,1,0:T(8,128)(2,1)} %convert_element_type.143), calls=%async_computation | async-start | bytes 3145728 | tf_op jit(solution)/shard_map/all_to_all | solution.py:249
  12.0 0.6 copy-done.17
  12.6 0.6 convert_reduce_fusion.2
  13.2 21.7 %shard_map.194.src_ref = bf16[8,16,2560]{2,1,0:T(8,128)(2,1)} custom-call(bf16[16,2560]{1,0:T(8,128)(2,1)} %bitcast.74), custom_call_target="tpu_custom_call" | custom-call | tf_op jit(solution)/shard_map/pallas_call | solution.py:124
  34.9 25.4 %shard_map.195 = (bf16[4,8,16,2560]{3,2,1,0:T(8,128)(2,1)}, bf16[2,4,16,2560]{3,2,1,0:T(8,128)(2,1)}) custom-call(bf16[8,16,2560]{2,1,0:T(8,128)(2,1)} %shard_map.194.src_ref), custom_call_target="tpu_custom_call" | custom-call | tf_op jit(solution)/shard_map/pallas_call | solution.py:107
  60.3 2.5 %fusion.3 = f32[512,2]{0,1:T(2,128)S(1)} fusion(bf16[512,2560]{1,0:T(8,128)(2,1)} %bitcast.68, bf16[2560,2]{0,1:T(2,128)(2,1)S(1)} %copy-done.8), kind=kOutput, calls=%fused_computation.21 | convolution fusion | flops 5244928 | bytes 2635776 | tf_op jit(solution)/shard_map/dot_general | solution.py:187
  63.7 0.7 fusion.65
  64.9 2.6 %convolution_convert_fusion.1 = bf16[512,256]{1,0:T(8,128)(2,1)S(1)} fusion(bf16[512,2560]{1,0:T(8,128)(2,1)} %bitcast.69, bf16[2560,256]{1,0:T(8,128)(2,1)S(1)} %copy-done), kind=kOutput, calls=%fused_computation.16 | convolution fusion | flops 671219712 | bytes 4194304 | tf_op jit(solution)/shard_map/dot_general | solution.py:187
  67.9 0.3 multiply_convert_fusion
  68.3 1.1 copy-done.1
  69.4 1.9 %convolution_convert_fusion.3 = bf16[512,128]{1,0:T(8,128)(2,1)S(1)} fusion(bf16[512,2560]{1,0:T(8,128)(2,1)S(1)} %bitcast.71, bf16[2560,128]{1,0:T(8,128)(2,1)} %param.33), kind=kOutput, calls=%fused_computation.19 | convolution fusion | flops 335609856 | bytes 3407872 | tf_op jit(solution)/shard_map/dot_general | solution.py:187
  72.0 0.9 copy.64
  72.9 0.7 copy.66
  73.7 0.3 copy.71
  74.0 0.6 gather_fusion.5
  74.6 0.6 gather_fusion.3
  75.2 1.4 gather_fusion.4
  76.6 0.6 gather_fusion.6
  77.2 0.6 gather_fusion.1
  77.8 1.5 gather_fusion.2
  79.3 0.6 compare_reduce_fusion
  79.9 0.7 compare_reduce_fusion.1
  80.6 0.6 and_bitcast_fusion
  81.3 0.7 select_select_fusion.6
  82.0 0.8 select_select_fusion.4
  82.8 0.2 fusion.44
  83.0 5.3 %convolution_multiply_fusion = f32[48,16,2,64]{3,1,2,0:T(8,128)S(1)} fusion(bf16[48,2,64,128]{3,2,1,0:T(8,128)(2,1)} %all-to-all-done, f32[48,16,128]{2,1,0:T(8,128)} %gather_fusion.4, f32[48,16,2]{1,2,0:T(2,128)S(1)} %get-tuple-element.79, pred[48]{0:T(512)(128)(4,1)S(1)} %get-tuple-element.82, pred[48]{0:T(512)(128)(4,1)S(1)} %get-tuple-element.83), kind=kOutput, calls=%fused_computation.12 | convolution fusion | flops 151289856 | bytes 2365536 | tf_op jit(solution)/shard_map/jhpn,jtn->jthp/dot_general | solution.py:261
  88.3 0.6 gather_fusion
  88.9 1.5 fusion.1
  90.4 0.3 copy.72
  90.7 0.3 reshape.374
  91.1 3.0 %multiply_reduce_fusion.1 = (f32[512]{0:T(512)S(1)}, f32[512,128]{0,1:T(8,128)S(1)}) fusion(f32[512,128]{0,1:T(8,128)S(1)} %copy.73, bf16[512,2560]{1,0:T(8,128)(2,1)} %bitcast.70, bf16[2560,128]{1,0:T(8,128)(2,1)} %param.32), kind=kOutput, calls=%fused_computation.58 | convolution fusion | flops 336133632 | bytes 3803136 | tf_op jit(solution)/shard_map/dot_general | solution.py:187
  94.3 1.3 fusion.42
  95.7 0.6 scatter.15
  96.3 0.9 convolution_convert_fusion
  97.2 1.7 pad_maximum_fusion
  98.9 31.0 %shard_map.196 = (bf16[4,8,16,2688]{3,2,1,0:T(8,128)(2,1)}, bf16[2,4,16,2688]{3,2,1,0:T(8,128)(2,1)}) custom-call(bf16[4,8,16,2688]{3,2,1,0:T(8,128)(2,1)} %bitcast.67), custom_call_target="tpu_custom_call" | custom-call | tf_op jit(solution)/shard_map/pallas_call | solution.py:107
  130.0 8.0 %add_convert_fusion = bf16[48,2,64,128]{3,2,1,0:T(8,128)(2,1)} fusion(bf16[48,2,64,128]{3,2,1,0:T(8,128)(2,1)} %all-to-all-done, f32[48,2]{1,0:T(8,128)S(1)} %copy-done.7, f32[48,16,2,64]{3,1,2,0:T(8,128)S(1)} %copy-done.2, f32[48,16,128]{2,1,0:T(8,128)S(1)} %gather_fusion.6, f32[48,16,2]{1,2,0:T(2,128)S(1)} %copy-done.5, ...), kind=kOutput, calls=%fused_computation.9 | convolution fusion | flops 154632192 | bytes 3938784 | tf_op jit(solution)/shard_map/jsh,jshp,jsn->jhpn/dot_general | solution.py:265
  138.0 7.2 %all-to-all-start.1 = ((bf16[48,2,64,128]{3,2,1,0:T(8,128)(2,1)}), bf16[48,2,64,128]{3,2,1,0:T(8,128)(2,1)S(1)}, u32[]{:S(2)}, u32[]{:S(2)}) async-start(bf16[48,2,64,128]{3,2,1,0:T(8,128)(2,1)} %add_convert_fusion), calls=%async_computation.1 | async-start | bytes 3145728 | tf_op jit(solution)/shard_map/all_to_all | solution.py:268
  145.2 2.4 %convert_reduce_fusion = f32[8,16,2688]{2,1,0:T(8,128)S(1)} fusion(bf16[4,8,16,2688]{3,2,1,0:T(8,128)(2,1)} %get-tuple-element.55), kind=kLoop, calls=%fused_computation.7 | loop fusion | flops 2408448 | bytes 4128768 | tf_op jit(solution)/shard_map/reduce_sum | solution.py:283
  147.6 0.9 convert_element_type.151
  148.6 1.4 scatter.16
  150.0 2.0 %scatter.19.src_ref = bf16[8,16,2688]{2,1,0:T(8,128)(2,1)} dynamic-update-slice(bf16[8,16,2688]{2,1,0:T(8,128)(2,1)} %scatter.16, bf16[8,16,1]{2,1,0:T(8,128)(2,1)S(1)} %get-tuple-element.58, s32[]{:T(128)} %constant.196.clone.1, s32[]{:T(128)} %constant.196.clone.1, s32[]{:T(128)} %constant.207.clone.1) | dynamic-update-slice | bytes 516 | tf_op jit(solution)/shard_map/scatter | solution.py:288
  152.0 19.9 %shard_map.197 = bf16[8,16,2688]{2,1,0:T(8,128)(2,1)} custom-call(bf16[8,16,2688]{2,1,0:T(8,128)(2,1)} %scatter.19.src_ref), custom_call_target="tpu_custom_call" | custom-call | tf_op jit(solution)/shard_map/pallas_call | solution.py:124
  171.9 1.2 convert_reduce_fusion.1
  173.3 0.7 fusion.47
  174.0 2.1 %convert_element_type.161 = f32[48,2,64,128]{3,2,1,0:T(8,128)} convert(bf16[48,2,64,128]{3,2,1,0:T(8,128)(2,1)S(1)} %all-to-all-done.1) | non-fusion elementwise | flops 786432 | bytes 4718592 | tf_op jit(solution)/shard_map/convert_element_type | solution.py:270
  (93 shorter events, 3.3 us)
Async XLA Ops:
  0.6 64.3 %copy-start = (bf16[2560,256]{1,0:T(8,128)(2,1)S(1)}, bf16[2560,256]{1,0:T(8,128)(2,1)}, u32[]{:S(2)}) copy-start(bf16[2560,256]{1,0:T(8,128)(2,1)} %param.34) | copy-start | bytes 3932164
  4.2 7.6 %copy-start.11 = (s32[32]{0:T(128)S(1)}, s32[32]{0:T(128)}, u32[]{:S(2)}) copy-start(s32[32]{0:T(128)} %param.48) | copy-start | bytes 388
  4.2 7.6 %copy-start.13 = (s32[32,1]{0,1:T(1,128)S(1)}, s32[32,1]{0,1:T(1,128)}, u32[]{:S(2)}) copy-start(s32[32,1]{0,1:T(1,128)} %param.47) | copy-start | bytes 388
  4.2 56.1 %copy-start.8 = (bf16[2560,2]{0,1:T(2,128)(2,1)S(1)}, bf16[2560,2]{0,1:T(2,128)(2,1)}, u32[]{:S(2)}) copy-start(bf16[2560,2]{0,1:T(2,128)(2,1)} %param.35) | copy-start | bytes 30724
  4.2 78.8 %all-to-all-start = ((bf16[48,2,64,128]{3,2,1,0:T(8,128)(2,1)}), bf16[48,2,64,128]{3,2,1,0:T(8,128)(2,1)}, u32[]{:S(2)}, u32[]{:S(2)}) async-start(bf16[48,2,64,128]{3,2,1,0:T(8,128)(2,1)} %convert_element_type.143), calls=%async_computation | async-start | bytes 3145728 | tf_op jit(solution)/shard_map/all_to_all | solution.py:249
  11.7 51.3 %copy-start.21 = (s32[4]{0:T(128)S(1)}, s32[4]{0:T(128)}, u32[]{:S(2)}) copy-start(s32[4]{0:T(128)} %param.46) | copy-start | bytes 52
  11.7 51.4 %copy-start.22 = (f32[2]{0:T(128)S(1)}, f32[2]{0:T(128)}, u32[]{:S(2)}) copy-start(f32[2]{0:T(128)} %param.39) | copy-start | bytes 28
  11.7 51.5 %copy-start.20 = (f32[4,2]{0,1:T(2,128)S(1)}, f32[4,2]{0,1:T(2,128)}, u32[]{:S(2)}) copy-start(f32[4,2]{0,1:T(2,128)} %param.38) | copy-start | bytes 100
  12.0 0.6 copy-start.17
  13.2 51.3 %copy-start.15 = (s32[48]{0:T(128)}, s32[48]{0:T(128)S(1)}, u32[]{:S(2)}) copy-start(s32[48]{0:T(128)S(1)} %get-tuple-element.57) | copy-start | bytes 580
  64.6 2.8 %copy-start.12 = (s32[32]{0:T(128)S(1)}, s32[32]{0:T(128)}, u32[]{:S(2)}) copy-start(s32[32]{0:T(128)} %param.49) | copy-start | bytes 388
  64.6 3.0 %copy-start.9 = (f32[4,256]{1,0:T(4,128)S(1)}, f32[4,256]{1,0:T(4,128)}, u32[]{:S(2)}) copy-start(f32[4,256]{1,0:T(4,128)} %param.37) | copy-start | bytes 12292
  64.7 3.0 %copy-start.4 = (bf16[32,3,256]{2,0,1:T(8,128)(2,1)S(1)}, bf16[32,3,256]{2,0,1:T(8,128)(2,1)}, u32[]{:S(2)}) copy-start(bf16[32,3,256]{2,0,1:T(8,128)(2,1)} %param.44) | copy-start | bytes 147460
  67.7 1.7 copy-start.1
  69.4 2.0 %copy-start.6 = (bf16[32,3,128]{2,0,1:T(8,128)(2,1)S(1)}, bf16[32,3,128]{2,0,1:T(8,128)(2,1)}, u32[]{:S(2)}) copy-start(bf16[32,3,128]{2,0,1:T(8,128)(2,1)} %param.43) | copy-start | bytes 73732
  69.4 2.1 %copy-start.10 = (f32[4,128]{1,0:T(4,128)S(1)}, f32[4,128]{1,0:T(4,128)}, u32[]{:S(2)}) copy-start(f32[4,128]{1,0:T(4,128)} %param.36) | copy-start | bytes 6148
  73.6 7.0 %copy-start.18 = (s32[32]{0:T(128)S(1)}, s32[32]{0:T(128)}, u32[]{:S(2)}) copy-start(s32[32]{0:T(128)} %copy-done.17) | copy-start | bytes 388
  73.7 7.6 %copy-start.14 = (s32[48]{0:T(128)S(1)}, s32[48]{0:T(128)}, u32[]{:S(2)}) copy-start(s32[48]{0:T(128)} %get-tuple-element.56) | copy-start | bytes 580
  73.7 7.6 %copy-start.16 = (s32[48]{0:T(128)S(1)}, s32[48]{0:T(128)}, u32[]{:S(2)}) copy-start(s32[48]{0:T(128)} %copy-done.15) | copy-start | bytes 580
  91.1 5.1 %copy-start.3 = (bf16[128,2560]{1,0:T(8,128)(2,1)S(1)}, bf16[128,2560]{1,0:T(8,128)(2,1)}, u32[]{:S(2)}) copy-start(bf16[128,2560]{1,0:T(8,128)(2,1)} %param.42) | copy-start | bytes 1966084
  91.1 5.1 %copy-start.19 = (f32[128]{0:T(128)S(1)}, f32[128]{0:T(128)}, u32[]{:S(2)}) copy-start(f32[128]{0:T(128)} %param.41) | copy-start | bytes 1540
  98.9 31.1 %copy-start.2 = (f32[48,16,2,64]{3,1,2,0:T(8,128)S(1)}, f32[48,16,2,64]{3,1,2,0:T(8,128)}, u32[]{:S(2)}) copy-start(f32[48,16,2,64]{3,1,2,0:T(8,128)} %gather_fusion.2) | copy-start | bytes 1179652
  98.9 31.1 %copy-start.5 = (f32[48,16,2]{1,2,0:T(2,128)S(1)}, f32[48,16,2]{1,2,0:T(2,128)}, u32[]{:S(2)}) copy-start(f32[48,16,2]{1,2,0:T(2,128)} %get-tuple-element.78) | copy-start | bytes 18436
  98.9 31.1 %copy-start.7 = (f32[48,2]{1,0:T(8,128)S(1)}, f32[48,2]{1,0:T(8,128)}, u32[]{:S(2)}) copy-start(f32[48,2]{1,0:T(8,128)} %select_select_fusion.6) | copy-start | bytes 1156
  138.0 36.0 %all-to-all-start.1 = ((bf16[48,2,64,128]{3,2,1,0:T(8,128)(2,1)}), bf16[48,2,64,128]{3,2,1,0:T(8,128)(2,1)S(1)}, u32[]{:S(2)}, u32[]{:S(2)}) async-start(bf16[48,2,64,128]{3,2,1,0:T(8,128)(2,1)} %add_convert_fusion), calls=%async_computation.1 | async-start | bytes 3145728 | tf_op jit(solution)/shard_map/all_to_all | solution.py:268

commit v6 on v5

--- a/solution.py
+++ b/solution.py
@@ -116,6 +116,82 @@
         ],
         compiler_params=pltpu.CompilerParams(collective_id=collective_id, has_side_effects=True),
     )(src)[0]
+
+
+def gather2d_kernel(nz, src_ref, dst_ref, send_sem, recv_sem, local_sem):
+    y, z = lax.axis_index("by"), lax.axis_index("bz")
+    rep = lax.axis_index("rep")
+    right, left = lax.rem(y + 1, 4), lax.rem(y + 3, 4)
+    half = src_ref.shape[0] // 2
+    first, second = pl.ds(0, half), pl.ds(half, half)
+    z_sem, r_sem, l_sem, ra_sem, lb_sem = 0, nz, 2 * nz, 3 * nz, 4 * nz
+
+    def remote(src, dst, index, yy, zz):
+        copy = pltpu.make_async_remote_copy(
+            src_ref=src,
+            dst_ref=dst,
+            send_sem=send_sem.at[index],
+            recv_sem=recv_sem.at[index],
+            device_id=(yy, zz, rep),
+            device_id_type=MESH,
+        )
+        copy.start()
+        return copy
+
+    barrier = pltpu.get_barrier_semaphore()
+    for offset in range(1, nz):
+        pl.semaphore_signal(
+            barrier, inc=1, device_id=(y, lax.rem(z + offset, nz), rep), device_id_type=MESH
+        )
+    for yy in (left, right):
+        pl.semaphore_signal(barrier, inc=1, device_id=(yy, z, rep), device_id_type=MESH)
+    pl.semaphore_wait(barrier, nz + 1)
+    local = pltpu.make_async_copy(src_ref, dst_ref.at[y, z], local_sem)
+    local.start()
+    sent = []
+    along_z = []
+    for offset in range(1, nz):
+        copy = remote(src_ref, dst_ref.at[y, z], z_sem + offset, y, lax.rem(z + offset, nz))
+        along_z.append(copy)
+    to_right = [remote(src_ref, dst_ref.at[y, z], r_sem, right, z)]
+    to_left = [remote(src_ref, dst_ref.at[y, z], l_sem, left, z)]
+    for offset in range(1, nz):
+        along_z[offset - 1].wait_recv()
+        zs = lax.rem(z + nz - offset, nz)
+        to_right.append(remote(dst_ref.at[y, zs], dst_ref.at[y, zs], r_sem + offset, right, z))
+        to_left.append(remote(dst_ref.at[y, zs], dst_ref.at[y, zs], l_sem + offset, left, z))
+    relays = []
+    for offset in range(nz):
+        zs = lax.rem(z + nz - offset, nz)
+        to_right[offset].wait_recv()
+        relays.append(
+            remote(dst_ref.at[left, zs, first], dst_ref.at[left, zs, first], ra_sem + offset, right, z)
+        )
+        to_left[offset].wait_recv()
+        relays.append(
+            remote(dst_ref.at[right, zs, second], dst_ref.at[right, zs, second], lb_sem + offset, left, z)
+        )
+    local.wait()
+    for copy in along_z + to_right + to_left:
+        copy.wait_send()
+    for copy in relays:
+        copy.wait()
+
+
+def gather2d(src, collective_id):
+    nz = lax.axis_size("bz")
+    return pl.pallas_call(
+        functools.partial(gather2d_kernel, nz),
+        out_shape=jax.ShapeDtypeStruct((4, nz) + tuple(src.shape), src.dtype),
+        in_specs=[pl.BlockSpec(memory_space=pl.ANY)],
+        out_specs=pl.BlockSpec(memory_space=pl.ANY),
+        scratch_shapes=[
+            pltpu.SemaphoreType.DMA((5 * nz,)),
+            pltpu.SemaphoreType.DMA((5 * nz,)),
+            pltpu.SemaphoreType.DMA,
+        ],
+        compiler_params=pltpu.CompilerParams(collective_id=collective_id, has_side_effects=True),
+    )(src)
 
 
 def exchange(src, axis, gather, collective_id):
@@ -180,8 +256,7 @@
     cap_group = slots_here // lax.axis_size("rep")
     weights_in = (w_z, w_x, w_dt, w_bc)
     n_blk = lax.axis_size(BLK)
-    along_z = exchange(rows_in, "bz", True, 0)
-    block_rows = exchange4(along_z, "by", True, 1).reshape(n_blk * local_rows, rows_in.shape[1])
+    block_rows = gather2d(rows_in, 0).reshape(n_blk * local_rows, rows_in.shape[1])
     projected = jnp.concatenate(
         [
             jnp.dot(block_rows, weight_cols, preferred_element_type=jnp.float32)

time: 177 us -> 170 us (0.960)
  Pallas kernels: 98 us -> 88.3 us
  starting transfers between devices: 14.8 us -> 17.2 us
    pallas_call x0 -> x1, Pallas kernels: none -> 37.1 us  [gather2d(): pl.pallas_call(functools.partial(gather2d_kernel, nz), out_shape=jax.Shap...]
    pallas_call x2 -> x1, Pallas kernels: 56.4 us -> 29.9 us  [exchange4(): pl.pallas_call(functools.partial(ring4_kernel, axis, gather), out_shape=(...]
    pallas_call x2 -> x1, Pallas kernels: 41.6 us -> 21.4 us  [exchange(): pl.pallas_call(functools.partial(exchange_kernel, n, axis, gather), out_s...]
    all_to_all x1, starting transfers between devices: 7.22 us -> 9.7 us  [shards(): lax.all_to_all(buffer.astype(jnp.bfloat16), 'rep', split_axis=0, concat_a...]
  transfers between devices with their start and end apart: 2 -> 2, of which waited for: 0 -> 0; matrix products, arithmetic and copies ran while one was open for 18% -> 18% of each run, Pallas kernels for 38% -> 35%
where the time goes in v6:
time: 170 us; the launch traced here: 169 us
  Pallas kernels  88.3 us (52%)
  matrix products  26.2 us (15%)
  other arithmetic  20.7 us (12%)
  starting transfers between devices  17.2 us (10%)
  local copies, waits for them, and re-layouts  15.3 us (9%)
    pallas_call x1, Pallas kernels, gather2d(): pl.pallas_call(functools.partial(gather2d_kernel, nz), out_shape=jax.Shap...  37.1 us
    pallas_call x1, Pallas kernels, exchange4(): pl.pallas_call(functools.partial(ring4_kernel, axis, gather), out_shape=(...  29.9 us
    pallas_call x1, Pallas kernels, exchange(): pl.pallas_call(functools.partial(exchange_kernel, n, axis, gather), out_s...  21.4 us
    dot_general x4, matrix products, shards(): jnp.dot(block_rows, weight_cols, preferred_element_type=jnp.float32)  10 us
    all_to_all x1, starting transfers between devices, shards(): lax.all_to_all(buffer.astype(jnp.bfloat16), 'rep', split_axis=0, concat_a...  9.7 us
    dot_general x1, matrix products, shards(): jnp.einsum('jsh,jshp,jsn->jhpn', to_slots(coef), to_slots(x_heads), to_sl...  8 us
    all_to_all x1, starting transfers between devices, shards(): lax.all_to_all(pool.astype(jnp.bfloat16), 'rep', split_axis=0, concat_axi...  7.55 us
    dot_general x1, matrix products, shards(): jnp.einsum('jhpn,jtn->jthp', fetched, to_slots(c_float), precision=highest)  5.33 us
  transfers between devices with their start and end apart: 2, of which 0 were waited for; matrix products, arithmetic and copies ran while one was open for 18% of the time, Pallas kernels for 35%

profile of v6, /device:TPU:1, one launch (start us, length us, event | category | flops | bytes accessed | tf_op | source)
XLA Modules:
  0.0 168.8 jit_solution(7596676817107140397)
XLA Ops:
  0.6 3.5 %convert_element_type.143 = bf16[48,2,64,128]{3,2,1,0:T(8,128)(2,1)} convert(f32[48,2,64,128]{3,2,1,0:T(8,128)} %param.45) | non-fusion elementwise | flops 786432 | bytes 4718592 | tf_op jit(solution)/shard_map/convert_element_type | solution.py:325
  4.2 7.5 %all-to-all-start = ((bf16[48,2,64,128]{3,2,1,0:T(8,128)(2,1)}), bf16[48,2,64,128]{3,2,1,0:T(8,128)(2,1)}, u32[]{:S(2)}, u32[]{:S(2)}) async-start(bf16[48,2,64,128]{3,2,1,0:T(8,128)(2,1)} %convert_element_type.143), calls=%async_computation | async-start | bytes 3145728 | tf_op jit(solution)/shard_map/all_to_all | solution.py:324
  12.0 0.5 copy-done.17
  12.5 0.6 convert_reduce_fusion.2
  13.1 37.1 %shard_map.194 = bf16[4,8,16,2560]{3,2,1,0:T(8,128)(2,1)} custom-call(bf16[16,2560]{1,0:T(8,128)(2,1)} %bitcast.74), custom_call_target="tpu_custom_call" | custom-call | tf_op jit(solution)/shard_map/pallas_call | solution.py:183
  50.2 2.5 %fusion.3 = f32[512,2]{0,1:T(2,128)S(1)} fusion(bf16[512,2560]{1,0:T(8,128)(2,1)} %bitcast.68, bf16[2560,2]{0,1:T(2,128)(2,1)S(1)} %copy-done.8), kind=kOutput, calls=%fused_computation.21 | convolution fusion | flops 5244928 | bytes 2635776 | tf_op jit(solution)/shard_map/dot_general | solution.py:262
  53.7 0.7 fusion.65
  54.8 2.6 %convolution_convert_fusion.1 = bf16[512,256]{1,0:T(8,128)(2,1)S(1)} fusion(bf16[512,2560]{1,0:T(8,128)(2,1)} %bitcast.69, bf16[2560,256]{1,0:T(8,128)(2,1)S(1)} %copy-done), kind=kOutput, calls=%fused_computation.16 | convolution fusion | flops 671219712 | bytes 4194304 | tf_op jit(solution)/shard_map/dot_general | solution.py:262
  57.8 0.3 multiply_convert_fusion
  58.2 1.1 copy-done.1
  59.4 1.9 %convolution_convert_fusion.3 = bf16[512,128]{1,0:T(8,128)(2,1)S(1)} fusion(bf16[512,2560]{1,0:T(8,128)(2,1)S(1)} %bitcast.71, bf16[2560,128]{1,0:T(8,128)(2,1)} %param.33), kind=kOutput, calls=%fused_computation.19 | convolution fusion | flops 335609856 | bytes 3407872 | tf_op jit(solution)/shard_map/dot_general | solution.py:262
  61.9 0.9 copy.64
  62.8 0.7 copy.66
  63.6 0.3 copy.71
  63.9 0.6 gather_fusion.5
  64.5 0.6 gather_fusion.3
  65.1 1.4 gather_fusion.4
  66.5 0.6 gather_fusion.6
  67.1 0.6 gather_fusion.1
  67.7 1.5 gather_fusion.2
  69.2 0.7 compare_reduce_fusion
  69.9 0.7 compare_reduce_fusion.1
  70.6 0.5 and_bitcast_fusion
  71.2 0.7 select_select_fusion.6
  71.9 0.8 select_select_fusion.4
  72.7 0.2 fusion.44
  72.9 5.3 %convolution_multiply_fusion = f32[48,16,2,64]{3,1,2,0:T(8,128)S(1)} fusion(bf16[48,2,64,128]{3,2,1,0:T(8,128)(2,1)} %all-to-all-done, f32[48,16,128]{2,1,0:T(8,128)} %gather_fusion.4, f32[48,16,2]{1,2,0:T(2,128)S(1)} %get-tuple-element.77, pred[48]{0:T(512)(128)(4,1)S(1)} %get-tuple-element.80, pred[48]{0:T(512)(128)(4,1)S(1)} %get-tuple-element.81), kind=kOutput, calls=%fused_computation.12 | convolution fusion | flops 151289856 | bytes 2365536 | tf_op jit(solution)/shard_map/jhpn,jtn->jthp/dot_general | solution.py:336
  78.2 0.6 gather_fusion
  78.8 1.5 fusion.1
  80.3 0.3 copy.72
  80.6 0.3 reshape.374
  81.0 3.0 %multiply_reduce_fusion.1 = (f32[512]{0:T(512)S(1)}, f32[512,128]{0,1:T(8,128)S(1)}) fusion(f32[512,128]{0,1:T(8,128)S(1)} %copy.73, bf16[512,2560]{1,0:T(8,128)(2,1)} %bitcast.70, bf16[2560,128]{1,0:T(8,128)(2,1)} %param.32), kind=kOutput, calls=%fused_computation.58 | convolution fusion | flops 336133632 | bytes 3803136 | tf_op jit(solution)/shard_map/dot_general | solution.py:262
  84.2 1.4 fusion.42
  85.6 0.6 scatter.15
  86.2 0.9 convolution_convert_fusion
  87.2 1.7 %pad_maximum_fusion = bf16[512,2688]{1,0:T(8,128)(2,1)} fusion(bf16[512,128]{1,0:T(8,128)(2,1)S(1)} %scatter.15, bf16[512,2560]{1,0:T(8,128)(2,1)S(1)} %convolution_convert_fusion), kind=kLoop, calls=%fused_computation.10 | loop fusion | flops 5505024 | bytes 5505024 | tf_op jit(solution)/shard_map/concatenate | solution.py:357
  88.9 29.9 %shard_map.195 = (bf16[4,8,16,2688]{3,2,1,0:T(8,128)(2,1)}, bf16[2,4,16,2688]{3,2,1,0:T(8,128)(2,1)}) custom-call(bf16[4,8,16,2688]{3,2,1,0:T(8,128)(2,1)} %bitcast.67), custom_call_target="tpu_custom_call" | custom-call | tf_op jit(solution)/shard_map/pallas_call | solution.py:107
  118.8 8.0 %add_convert_fusion = bf16[48,2,64,128]{3,2,1,0:T(8,128)(2,1)} fusion(bf16[48,2,64,128]{3,2,1,0:T(8,128)(2,1)} %all-to-all-done, f32[48,2]{1,0:T(8,128)S(1)} %copy-done.7, f32[48,16,2,64]{3,1,2,0:T(8,128)S(1)} %copy-done.2, f32[48,16,128]{2,1,0:T(8,128)S(1)} %gather_fusion.6, f32[48,16,2]{1,2,0:T(2,128)S(1)} %copy-done.5, ...), kind=kOutput, calls=%fused_computation.9 | convolution fusion | flops 154632192 | bytes 3938784 | tf_op jit(solution)/shard_map/jsh,jshp,jsn->jhpn/dot_general | solution.py:340
  126.8 9.7 %all-to-all-start.1 = ((bf16[48,2,64,128]{3,2,1,0:T(8,128)(2,1)}), bf16[48,2,64,128]{3,2,1,0:T(8,128)(2,1)S(1)}, u32[]{:S(2)}, u32[]{:S(2)}) async-start(bf16[48,2,64,128]{3,2,1,0:T(8,128)(2,1)} %add_convert_fusion), calls=%async_computation.1 | async-start | bytes 3145728 | tf_op jit(solution)/shard_map/all_to_all | solution.py:343
  136.5 2.4 %convert_reduce_fusion = f32[8,16,2688]{2,1,0:T(8,128)S(1)} fusion(bf16[4,8,16,2688]{3,2,1,0:T(8,128)(2,1)} %get-tuple-element.53), kind=kLoop, calls=%fused_computation.7 | loop fusion | flops 2408448 | bytes 4128768 | tf_op jit(solution)/shard_map/reduce_sum | solution.py:358
  138.9 0.9 convert_element_type.151
  139.9 1.4 scatter.16
  141.3 2.0 %scatter.19.src_ref = bf16[8,16,2688]{2,1,0:T(8,128)(2,1)} dynamic-update-slice(bf16[8,16,2688]{2,1,0:T(8,128)(2,1)} %scatter.16, bf16[8,16,1]{2,1,0:T(8,128)(2,1)S(1)} %get-tuple-element.56, s32[]{:T(128)} %constant.196.clone.1, s32[]{:T(128)} %constant.196.clone.1, s32[]{:T(128)} %constant.207.clone.1) | dynamic-update-slice | bytes 516 | tf_op jit(solution)/shard_map/scatter | solution.py:363
  143.3 21.4 %shard_map.196 = bf16[8,16,2688]{2,1,0:T(8,128)(2,1)} custom-call(bf16[8,16,2688]{2,1,0:T(8,128)(2,1)} %scatter.19.src_ref), custom_call_target="tpu_custom_call" | custom-call | tf_op jit(solution)/shard_map/pallas_call | solution.py:200
  164.6 1.2 convert_reduce_fusion.1
  165.9 0.2 fusion.54
  166.0 0.7 fusion.47
  166.8 2.1 %convert_element_type.161 = f32[48,2,64,128]{3,2,1,0:T(8,128)} convert(bf16[48,2,64,128]{3,2,1,0:T(8,128)(2,1)S(1)} %all-to-all-done.1) | non-fusion elementwise | flops 786432 | bytes 4718592 | tf_op jit(solution)/shard_map/convert_element_type | solution.py:345
  (92 shorter events, 3.1 us)
Async XLA Ops:
  0.6 54.2 %copy-start = (bf16[2560,256]{1,0:T(8,128)(2,1)S(1)}, bf16[2560,256]{1,0:T(8,128)(2,1)}, u32[]{:S(2)}) copy-start(bf16[2560,256]{1,0:T(8,128)(2,1)} %param.34) | copy-start | bytes 3932164
  4.2 7.6 %copy-start.11 = (s32[32]{0:T(128)S(1)}, s32[32]{0:T(128)}, u32[]{:S(2)}) copy-start(s32[32]{0:T(128)} %param.48) | copy-start | bytes 388
  4.2 7.6 %copy-start.13 = (s32[32,1]{0,1:T(1,128)S(1)}, s32[32,1]{0,1:T(1,128)}, u32[]{:S(2)}) copy-start(s32[32,1]{0,1:T(1,128)} %param.47) | copy-start | bytes 388
  4.2 46.0 %copy-start.8 = (bf16[2560,2]{0,1:T(2,128)(2,1)S(1)}, bf16[2560,2]{0,1:T(2,128)(2,1)}, u32[]{:S(2)}) copy-start(bf16[2560,2]{0,1:T(2,128)(2,1)} %param.35) | copy-start | bytes 30724
  4.2 68.7 %all-to-all-start = ((bf16[48,2,64,128]{3,2,1,0:T(8,128)(2,1)}), bf16[48,2,64,128]{3,2,1,0:T(8,128)(2,1)}, u32[]{:S(2)}, u32[]{:S(2)}) async-start(bf16[48,2,64,128]{3,2,1,0:T(8,128)(2,1)} %convert_element_type.143), calls=%async_computation | async-start | bytes 3145728 | tf_op jit(solution)/shard_map/all_to_all | solution.py:324
  11.9 0.5 copy-start.17
  13.1 39.7 %copy-start.15 = (s32[48]{0:T(128)}, s32[48]{0:T(128)S(1)}, u32[]{:S(2)}) copy-start(s32[48]{0:T(128)S(1)} %get-tuple-element.55) | copy-start | bytes 580
  13.1 39.8 %copy-start.21 = (s32[4]{0:T(128)S(1)}, s32[4]{0:T(128)}, u32[]{:S(2)}) copy-start(s32[4]{0:T(128)} %param.46) | copy-start | bytes 52
  13.1 40.0 %copy-start.22 = (f32[2]{0:T(128)S(1)}, f32[2]{0:T(128)}, u32[]{:S(2)}) copy-start(f32[2]{0:T(128)} %param.39) | copy-start | bytes 28
  13.1 40.1 %copy-start.20 = (f32[4,2]{0,1:T(2,128)S(1)}, f32[4,2]{0,1:T(2,128)}, u32[]{:S(2)}) copy-start(f32[4,2]{0,1:T(2,128)} %param.38) | copy-start | bytes 100
  54.6 2.8 %copy-start.12 = (s32[32]{0:T(128)S(1)}, s32[32]{0:T(128)}, u32[]{:S(2)}) copy-start(s32[32]{0:T(128)} %param.49) | copy-start | bytes 388
  54.6 3.0 %copy-start.9 = (f32[4,256]{1,0:T(4,128)S(1)}, f32[4,256]{1,0:T(4,128)}, u32[]{:S(2)}) copy-start(f32[4,256]{1,0:T(4,128)} %param.37) | copy-start | bytes 12292
  54.6 3.0 %copy-start.4 = (bf16[32,3,256]{2,0,1:T(8,128)(2,1)S(1)}, bf16[32,3,256]{2,0,1:T(8,128)(2,1)}, u32[]{:S(2)}) copy-start(bf16[32,3,256]{2,0,1:T(8,128)(2,1)} %param.44) | copy-start | bytes 147460
  57.6 1.7 %copy-start.1 = (bf16[4,8,16,2560]{3,2,1,0:T(8,128)(2,1)S(1)}, bf16[4,8,16,2560]{3,2,1,0:T(8,128)(2,1)}, u32[]{:S(2)}) copy-start(bf16[4,8,16,2560]{3,2,1,0:T(8,128)(2,1)} %shard_map.194) | copy-start | bytes 7864324
  59.3 2.0 %copy-start.6 = (bf16[32,3,128]{2,0,1:T(8,128)(2,1)S(1)}, bf16[32,3,128]{2,0,1:T(8,128)(2,1)}, u32[]{:S(2)}) copy-start(bf16[32,3,128]{2,0,1:T(8,128)(2,1)} %param.43) | copy-start | bytes 73732
  59.3 2.1 %copy-start.10 = (f32[4,128]{1,0:T(4,128)S(1)}, f32[4,128]{1,0:T(4,128)}, u32[]{:S(2)}) copy-start(f32[4,128]{1,0:T(4,128)} %param.36) | copy-start | bytes 6148
  63.6 7.1 %copy-start.18 = (s32[32]{0:T(128)S(1)}, s32[32]{0:T(128)}, u32[]{:S(2)}) copy-start(s32[32]{0:T(128)} %copy-done.17) | copy-start | bytes 388
  63.6 7.6 %copy-start.14 = (s32[48]{0:T(128)S(1)}, s32[48]{0:T(128)}, u32[]{:S(2)}) copy-start(s32[48]{0:T(128)} %get-tuple-element.54) | copy-start | bytes 580
  63.6 7.6 %copy-start.16 = (s32[48]{0:T(128)S(1)}, s32[48]{0:T(128)}, u32[]{:S(2)}) copy-start(s32[48]{0:T(128)} %copy-done.15) | copy-start | bytes 580
  81.0 5.2 %copy-start.3 = (bf16[128,2560]{1,0:T(8,128)(2,1)S(1)}, bf16[128,2560]{1,0:T(8,128)(2,1)}, u32[]{:S(2)}) copy-start(bf16[128,2560]{1,0:T(8,128)(2,1)} %param.42) | copy-start | bytes 1966084
  81.0 5.2 %copy-start.19 = (f32[128]{0:T(128)S(1)}, f32[128]{0:T(128)}, u32[]{:S(2)}) copy-start(f32[128]{0:T(128)} %param.41) | copy-start | bytes 1540
  88.9 29.9 %copy-start.2 = (f32[48,16,2,64]{3,1,2,0:T(8,128)S(1)}, f32[48,16,2,64]{3,1,2,0:T(8,128)}, u32[]{:S(2)}) copy-start(f32[48,16,2,64]{3,1,2,0:T(8,128)} %gather_fusion.2) | copy-start | bytes 1179652
  88.9 29.9 %copy-start.5 = (f32[48,16,2]{1,2,0:T(2,128)S(1)}, f32[48,16,2]{1,2,0:T(2,128)}, u32[]{:S(2)}) copy-start(f32[48,16,2]{1,2,0:T(2,128)} %get-tuple-element.76) | copy-start | bytes 18436
  88.9 29.9 %copy-start.7 = (f32[48,2]{1,0:T(8,128)S(1)}, f32[48,2]{1,0:T(8,128)}, u32[]{:S(2)}) copy-start(f32[48,2]{1,0:T(8,128)} %select_select_fusion.6) | copy-start | bytes 1156
  126.8 40.0 %all-to-all-start.1 = ((bf16[48,2,64,128]{3,2,1,0:T(8,128)(2,1)}), bf16[48,2,64,128]{3,2,1,0:T(8,128)(2,1)S(1)}, u32[]{:S(2)}, u32[]{:S(2)}) async-start(bf16[48,2,64,128]{3,2,1,0:T(8,128)(2,1)} %add_convert_fusion), calls=%async_computation.1 | async-start | bytes 3145728 | tf_op jit(solution)/shard_map/all_to_all | solution.py:343

commit v7 on v6

--- a/solution.py
+++ b/solution.py
@@ -220,6 +220,14 @@
     for offset in range(1, kernel.shape[0]):
         summed = summed + kernel[offset] * sequence[:, offset : offset + steps_count]
     return jax.nn.silu(summed).astype(jnp.bfloat16)
+
+
+def split_dot(spec, wide, narrow):
+    high = wide.astype(jnp.bfloat16)
+    low = (wide - high.astype(jnp.float32)).astype(jnp.bfloat16)
+    return jnp.einsum(spec, high, narrow, preferred_element_type=jnp.float32) + jnp.einsum(
+        spec, low, narrow, preferred_element_type=jnp.float32
+    )
 
 
 def shards(
@@ -290,7 +298,7 @@
     log_decay = jnp.cumsum(step_size * (-jnp.exp(a_log))[None, None, :], axis=1)
     draft_index = jnp.arange(drafts, dtype=jnp.int32)
     causal = draft_index[:, None] >= draft_index[None, :]
-    scores = jnp.einsum("rtn,rsn->rts", c_float, b_float, precision=highest)
+    scores = jnp.einsum("rtn,rsn->rts", c_half, b_half, preferred_element_type=jnp.float32)
     log_gap = log_decay[:, :, None, :] - log_decay[:, None, :, :]
     weight = (
         jnp.where(causal[None, :, :, None], jnp.exp(jnp.minimum(log_gap, 0.0)), 0.0)
@@ -298,7 +306,7 @@
         * scores[:, :, :, None]
     )
     y_local = (
-        jnp.einsum("rtsh,rshp->rthp", weight, x_heads, precision=highest)
+        split_dot("rtsh,rshp->rthp", weight, x_conv.reshape(n_req, drafts, heads_here, head_dim))
         + d_skip[None, None, :, None] * x_heads
     )
     pick_last = (draft_index[None, :] == accepted[:, None] - 1).astype(jnp.float32)
@@ -321,9 +329,10 @@
     )
     rank_within = jnp.sum(earlier.astype(jnp.int32), axis=1)
     slot_index = owner_of * cap_group + rank_within
-    fetched = lax.all_to_all(
+    fetched_half = lax.all_to_all(
         pool.astype(jnp.bfloat16), "rep", split_axis=0, concat_axis=0, tiled=True
-    ).astype(pool.dtype)
+    )
+    fetched = fetched_half.astype(pool.dtype)
     slots = jnp.arange(slots_here, dtype=jnp.int32)
     slot_pick = (slots[:, None] == slot_index[None, :]).astype(jnp.int32)
     slot_used = jnp.sum(slot_pick, axis=1) > 0
@@ -334,11 +343,11 @@
         return jnp.where(slot_used.reshape((-1,) + (1,) * (per_req.ndim - 1)), taken, 0.0)
 
     prior_slot = to_slots(decay_now)[:, :, :, None] * jnp.einsum(
-        "jhpn,jtn->jthp", fetched, to_slots(c_float), precision=highest
+        "jhpn,jtn->jthp", fetched_half, to_slots(c_half), preferred_element_type=jnp.float32
     )
     y_prior = jnp.take(prior_slot, slot_index, axis=0)
-    buffer = to_slots(carry_decay)[:, :, None, None] * fetched + jnp.einsum(
-        "jsh,jshp,jsn->jhpn", to_slots(coef), to_slots(x_heads), to_slots(b_float), precision=highest
+    buffer = to_slots(carry_decay)[:, :, None, None] * fetched + split_dot(
+        "jshp,jsn->jhpn", to_slots(coef[:, :, :, None] * x_heads), to_slots(b_half)
     )
     new_pool = lax.all_to_all(
         buffer.astype(jnp.bfloat16), "rep", split_axis=0, concat_axis=0, tiled=True

time: 170 us -> 166 us (0.976)
  local copies, waits for them, and re-layouts: 15.3 us -> 12.7 us
    gather x6 -> x5, local copies, waits for them, and re-layouts: 5.31 us -> 3.05 us  [to_slots(): taken = jnp.take(per_req, slot_req, axis=0)]
    dot_general x4 -> x6, matrix products: 15 us -> 14 us  [the longest x2 5.37 us: split_dot(): jnp.einsum(spec, low, narrow, preferred_element_type=jnp.float32)]
  transfers between devices with their start and end apart: 2 -> 2, of which waited for: 0 -> 0; matrix products, arithmetic and copies ran while one was open for 18% -> 20% of each run, Pallas kernels for 35% -> 35%
where the time goes in v7:
time: 166 us
  Pallas kernels  88.1 us (53%)
  matrix products  26.8 us (16%)
  other arithmetic  19.5 us (12%)
  starting transfers between devices  17.3 us (10%)
  local copies, waits for them, and re-layouts  12.7 us (8%)
    pallas_call x1, Pallas kernels, gather2d(): pl.pallas_call(functools.partial(gather2d_kernel, nz), out_shape=jax.Shap...  36.8 us
    pallas_call x1, Pallas kernels, exchange4(): pl.pallas_call(functools.partial(ring4_kernel, axis, gather), out_shape=(...  29.9 us
    pallas_call x1, Pallas kernels, exchange(): pl.pallas_call(functools.partial(exchange_kernel, n, axis, gather), out_s...  21.4 us
    dot_general x4, matrix products, shards(): jnp.dot(block_rows, weight_cols, preferred_element_type=jnp.float32)  10.7 us
    all_to_all x1, starting transfers between devices, shards(): lax.all_to_all(buffer.astype(jnp.bfloat16), 'rep', split_axis=0, concat_a...  9.74 us
    all_to_all x1, starting transfers between devices, shards(): lax.all_to_all(pool.astype(jnp.bfloat16), 'rep', split_axis=0, concat_axi...  7.55 us
    dot_general x2, matrix products, split_dot(): jnp.einsum(spec, low, narrow, preferred_element_type=jnp.float32)  5.37 us
    dot_general x2, matrix products, split_dot(): jnp.einsum(spec, high, narrow, preferred_element_type=jnp.float32)  4.69 us
  transfers between devices with their start and end apart: 2, of which 0 were waited for; matrix products, arithmetic and copies ran while one was open for 20% of the time, Pallas kernels for 35%

profile of v7, /device:TPU:1, one launch (start us, length us, event | category | flops | bytes accessed | tf_op | source)
XLA Modules:
  0.0 165.6 jit_solution(17637609777596763146)
XLA Ops:
  0.6 3.5 %convert_element_type.164 = bf16[48,2,64,128]{3,2,1,0:T(8,128)(2,1)} convert(f32[48,2,64,128]{3,2,1,0:T(8,128)} %param.43) | non-fusion elementwise | flops 786432 | bytes 4718592 | tf_op jit(solution)/shard_map/convert_element_type | solution.py:333
  4.2 7.6 %all-to-all-start = ((bf16[48,2,64,128]{3,2,1,0:T(8,128)(2,1)}), bf16[48,2,64,128]{3,2,1,0:T(8,128)(2,1)}, u32[]{:S(2)}, u32[]{:S(2)}) async-start(bf16[48,2,64,128]{3,2,1,0:T(8,128)(2,1)} %convert_element_type.164), calls=%async_computation | async-start | bytes 3145728 | tf_op jit(solution)/shard_map/all_to_all | solution.py:332
  12.0 0.5 and_bitcast_fusion
  12.5 0.6 compare_reduce_fusion
  13.2 0.7 compare_reduce_fusion.1
  13.9 36.8 %shard_map.194 = bf16[4,8,16,2560]{3,2,1,0:T(8,128)(2,1)} custom-call(bf16[16,2560]{1,0:T(8,128)(2,1)} %bitcast.76), custom_call_target="tpu_custom_call" | custom-call | tf_op jit(solution)/shard_map/pallas_call | solution.py:183
  50.8 2.5 %fusion.4 = f32[512,2]{0,1:T(2,128)S(1)} fusion(bf16[512,2560]{1,0:T(8,128)(2,1)} %bitcast.70, bf16[2560,2]{0,1:T(2,128)(2,1)S(1)} %copy-done.7), kind=kOutput, calls=%fused_computation.21 | convolution fusion | flops 5244928 | bytes 2635776 | tf_op jit(solution)/shard_map/dot_general | solution.py:270
  53.4 0.2 reduce-window.4
  53.7 0.2 fusion.47
  54.2 0.7 fusion.69
  54.9 0.9 copy.68
  56.3 2.6 %convolution_convert_fusion.1 = bf16[512,256]{1,0:T(8,128)(2,1)S(1)} fusion(bf16[512,2560]{1,0:T(8,128)(2,1)} %bitcast.71, bf16[2560,256]{1,0:T(8,128)(2,1)S(1)} %copy-done), kind=kOutput, calls=%fused_computation.16 | convolution fusion | flops 671219712 | bytes 4194304 | tf_op jit(solution)/shard_map/dot_general | solution.py:270
  59.1 0.7 copy.70
  59.8 2.6 %convolution_convert_fusion.3 = bf16[512,128]{1,0:T(8,128)(2,1)S(1)} fusion(bf16[512,2560]{1,0:T(8,128)(2,1)} %bitcast.72, bf16[2560,128]{1,0:T(8,128)(2,1)S(1)} %copy-done.15), kind=kOutput, calls=%fused_computation.19 | convolution fusion | flops 335609856 | bytes 3407872 | tf_op jit(solution)/shard_map/dot_general | solution.py:270
  62.9 0.3 copy.76
  63.5 0.3 multiply_convert_fusion
  63.9 0.6 pad_clamp_fusion
  64.6 0.6 gather_fusion
  65.2 0.2 convert_multiply_fusion
  65.4 0.6 gather_fusion.3
  66.0 0.6 gather_fusion.4
  66.6 0.6 gather_fusion.5
  67.3 0.6 gather_fusion.2
  68.1 0.2 fusion.63
  68.3 2.0 %fusion.30 = f32[32,2,64,16]{2,3,1,0:T(8,128)} fusion(f32[32,16,16]{2,1,0:T(8,128)S(1)} %fusion.63, f32[32,16,2]{1,2,0:T(2,128)} %copy.70, f32[32,16,2]{1,2,0:T(2,128)} %copy.68, pred[16,16]{1,0:T(8,128)(4,1)S(1)} %iota_compare_fusion.6, bf16[32,16,2,64]{3,2,1,0:T(2,128)(2,1)S(1)} %reshape.390), kind=kOutput, calls=%fused_computation.67 | convolution fusion | flops 2195456 | bytes 434432 | tf_op jit(solution)/shard_map/rtsh,rshp->rthp/dot_general | solution.py:228
  70.4 2.6 %fusion.10 = f32[48,2,64,128]{3,2,1,0:T(8,128)} fusion(f32[48,16,2,64]{3,1,2,0:T(8,128)S(1)} %gather_fusion.3, pred[48]{0:T(512)(128)(4,1)S(1)} %get-tuple-element.77, pred[48]{0:T(512)(128)(4,1)S(1)} %get-tuple-element.78, bf16[48,16,128]{2,1,0:T(8,128)(2,1)S(1)} %gather_fusion.5), kind=kOutput, calls=%fused_computation.38 | convolution fusion | flops 25559040 | bytes 3735648 | tf_op jit(solution)/shard_map/jshp,jsn->jhpn/dot_general | solution.py:228
  73.1 3.7 %convolution_multiply_fusion = f32[48,16,2,64]{3,1,2,0:T(8,128)} fusion(bf16[48,2,64,128]{3,2,1,0:T(8,128)(2,1)} %all-to-all-done, f32[48,16,2]{1,2,0:T(2,128)S(1)} %select_select_fusion.4, bf16[48,16,128]{2,1,0:T(8,128)(2,1)S(1)} %gather_fusion.4, pred[48]{0:T(512)(128)(4,1)S(1)} %get-tuple-element.77, pred[48]{0:T(512)(128)(4,1)S(1)} %get-tuple-element.78), kind=kOutput, calls=%fused_computation.11 | convolution fusion | flops 25460736 | bytes 2168928 | tf_op jit(solution)/shard_map/jhpn,jtn->jthp/dot_general | solution.py:345
  76.8 1.8 %gather_fusion.1 = f32[32,16,2,64]{3,1,2,0:T(8,128)S(1)} fusion(f32[48,16,2,64]{3,1,2,0:T(8,128)} %convolution_multiply_fusion, s32[1024]{0:T(1024)} %pad_clamp_fusion), kind=kCustom, calls=%fused_computation.3 | custom fusion | bytes 524416 | tf_op jit(solution)/shard_map/jit(_take)/gather | solution.py:348
  78.7 1.4 fusion.2
  80.1 0.3 copy.77
  80.4 0.3 reshape.393
  80.8 3.0 %multiply_reduce_fusion.1 = (f32[512]{0:T(512)S(1)}, f32[512,128]{0,1:T(8,128)S(1)}) fusion(f32[512,128]{0,1:T(8,128)S(1)} %copy.78, bf16[512,2560]{1,0:T(8,128)(2,1)} %bitcast.73, bf16[2560,128]{1,0:T(8,128)(2,1)} %param.30), kind=kOutput, calls=%fused_computation.57 | convolution fusion | flops 336133632 | bytes 3803136 | tf_op jit(solution)/shard_map/dot_general | solution.py:270
  83.9 1.3 fusion.40
  85.3 0.6 scatter.15
  85.9 2.0 %convolution_convert_fusion = bf16[512,2560]{1,0:T(8,128)(2,1)S(1)} fusion(bf16[128,2560]{1,0:T(8,128)(2,1)} %param.40, f32[512,128]{0,1:T(8,128)S(1)} %get-tuple-element.76, f32[128]{0:T(128)S(1)} %copy-done.14), kind=kOutput, calls=%fused_computation.7 | convolution fusion | flops 336986112 | bytes 3539456 | tf_op jit(solution)/shard_map/dot_general | solution.py:361
  87.9 1.8 %pad_maximum_fusion = bf16[512,2688]{1,0:T(8,128)(2,1)} fusion(bf16[512,128]{1,0:T(8,128)(2,1)S(1)} %scatter.15, bf16[512,2560]{1,0:T(8,128)(2,1)S(1)} %convolution_convert_fusion), kind=kLoop, calls=%fused_computation.9 | loop fusion | flops 5505024 | bytes 5505024 | tf_op jit(solution)/shard_map/concatenate | solution.py:366
  89.7 29.9 %shard_map.195 = (bf16[4,8,16,2688]{3,2,1,0:T(8,128)(2,1)}, bf16[2,4,16,2688]{3,2,1,0:T(8,128)(2,1)}) custom-call(bf16[4,8,16,2688]{3,2,1,0:T(8,128)(2,1)} %bitcast.69), custom_call_target="tpu_custom_call" | custom-call | tf_op jit(solution)/shard_map/pallas_call | solution.py:107
  119.5 3.9 %add_convert_fusion = bf16[48,2,64,128]{3,2,1,0:T(8,128)(2,1)} fusion(f32[48,2,64,128]{3,2,1,0:T(8,128)} %fusion.10, bf16[48,2,64,128]{3,2,1,0:T(8,128)(2,1)} %all-to-all-done, f32[48,2]{1,0:T(8,128)S(1)} %select_select_fusion.5, f32[48,16,2,64]{3,1,2,0:T(8,128)S(1)} %gather_fusion.3, pred[48]{0:T(512)(128)(4,1)S(1)} %get-tuple-element.77, ...), kind=kOutput, calls=%fused_computation.8 | convolution fusion | flops 29884416 | bytes 6881760 | tf_op jit(solution)/shard_map/jshp,jsn->jhpn/dot_general | solution.py:228
  123.5 9.7 %all-to-all-start.1 = ((bf16[48,2,64,128]{3,2,1,0:T(8,128)(2,1)}), bf16[48,2,64,128]{3,2,1,0:T(8,128)(2,1)S(1)}, u32[]{:S(2)}, u32[]{:S(2)}) async-start(bf16[48,2,64,128]{3,2,1,0:T(8,128)(2,1)} %add_convert_fusion), calls=%async_computation.1 | async-start | bytes 3145728 | tf_op jit(solution)/shard_map/all_to_all | solution.py:352
  133.2 2.4 %convert_reduce_fusion = f32[8,16,2688]{2,1,0:T(8,128)S(1)} fusion(bf16[4,8,16,2688]{3,2,1,0:T(8,128)(2,1)} %get-tuple-element.52), kind=kLoop, calls=%fused_computation.6 | loop fusion | flops 2408448 | bytes 4128768 | tf_op jit(solution)/shard_map/reduce_sum | solution.py:367
  135.6 0.9 convert_element_type.172
  136.6 1.4 scatter.16
  138.0 2.0 %scatter.19.src_ref = bf16[8,16,2688]{2,1,0:T(8,128)(2,1)} dynamic-update-slice(bf16[8,16,2688]{2,1,0:T(8,128)(2,1)} %scatter.16, bf16[8,16,1]{2,1,0:T(8,128)(2,1)S(1)} %get-tuple-element.55, s32[]{:T(128)} %constant.199.clone.1, s32[]{:T(128)} %constant.199.clone.1, s32[]{:T(128)} %constant.211.clone.1) | dynamic-update-slice | bytes 516 | tf_op jit(solution)/shard_map/scatter | solution.py:372
  140.0 21.4 %shard_map.196 = bf16[8,16,2688]{2,1,0:T(8,128)(2,1)} custom-call(bf16[8,16,2688]{2,1,0:T(8,128)(2,1)} %scatter.19.src_ref), custom_call_target="tpu_custom_call" | custom-call | tf_op jit(solution)/shard_map/pallas_call | solution.py:200
  161.4 1.2 convert_reduce_fusion.1
  162.6 0.2 fusion.51
  162.8 0.7 fusion.44
  163.6 2.1 %convert_element_type.184 = f32[48,2,64,128]{3,2,1,0:T(8,128)} convert(bf16[48,2,64,128]{3,2,1,0:T(8,128)(2,1)S(1)} %all-to-all-done.1) | non-fusion elementwise | flops 786432 | bytes 4718592 | tf_op jit(solution)/shard_map/convert_element_type | solution.py:354
  (87 shorter events, 3.0 us)
Async XLA Ops:
  0.6 55.6 %copy-start = (bf16[2560,256]{1,0:T(8,128)(2,1)S(1)}, bf16[2560,256]{1,0:T(8,128)(2,1)}, u32[]{:S(2)}) copy-start(bf16[2560,256]{1,0:T(8,128)(2,1)} %param.32) | copy-start | bytes 3932164
  4.2 7.6 %copy-start.11 = (s32[32,1]{0,1:T(1,128)S(1)}, s32[32,1]{0,1:T(1,128)}, u32[]{:S(2)}) copy-start(s32[32,1]{0,1:T(1,128)} %param.45) | copy-start | bytes 388
  4.2 46.5 %copy-start.17 = (f32[2]{0:T(128)S(1)}, f32[2]{0:T(128)}, u32[]{:S(2)}) copy-start(f32[2]{0:T(128)} %param.37) | copy-start | bytes 28
  4.2 46.6 %copy-start.7 = (bf16[2560,2]{0,1:T(2,128)(2,1)S(1)}, bf16[2560,2]{0,1:T(2,128)(2,1)}, u32[]{:S(2)}) copy-start(bf16[2560,2]{0,1:T(2,128)(2,1)} %param.33) | copy-start | bytes 30724
  4.2 68.9 %all-to-all-start = ((bf16[48,2,64,128]{3,2,1,0:T(8,128)(2,1)}), bf16[48,2,64,128]{3,2,1,0:T(8,128)(2,1)}, u32[]{:S(2)}, u32[]{:S(2)}) async-start(bf16[48,2,64,128]{3,2,1,0:T(8,128)(2,1)} %convert_element_type.164), calls=%async_computation | async-start | bytes 3145728 | tf_op jit(solution)/shard_map/all_to_all | solution.py:332
  13.9 39.6 %copy-start.18 = (s32[4]{0:T(128)S(1)}, s32[4]{0:T(128)}, u32[]{:S(2)}) copy-start(s32[4]{0:T(128)} %param.44) | copy-start | bytes 52
  13.9 39.8 %copy-start.16 = (f32[4,2]{0,1:T(2,128)S(1)}, f32[4,2]{0,1:T(2,128)}, u32[]{:S(2)}) copy-start(f32[4,2]{0,1:T(2,128)} %param.36) | copy-start | bytes 100
  50.7 5.2 %copy-start.10 = (s32[32]{0:T(128)S(1)}, s32[32]{0:T(128)}, u32[]{:S(2)}) copy-start(s32[32]{0:T(128)} %param.46) | copy-start | bytes 388
  56.0 2.9 %copy-start.12 = (s32[32]{0:T(128)S(1)}, s32[32]{0:T(128)}, u32[]{:S(2)}) copy-start(s32[32]{0:T(128)} %param.47) | copy-start | bytes 388
  56.0 3.1 %copy-start.8 = (f32[4,256]{1,0:T(4,128)S(1)}, f32[4,256]{1,0:T(4,128)}, u32[]{:S(2)}) copy-start(f32[4,256]{1,0:T(4,128)} %param.35) | copy-start | bytes 12292
  56.2 3.7 %copy-start.15 = (bf16[2560,128]{1,0:T(8,128)(2,1)S(1)}, bf16[2560,128]{1,0:T(8,128)(2,1)}, u32[]{:S(2)}) copy-start(bf16[2560,128]{1,0:T(8,128)(2,1)} %param.31) | copy-start | bytes 1966084
  58.9 3.5 %copy-start.6 = (bf16[32,3,128]{2,0,1:T(8,128)(2,1)S(1)}, bf16[32,3,128]{2,0,1:T(8,128)(2,1)}, u32[]{:S(2)}) copy-start(bf16[32,3,128]{2,0,1:T(8,128)(2,1)} %param.41) | copy-start | bytes 73732
  58.9 3.6 %copy-start.9 = (f32[4,128]{1,0:T(4,128)S(1)}, f32[4,128]{1,0:T(4,128)}, u32[]{:S(2)}) copy-start(f32[4,128]{1,0:T(4,128)} %param.34) | copy-start | bytes 6148
  59.8 3.4 %copy-start.3 = (bf16[32,3,256]{2,0,1:T(8,128)(2,1)S(1)}, bf16[32,3,256]{2,0,1:T(8,128)(2,1)}, u32[]{:S(2)}) copy-start(bf16[32,3,256]{2,0,1:T(8,128)(2,1)} %param.42) | copy-start | bytes 147460
  68.3 4.7 %copy-start.1 = (f32[32,16,16]{2,1,0:T(8,128)}, f32[32,16,16]{2,1,0:T(8,128)S(1)}, u32[]{:S(2)}) copy-start(f32[32,16,16]{2,1,0:T(8,128)S(1)} %fusion.63) | copy-start | bytes 98308
  73.0 5.6 %copy-start.4 = (f32[32,16,2]{1,2,0:T(2,128)S(1)}, f32[32,16,2]{1,2,0:T(2,128)}, u32[]{:S(2)}) copy-start(f32[32,16,2]{1,2,0:T(2,128)} %copy.68) | copy-start | bytes 12292
  73.0 5.6 %copy-start.5 = (f32[32,16,2]{1,2,0:T(2,128)S(1)}, f32[32,16,2]{1,2,0:T(2,128)}, u32[]{:S(2)}) copy-start(f32[32,16,2]{1,2,0:T(2,128)} %copy.70) | copy-start | bytes 12292
  73.0 5.6 %copy-start.13 = (pred[32]{0:T(512)(128)(4,1)S(1)}, pred[32]{0:T(512)(128)(4,1)}, u32[]{:S(2)}) copy-start(pred[32]{0:T(512)(128)(4,1)} %get-tuple-element.57) | copy-start | bytes 100
  73.0 5.6 %copy-start.19 = (f32[2]{0:T(128)S(1)}, f32[2]{0:T(128)}, u32[]{:S(2)}) copy-start(f32[2]{0:T(128)} %param.38) | copy-start | bytes 28
  73.0 5.6 %copy-start.2 = (f32[32,16,16]{2,1,0:T(8,128)S(1)}, f32[32,16,16]{2,1,0:T(8,128)}, u32[]{:S(2)}) copy-start(f32[32,16,16]{2,1,0:T(8,128)} %copy-done.1) | copy-start | bytes 98308
  80.8 5.1 %copy-start.14 = (f32[128]{0:T(128)S(1)}, f32[128]{0:T(128)}, u32[]{:S(2)}) copy-start(f32[128]{0:T(128)} %param.39) | copy-start | bytes 1540
  123.5 40.1 %all-to-all-start.1 = ((bf16[48,2,64,128]{3,2,1,0:T(8,128)(2,1)}), bf16[48,2,64,128]{3,2,1,0:T(8,128)(2,1)S(1)}, u32[]{:S(2)}, u32[]{:S(2)}) async-start(bf16[48,2,64,128]{3,2,1,0:T(8,128)(2,1)} %add_convert_fusion), calls=%async_computation.1 | async-start | bytes 3145728 | tf_op jit(solution)/shard_map/all_to_all | solution.py:352

commit v8 on v7

--- a/solution.py
+++ b/solution.py
@@ -192,6 +192,107 @@
         ],
         compiler_params=pltpu.CompilerParams(collective_id=collective_id, has_side_effects=True),
     )(src)
+
+
+def scatter2d_kernel(nz, width, src_ref, out_ref, mid_ref, stage_ref, sent_ref, held, ready,
+                     send_sem, recv_sem, load_sem, put_sem, local_sem):
+    y, z = lax.axis_index("by"), lax.axis_index("bz")
+    rep = lax.axis_index("rep")
+    right, left = lax.rem(y + 1, 4), lax.rem(y + 3, 4)
+    opposite = lax.rem(y + 2, 4)
+    half = nz // 2
+    first, second = pl.ds(0, half), pl.ds(half, half)
+
+    def remote(src, dst, index, yy, zz):
+        copy = pltpu.make_async_remote_copy(
+            src_ref=src,
+            dst_ref=dst,
+            send_sem=send_sem.at[index],
+            recv_sem=recv_sem.at[index],
+            device_id=(yy, zz, rep),
+            device_id_type=MESH,
+        )
+        copy.start()
+        return copy
+
+    barrier = pltpu.get_barrier_semaphore()
+    for offset in range(1, nz):
+        pl.semaphore_signal(
+            barrier, inc=1, device_id=(y, lax.rem(z + offset, nz), rep), device_id_type=MESH
+        )
+    for yy in (left, right):
+        pl.semaphore_signal(barrier, inc=1, device_id=(yy, z, rep), device_id_type=MESH)
+    pl.semaphore_wait(barrier, nz + 1)
+    local = pltpu.make_async_copy(src_ref.at[y], mid_ref.at[y], local_sem)
+    local.start()
+    to_right = remote(src_ref.at[right], mid_ref.at[y], 0, right, z)
+    to_left = remote(src_ref.at[left], mid_ref.at[y], 1, left, z)
+    stage_right = remote(src_ref.at[opposite, first], stage_ref.at[0], 2, right, z)
+    stage_left = remote(src_ref.at[opposite, second], stage_ref.at[1], 3, left, z)
+    stage_right.wait_recv()
+    pass_right = remote(stage_ref.at[0], mid_ref.at[left, first], 4, right, z)
+    stage_left.wait_recv()
+    pass_left = remote(stage_ref.at[1], mid_ref.at[right, second], 5, left, z)
+    local.wait()
+    to_right.wait()
+    to_left.wait()
+    pass_right.wait()
+    pass_left.wait()
+    stage_right.wait_send()
+    stage_left.wait_send()
+    column = lax.broadcasted_iota(jnp.int32, held.shape[1:], 1)
+    along_z = []
+    for offset in range(nz):
+        target = lax.rem(z + offset, nz)
+        load = pltpu.make_async_copy(mid_ref.at[:, target], held, load_sem)
+        load.start()
+        load.wait()
+        total = jnp.sum(held[...].astype(jnp.float32), axis=0)
+        squares = jnp.sum(
+            jnp.where((column == width) | (column == width + 1), total, 0.0), axis=1, keepdims=True
+        )
+        high = squares.astype(jnp.bfloat16).astype(jnp.float32)
+        low = squares - high
+        total = jnp.where(column == width, high, jnp.where(column == width + 1, low, total))
+        ready[offset] = total.astype(ready.dtype)
+        put = pltpu.make_async_copy(ready.at[offset], sent_ref.at[offset], put_sem)
+        put.start()
+        put.wait()
+        if offset == 0:
+            mine = pltpu.make_async_copy(sent_ref.at[0], out_ref.at[z], local_sem)
+            mine.start()
+        else:
+            along_z.append(remote(sent_ref.at[offset], out_ref.at[z], 6 + offset, y, target))
+    mine.wait()
+    for copy in along_z:
+        copy.wait()
+
+
+def scatter2d(src, width, collective_id):
+    nz = src.shape[1]
+    block = tuple(src.shape[2:])
+    kind = jax.ShapeDtypeStruct
+    return pl.pallas_call(
+        functools.partial(scatter2d_kernel, nz, width),
+        out_shape=(
+            kind((nz,) + block, src.dtype),
+            kind((4, nz) + block, src.dtype),
+            kind((2, nz // 2) + block, src.dtype),
+            kind((nz,) + block, src.dtype),
+        ),
+        in_specs=[pl.BlockSpec(memory_space=pl.ANY)],
+        out_specs=tuple(pl.BlockSpec(memory_space=pl.ANY) for _ in range(4)),
+        scratch_shapes=[
+            pltpu.VMEM((4,) + block, src.dtype),
+            pltpu.VMEM((nz,) + block, src.dtype),
+            pltpu.SemaphoreType.DMA((6 + nz,)),
+            pltpu.SemaphoreType.DMA((6 + nz,)),
+            pltpu.SemaphoreType.DMA,
+            pltpu.SemaphoreType.DMA,
+            pltpu.SemaphoreType.DMA,
+        ],
+        compiler_params=pltpu.CompilerParams(collective_id=collective_id, has_side_effects=True),
+    )(src)[0]
 
 
 def exchange(src, axis, gather, collective_id):
@@ -364,14 +465,7 @@
     extra = extra.at[:, 0].set(sq_hi).at[:, 1].set(sq_lo)
     n_y = lax.axis_size("by")
     packed = jnp.concatenate([partial, extra], 1).reshape(n_y, n_blk // n_y, local_rows, width + 128)
-    half_sum = jnp.sum(exchange4(packed, "by", False, 2).astype(jnp.float32), axis=0)
-    sq_mid = half_sum[:, :, width] + half_sum[:, :, width + 1]
-    sq_mid_hi = sq_mid.astype(jnp.bfloat16)
-    sq_mid_lo = (sq_mid - sq_mid_hi.astype(jnp.float32)).astype(jnp.bfloat16)
-    half_packed = (
-        half_sum.astype(jnp.bfloat16).at[:, :, width].set(sq_mid_hi).at[:, :, width + 1].set(sq_mid_lo)
-    )
-    summed = jnp.sum(exchange(half_packed, "bz", False, 3).astype(jnp.float32), axis=0)
+    summed = jnp.sum(scatter2d(packed, width, 2).astype(jnp.float32), axis=0)
     inner_all = inner_here * n_blk
     mean_sq = (summed[:, width] + summed[:, width + 1]) / inner_all
     mixed = (summed[:, :width] * lax.rsqrt(mean_sq + 1e-05)[:, None]).astype(jnp.bfloat16)

time: 166 us -> 173 us (1.042)
  Pallas kernels: 88.1 us -> 101 us
  starting transfers between devices: 17.3 us -> 13.5 us
  local copies, waits for them, and re-layouts: 12.7 us -> 9.11 us
  matrix products: 26.8 us -> 29.1 us
    pallas_call x2 -> x1, Pallas kernels: 51.3 us -> 64 us  [scatter2d(): pl.pallas_call(functools.partial(scatter2d_kernel, nz, width), out_shape=...]
    all_to_all x1, starting transfers between devices: 9.74 us -> 5.99 us  [shards(): lax.all_to_all(buffer.astype(jnp.bfloat16), 'rep', split_axis=0, concat_a...]
    scatter x2 -> x0, local copies, waits for them, and re-layouts: 3.41 us -> none  [shards(): half_sum.astype(jnp.bfloat16).at[:, :, width].set(sq_mid_hi)]
    reduce_sum x2 -> x1, other arithmetic: 3.56 us -> 1.21 us  [shards(): summed = jnp.sum(scatter2d(packed, width, 2).astype(jnp.float32), axis=0)]
  transfers between devices with their start and end apart: 2 -> 2, of which waited for: 0 -> 0; matrix products, arithmetic and copies ran while one was open for 20% -> 20% of each run, Pallas kernels for 35% -> 59%
where the time goes in v8:
time: 173 us; the launch traced here: 172 us
  Pallas kernels  101 us (58%)
  matrix products  29.1 us (17%)
  other arithmetic  17.9 us (10%)
  starting transfers between devices  13.5 us (8%)
  local copies, waits for them, and re-layouts  9.11 us (5%)
    pallas_call x1, Pallas kernels, scatter2d(): pl.pallas_call(functools.partial(scatter2d_kernel, nz, width), out_shape=...  64 us
    pallas_call x1, Pallas kernels, gather2d(): pl.pallas_call(functools.partial(gather2d_kernel, nz), out_shape=jax.Shap...  37 us
    dot_general x4, matrix products, shards(): jnp.dot(block_rows, weight_cols, preferred_element_type=jnp.float32)  11.4 us
    all_to_all x1, starting transfers between devices, shards(): lax.all_to_all(pool.astype(jnp.bfloat16), 'rep', split_axis=0, concat_axi...  7.54 us
    all_to_all x1, starting transfers between devices, shards(): lax.all_to_all(buffer.astype(jnp.bfloat16), 'rep', split_axis=0, concat_a...  5.99 us
    dot_general x2, matrix products, split_dot(): jnp.einsum(spec, low, narrow, preferred_element_type=jnp.float32)  5.39 us
    dot_general x2, matrix products, split_dot(): jnp.einsum(spec, high, narrow, preferred_element_type=jnp.float32)  4.7 us
    dot_general x1, matrix products, shards(): jnp.einsum('jhpn,jtn->jthp', fetched_half, to_slots(c_half), preferred_el...  3.71 us
  transfers between devices with their start and end apart: 2, of which 0 were waited for; matrix products, arithmetic and copies ran while one was open for 20% of the time, Pallas kernels for 59%

profile of v8, /device:TPU:1, one launch (start us, length us, event | category | flops | bytes accessed | tf_op | source)
XLA Modules:
  0.0 171.7 jit_solution(11947983244298852098)
XLA Ops:
  0.6 3.6 %convert_element_type.145 = bf16[48,2,64,128]{3,2,1,0:T(8,128)(2,1)} convert(f32[48,2,64,128]{3,2,1,0:T(8,128)} %param.39) | non-fusion elementwise | flops 786432 | bytes 4718592 | tf_op jit(solution)/shard_map/convert_element_type | solution.py:434
  4.2 7.5 %all-to-all-start = ((bf16[48,2,64,128]{3,2,1,0:T(8,128)(2,1)}), bf16[48,2,64,128]{3,2,1,0:T(8,128)(2,1)}, u32[]{:S(2)}, u32[]{:S(2)}) async-start(bf16[48,2,64,128]{3,2,1,0:T(8,128)(2,1)} %convert_element_type.145), calls=%async_computation | async-start | bytes 3145728 | tf_op jit(solution)/shard_map/all_to_all | solution.py:433
  11.8 0.2 convert_reduce_fusion.2
  12.1 0.5 and_bitcast_fusion
  12.6 0.7 compare_reduce_fusion
  13.2 0.7 compare_reduce_fusion.1
  13.9 37.0 %shard_map.194 = bf16[4,8,16,2560]{3,2,1,0:T(8,128)(2,1)} custom-call(bf16[16,2560]{1,0:T(8,128)(2,1)} %bitcast.76), custom_call_target="tpu_custom_call" | custom-call | tf_op jit(solution)/shard_map/pallas_call | solution.py:183
  50.9 2.5 %fusion.4 = f32[512,2]{0,1:T(2,128)S(1)} fusion(bf16[512,2560]{1,0:T(8,128)(2,1)} %bitcast.70, bf16[2560,2]{0,1:T(2,128)(2,1)S(1)} %copy-done.8), kind=kOutput, calls=%fused_computation.20 | convolution fusion | flops 5244928 | bytes 2635776 | tf_op jit(solution)/shard_map/dot_general | solution.py:371
  53.6 0.2 reduce-window.4
  53.9 0.2 fusion.46
  54.2 0.2 copy.67
  54.4 0.7 fusion.67
  55.1 0.9 copy.68
  56.0 0.2 copy.82
  56.5 2.6 %convolution_convert_fusion.1 = bf16[512,256]{1,0:T(8,128)(2,1)S(1)} fusion(bf16[512,2560]{1,0:T(8,128)(2,1)} %bitcast.71, bf16[2560,256]{1,0:T(8,128)(2,1)S(1)} %copy-done), kind=kOutput, calls=%fused_computation.15 | convolution fusion | flops 671219712 | bytes 4194304 | tf_op jit(solution)/shard_map/dot_general | solution.py:371
  59.3 0.7 copy.70
  60.0 2.6 %convolution_convert_fusion.3 = bf16[512,128]{1,0:T(8,128)(2,1)S(1)} fusion(bf16[512,2560]{1,0:T(8,128)(2,1)} %bitcast.72, bf16[2560,128]{1,0:T(8,128)(2,1)S(1)} %copy-done.16), kind=kOutput, calls=%fused_computation.18 | convolution fusion | flops 335609856 | bytes 3407872 | tf_op jit(solution)/shard_map/dot_general | solution.py:371
  62.8 0.2 multiply_convert_fusion.2
  63.1 0.3 copy.76
  63.7 0.3 multiply_convert_fusion
  64.1 0.6 pad_clamp_fusion
  64.7 0.6 gather_fusion
  65.4 0.2 convert_multiply_fusion
  65.6 0.6 gather_fusion.3
  66.2 0.6 gather_fusion.4
  66.8 0.6 gather_fusion.5
  67.4 0.6 gather_fusion.2
  68.1 0.2 select_select_fusion.4
  68.3 0.2 fusion.62
  68.5 2.1 %fusion.30 = f32[32,2,64,16]{2,3,1,0:T(8,128)} fusion(f32[32,16,16]{2,1,0:T(8,128)S(1)} %fusion.62, f32[32,16,2]{1,2,0:T(2,128)} %copy.70, f32[32,16,2]{1,2,0:T(2,128)} %copy.68, pred[16,16]{1,0:T(8,128)(4,1)S(1)} %iota_compare_fusion.6, bf16[32,16,2,64]{3,2,1,0:T(2,128)(2,1)S(1)} %reshape.335), kind=kOutput, calls=%fused_computation.66 | convolution fusion | flops 2195456 | bytes 434432 | tf_op jit(solution)/shard_map/rtsh,rshp->rthp/dot_general | solution.py:329
  70.5 2.6 %fusion.10 = f32[48,2,64,128]{3,2,1,0:T(8,128)} fusion(f32[48,16,2,64]{3,1,2,0:T(8,128)S(1)} %gather_fusion.3, pred[48]{0:T(512)(128)(4,1)S(1)} %get-tuple-element.51, pred[48]{0:T(512)(128)(4,1)S(1)} %get-tuple-element.52, bf16[48,16,128]{2,1,0:T(8,128)(2,1)S(1)} %gather_fusion.5), kind=kOutput, calls=%fused_computation.37 | convolution fusion | flops 25559040 | bytes 3735648 | tf_op jit(solution)/shard_map/jshp,jsn->jhpn/dot_general | solution.py:329
  73.2 3.7 %convolution_multiply_fusion = f32[48,16,2,64]{3,1,2,0:T(8,128)} fusion(bf16[48,2,64,128]{3,2,1,0:T(8,128)(2,1)} %all-to-all-done, f32[48,16,2]{1,2,0:T(2,128)S(1)} %select_select_fusion.4, bf16[48,16,128]{2,1,0:T(8,128)(2,1)S(1)} %gather_fusion.4, pred[48]{0:T(512)(128)(4,1)S(1)} %get-tuple-element.51, pred[48]{0:T(512)(128)(4,1)S(1)} %get-tuple-element.52), kind=kOutput, calls=%fused_computation.10 | convolution fusion | flops 25460736 | bytes 2168928 | tf_op jit(solution)/shard_map/jhpn,jtn->jthp/dot_general | solution.py:446
  76.9 1.8 %gather_fusion.1 = f32[32,16,2,64]{3,1,2,0:T(8,128)S(1)} fusion(f32[48,16,2,64]{3,1,2,0:T(8,128)} %convolution_multiply_fusion, s32[1024]{0:T(1024)} %pad_clamp_fusion), kind=kCustom, calls=%fused_computation.3 | custom fusion | bytes 524416 | tf_op jit(solution)/shard_map/jit(_take)/gather | solution.py:449
  78.8 1.4 fusion.2
  80.3 0.3 copy.77
  80.6 0.3 reshape.338
  81.0 3.7 %multiply_reduce_fusion.1 = (f32[512]{0:T(512)S(1)}, f32[512,128]{0,1:T(8,128)}) fusion(f32[512,128]{0,1:T(8,128)S(1)} %copy.78, bf16[512,2560]{1,0:T(8,128)(2,1)} %bitcast.73, bf16[2560,128]{1,0:T(8,128)(2,1)} %param.26), kind=kOutput, calls=%fused_computation.56 | convolution fusion | flops 336133632 | bytes 3803136 | tf_op jit(solution)/shard_map/dot_general | solution.py:371
  84.8 4.0 %add_convert_fusion = bf16[48,2,64,128]{3,2,1,0:T(8,128)(2,1)} fusion(f32[48,2,64,128]{3,2,1,0:T(8,128)} %fusion.10, bf16[48,2,64,128]{3,2,1,0:T(8,128)(2,1)} %all-to-all-done, f32[48,2]{1,0:T(8,128)S(1)} %select_select_fusion.5, f32[48,16,2,64]{3,1,2,0:T(8,128)S(1)} %gather_fusion.3, pred[48]{0:T(512)(128)(4,1)S(1)} %get-tuple-element.51, ...), kind=kOutput, calls=%fused_computation.7 | convolution fusion | flops 29884416 | bytes 6881760 | tf_op jit(solution)/shard_map/jshp,jsn->jhpn/dot_general | solution.py:329
  88.8 6.0 %all-to-all-start.1 = ((bf16[48,2,64,128]{3,2,1,0:T(8,128)(2,1)}), bf16[48,2,64,128]{3,2,1,0:T(8,128)(2,1)S(1)}, u32[]{:S(2)}, u32[]{:S(2)}) async-start(bf16[48,2,64,128]{3,2,1,0:T(8,128)(2,1)} %add_convert_fusion), calls=%async_computation.1 | async-start | bytes 3145728 | tf_op jit(solution)/shard_map/all_to_all | solution.py:453
  94.8 3.5 %convolution_convert_fusion = bf16[512,2560]{1,0:T(8,128)(2,1)} fusion(bf16[128,2560]{1,0:T(8,128)(2,1)} %param.36, f32[512,128]{0,1:T(8,128)S(1)} %copy-done.3, f32[128]{0:T(128)S(1)} %copy-done.15), kind=kOutput, calls=%fused_computation.6 | convolution fusion | flops 336986112 | bytes 3539456 | tf_op jit(solution)/shard_map/dot_general | solution.py:462
  98.3 1.3 fusion.40
  99.7 0.4 scatter.9
  100.1 3.5 %pad_maximum_fusion = bf16[512,2688]{1,0:T(8,128)(2,1)} fusion(bf16[512,128]{1,0:T(8,128)(2,1)S(1)} %scatter.9, bf16[512,2560]{1,0:T(8,128)(2,1)} %convolution_convert_fusion), kind=kLoop, calls=%fused_computation.8 | loop fusion | flops 5505024 | bytes 5505024 | tf_op jit(solution)/shard_map/concatenate | solution.py:467
  103.5 64.0 %shard_map.195 = (bf16[8,16,2688]{2,1,0:T(8,128)(2,1)}, bf16[4,8,16,2688]{3,2,1,0:T(8,128)(2,1)}, bf16[2,4,16,2688]{3,2,1,0:T(8,128)(2,1)}, bf16[8,16,2688]{2,1,0:T(8,128)(2,1)}) custom-call(bf16[4,8,16,2688]{3,2,1,0:T(8,128)(2,1)} %bitcast.69), custom_call_target="tpu_custom_call" | custom-call | tf_op jit(solution)/shard_map/pallas_call | solution.py:275
  167.5 1.2 convert_reduce_fusion
  168.7 0.2 fusion.50
  168.9 0.7 fusion.44
  169.7 2.1 %convert_element_type.160 = f32[48,2,64,128]{3,2,1,0:T(8,128)} convert(bf16[48,2,64,128]{3,2,1,0:T(8,128)(2,1)S(1)} %all-to-all-done.1) | non-fusion elementwise | flops 786432 | bytes 4718592 | tf_op jit(solution)/shard_map/convert_element_type | solution.py:455
  (83 shorter events, 2.1 us)
Async XLA Ops:
  0.6 55.8 %copy-start = (bf16[2560,256]{1,0:T(8,128)(2,1)S(1)}, bf16[2560,256]{1,0:T(8,128)(2,1)}, u32[]{:S(2)}) copy-start(bf16[2560,256]{1,0:T(8,128)(2,1)} %param.28) | copy-start | bytes 3932164
  4.2 7.6 %copy-start.12 = (s32[32,1]{0,1:T(1,128)S(1)}, s32[32,1]{0,1:T(1,128)}, u32[]{:S(2)}) copy-start(s32[32,1]{0,1:T(1,128)} %param.41) | copy-start | bytes 388
  4.2 46.7 %copy-start.18 = (f32[2]{0:T(128)S(1)}, f32[2]{0:T(128)}, u32[]{:S(2)}) copy-start(f32[2]{0:T(128)} %param.33) | copy-start | bytes 28
  4.2 46.7 %copy-start.8 = (bf16[2560,2]{0,1:T(2,128)(2,1)S(1)}, bf16[2560,2]{0,1:T(2,128)(2,1)}, u32[]{:S(2)}) copy-start(bf16[2560,2]{0,1:T(2,128)(2,1)} %param.29) | copy-start | bytes 30724
  4.2 69.0 %all-to-all-start = ((bf16[48,2,64,128]{3,2,1,0:T(8,128)(2,1)}), bf16[48,2,64,128]{3,2,1,0:T(8,128)(2,1)}, u32[]{:S(2)}, u32[]{:S(2)}) async-start(bf16[48,2,64,128]{3,2,1,0:T(8,128)(2,1)} %convert_element_type.145), calls=%async_computation | async-start | bytes 3145728 | tf_op jit(solution)/shard_map/all_to_all | solution.py:433
  13.9 39.7 %copy-start.19 = (s32[4]{0:T(128)S(1)}, s32[4]{0:T(128)}, u32[]{:S(2)}) copy-start(s32[4]{0:T(128)} %param.40) | copy-start | bytes 52
  13.9 40.0 %copy-start.17 = (f32[4,2]{0,1:T(2,128)S(1)}, f32[4,2]{0,1:T(2,128)}, u32[]{:S(2)}) copy-start(f32[4,2]{0,1:T(2,128)} %param.32) | copy-start | bytes 100
  50.9 5.2 %copy-start.11 = (s32[32]{0:T(128)S(1)}, s32[32]{0:T(128)}, u32[]{:S(2)}) copy-start(s32[32]{0:T(128)} %param.42) | copy-start | bytes 388
  56.2 2.9 %copy-start.13 = (s32[32]{0:T(128)S(1)}, s32[32]{0:T(128)}, u32[]{:S(2)}) copy-start(s32[32]{0:T(128)} %param.43) | copy-start | bytes 388
  56.2 3.1 %copy-start.9 = (f32[4,256]{1,0:T(4,128)S(1)}, f32[4,256]{1,0:T(4,128)}, u32[]{:S(2)}) copy-start(f32[4,256]{1,0:T(4,128)} %param.31) | copy-start | bytes 12292
  56.3 3.7 %copy-start.16 = (bf16[2560,128]{1,0:T(8,128)(2,1)S(1)}, bf16[2560,128]{1,0:T(8,128)(2,1)}, u32[]{:S(2)}) copy-start(bf16[2560,128]{1,0:T(8,128)(2,1)} %param.27) | copy-start | bytes 1966084
  59.1 3.5 %copy-start.7 = (bf16[32,3,128]{2,0,1:T(8,128)(2,1)S(1)}, bf16[32,3,128]{2,0,1:T(8,128)(2,1)}, u32[]{:S(2)}) copy-start(bf16[32,3,128]{2,0,1:T(8,128)(2,1)} %param.37) | copy-start | bytes 73732
  59.1 3.6 %copy-start.10 = (f32[4,128]{1,0:T(4,128)S(1)}, f32[4,128]{1,0:T(4,128)}, u32[]{:S(2)}) copy-start(f32[4,128]{1,0:T(4,128)} %param.30) | copy-start | bytes 6148
  60.0 3.4 %copy-start.4 = (bf16[32,3,256]{2,0,1:T(8,128)(2,1)S(1)}, bf16[32,3,256]{2,0,1:T(8,128)(2,1)}, u32[]{:S(2)}) copy-start(bf16[32,3,256]{2,0,1:T(8,128)(2,1)} %param.38) | copy-start | bytes 147460
  68.5 4.7 %copy-start.1 = (f32[32,16,16]{2,1,0:T(8,128)}, f32[32,16,16]{2,1,0:T(8,128)S(1)}, u32[]{:S(2)}) copy-start(f32[32,16,16]{2,1,0:T(8,128)S(1)} %fusion.62) | copy-start | bytes 98308
  73.2 5.6 %copy-start.5 = (f32[32,16,2]{1,2,0:T(2,128)S(1)}, f32[32,16,2]{1,2,0:T(2,128)}, u32[]{:S(2)}) copy-start(f32[32,16,2]{1,2,0:T(2,128)} %copy.68) | copy-start | bytes 12292
  73.2 5.6 %copy-start.6 = (f32[32,16,2]{1,2,0:T(2,128)S(1)}, f32[32,16,2]{1,2,0:T(2,128)}, u32[]{:S(2)}) copy-start(f32[32,16,2]{1,2,0:T(2,128)} %copy.70) | copy-start | bytes 12292
  73.2 5.6 %copy-start.14 = (pred[32]{0:T(512)(128)(4,1)S(1)}, pred[32]{0:T(512)(128)(4,1)}, u32[]{:S(2)}) copy-start(pred[32]{0:T(512)(128)(4,1)} %get-tuple-element.31) | copy-start | bytes 100
  73.2 5.6 %copy-start.20 = (f32[2]{0:T(128)S(1)}, f32[2]{0:T(128)}, u32[]{:S(2)}) copy-start(f32[2]{0:T(128)} %param.34) | copy-start | bytes 28
  73.2 5.6 %copy-start.2 = (f32[32,16,16]{2,1,0:T(8,128)S(1)}, f32[32,16,16]{2,1,0:T(8,128)}, u32[]{:S(2)}) copy-start(f32[32,16,16]{2,1,0:T(8,128)} %copy-done.1) | copy-start | bytes 98308
  88.8 6.0 %copy-start.3 = (f32[512,128]{0,1:T(8,128)S(1)}, f32[512,128]{0,1:T(8,128)}, u32[]{:S(2)}) copy-start(f32[512,128]{0,1:T(8,128)} %get-tuple-element.50) | copy-start | bytes 786436
  88.8 6.0 %copy-start.15 = (f32[128]{0:T(128)S(1)}, f32[128]{0:T(128)}, u32[]{:S(2)}) copy-start(f32[128]{0:T(128)} %param.35) | copy-start | bytes 1540
  88.8 80.9 %all-to-all-start.1 = ((bf16[48,2,64,128]{3,2,1,0:T(8,128)(2,1)}), bf16[48,2,64,128]{3,2,1,0:T(8,128)(2,1)S(1)}, u32[]{:S(2)}, u32[]{:S(2)}) async-start(bf16[48,2,64,128]{3,2,1,0:T(8,128)(2,1)} %add_convert_fusion), calls=%async_computation.1 | async-start | bytes 3145728 | tf_op jit(solution)/shard_map/all_to_all | solution.py:453

commit v9 on v7

--- a/solution.py
+++ b/solution.py
@@ -155,22 +155,26 @@
         along_z.append(copy)
     to_right = [remote(src_ref, dst_ref.at[y, z], r_sem, right, z)]
     to_left = [remote(src_ref, dst_ref.at[y, z], l_sem, left, z)]
+    relays = []
+
+    def relay(offset):
+        zs = lax.rem(z + nz - offset, nz)
+        to_right[offset].wait_recv()
+        relays.append(
+            remote(dst_ref.at[left, zs, first], dst_ref.at[left, zs, first], ra_sem + offset, right, z)
+        )
+        to_left[offset].wait_recv()
+        relays.append(
+            remote(dst_ref.at[right, zs, second], dst_ref.at[right, zs, second], lb_sem + offset, left, z)
+        )
+
     for offset in range(1, nz):
         along_z[offset - 1].wait_recv()
         zs = lax.rem(z + nz - offset, nz)
         to_right.append(remote(dst_ref.at[y, zs], dst_ref.at[y, zs], r_sem + offset, right, z))
         to_left.append(remote(dst_ref.at[y, zs], dst_ref.at[y, zs], l_sem + offset, left, z))
-    relays = []
-    for offset in range(nz):
-        zs = lax.rem(z + nz - offset, nz)
-        to_right[offset].wait_recv()
-        relays.append(
-            remote(dst_ref.at[left, zs, first], dst_ref.at[left, zs, first], ra_sem + offset, right, z)
-        )
-        to_left[offset].wait_recv()
-        relays.append(
-            remote(dst_ref.at[right, zs, second], dst_ref.at[right, zs, second], lb_sem + offset, left, z)
-        )
+        relay(offset - 1)
+    relay(nz - 1)
     local.wait()
     for copy in along_z + to_right + to_left:
         copy.wait_send()

time: 166 us -> 167 us (level)
  no operation moved by 1% of the time
where the time goes in v9:
time: 167 us; the launch traced here: 166 us
  Pallas kernels  87.7 us (53%)
  matrix products  26.8 us (16%)
  other arithmetic  19.5 us (12%)
  starting transfers between devices  18 us (11%)
  local copies, waits for them, and re-layouts  12.7 us (8%)
    pallas_call x1, Pallas kernels, gather2d(): pl.pallas_call(functools.partial(gather2d_kernel, nz), out_shape=jax.Shap...  35.8 us
    pallas_call x1, Pallas kernels, exchange4(): pl.pallas_call(functools.partial(ring4_kernel, axis, gather), out_shape=(...  29.9 us
    pallas_call x1, Pallas kernels, exchange(): pl.pallas_call(functools.partial(exchange_kernel, n, axis, gather), out_s...  22.1 us
    dot_general x4, matrix products, shards(): jnp.dot(block_rows, weight_cols, preferred_element_type=jnp.float32)  10.7 us
    all_to_all x1, starting transfers between devices, shards(): lax.all_to_all(buffer.astype(jnp.bfloat16), 'rep', split_axis=0, concat_a...  10.5 us
    all_to_all x1, starting transfers between devices, shards(): lax.all_to_all(pool.astype(jnp.bfloat16), 'rep', split_axis=0, concat_axi...  7.55 us
    dot_general x2, matrix products, split_dot(): jnp.einsum(spec, low, narrow, preferred_element_type=jnp.float32)  5.37 us
    dot_general x2, matrix products, split_dot(): jnp.einsum(spec, high, narrow, preferred_element_type=jnp.float32)  4.69 us
  transfers between devices with their start and end apart: 2, of which 0 were waited for; matrix products, arithmetic and copies ran while one was open for 20% of the time, Pallas kernels for 35%

profile of v9, /device:TPU:1, one launch (start us, length us, event | category | flops | bytes accessed | tf_op | source)
XLA Modules:
  0.0 165.9 jit_solution(4137052418891580061)
XLA Ops:
  0.6 3.5 %convert_element_type.164 = bf16[48,2,64,128]{3,2,1,0:T(8,128)(2,1)} convert(f32[48,2,64,128]{3,2,1,0:T(8,128)} %param.43) | non-fusion elementwise | flops 786432 | bytes 4718592 | tf_op jit(solution)/shard_map/convert_element_type | solution.py:337
  4.2 7.6 %all-to-all-start = ((bf16[48,2,64,128]{3,2,1,0:T(8,128)(2,1)}), bf16[48,2,64,128]{3,2,1,0:T(8,128)(2,1)}, u32[]{:S(2)}, u32[]{:S(2)}) async-start(bf16[48,2,64,128]{3,2,1,0:T(8,128)(2,1)} %convert_element_type.164), calls=%async_computation | async-start | bytes 3145728 | tf_op jit(solution)/shard_map/all_to_all | solution.py:336
  12.0 0.5 and_bitcast_fusion
  12.5 0.6 compare_reduce_fusion
  13.2 0.7 compare_reduce_fusion.1
  13.9 35.8 %shard_map.194 = bf16[4,8,16,2560]{3,2,1,0:T(8,128)(2,1)} custom-call(bf16[16,2560]{1,0:T(8,128)(2,1)} %bitcast.76), custom_call_target="tpu_custom_call" | custom-call | tf_op jit(solution)/shard_map/pallas_call | solution.py:187
  49.7 2.5 %fusion.4 = f32[512,2]{0,1:T(2,128)S(1)} fusion(bf16[512,2560]{1,0:T(8,128)(2,1)} %bitcast.70, bf16[2560,2]{0,1:T(2,128)(2,1)S(1)} %copy-done.7), kind=kOutput, calls=%fused_computation.21 | convolution fusion | flops 5244928 | bytes 2635776 | tf_op jit(solution)/shard_map/dot_general | solution.py:274
  52.4 0.2 reduce-window.4
  52.7 0.2 fusion.47
  53.1 0.7 fusion.69
  53.9 0.9 copy.68
  55.2 2.6 %convolution_convert_fusion.1 = bf16[512,256]{1,0:T(8,128)(2,1)S(1)} fusion(bf16[512,2560]{1,0:T(8,128)(2,1)} %bitcast.71, bf16[2560,256]{1,0:T(8,128)(2,1)S(1)} %copy-done), kind=kOutput, calls=%fused_computation.16 | convolution fusion | flops 671219712 | bytes 4194304 | tf_op jit(solution)/shard_map/dot_general | solution.py:274
  58.1 0.7 copy.70
  58.8 2.6 %convolution_convert_fusion.3 = bf16[512,128]{1,0:T(8,128)(2,1)S(1)} fusion(bf16[512,2560]{1,0:T(8,128)(2,1)} %bitcast.72, bf16[2560,128]{1,0:T(8,128)(2,1)S(1)} %copy-done.15), kind=kOutput, calls=%fused_computation.19 | convolution fusion | flops 335609856 | bytes 3407872 | tf_op jit(solution)/shard_map/dot_general | solution.py:274
  61.9 0.3 copy.76
  62.4 0.3 multiply_convert_fusion
  62.8 0.6 pad_clamp_fusion
  63.5 0.6 gather_fusion
  64.2 0.2 convert_multiply_fusion
  64.4 0.6 gather_fusion.3
  65.0 0.6 gather_fusion.4
  65.6 0.6 gather_fusion.5
  66.2 0.6 gather_fusion.2
  67.1 0.2 fusion.63
  67.3 2.0 %fusion.30 = f32[32,2,64,16]{2,3,1,0:T(8,128)} fusion(f32[32,16,16]{2,1,0:T(8,128)S(1)} %fusion.63, f32[32,16,2]{1,2,0:T(2,128)} %copy.70, f32[32,16,2]{1,2,0:T(2,128)} %copy.68, pred[16,16]{1,0:T(8,128)(4,1)S(1)} %iota_compare_fusion.6, bf16[32,16,2,64]{3,2,1,0:T(2,128)(2,1)S(1)} %reshape.390), kind=kOutput, calls=%fused_computation.67 | convolution fusion | flops 2195456 | bytes 434432 | tf_op jit(solution)/shard_map/rtsh,rshp->rthp/dot_general | solution.py:232
  69.3 2.6 %fusion.10 = f32[48,2,64,128]{3,2,1,0:T(8,128)} fusion(f32[48,16,2,64]{3,1,2,0:T(8,128)S(1)} %gather_fusion.3, pred[48]{0:T(512)(128)(4,1)S(1)} %get-tuple-element.77, pred[48]{0:T(512)(128)(4,1)S(1)} %get-tuple-element.78, bf16[48,16,128]{2,1,0:T(8,128)(2,1)S(1)} %gather_fusion.5), kind=kOutput, calls=%fused_computation.38 | convolution fusion | flops 25559040 | bytes 3735648 | tf_op jit(solution)/shard_map/jshp,jsn->jhpn/dot_general | solution.py:232
  72.0 3.7 %convolution_multiply_fusion = f32[48,16,2,64]{3,1,2,0:T(8,128)} fusion(bf16[48,2,64,128]{3,2,1,0:T(8,128)(2,1)} %all-to-all-done, f32[48,16,2]{1,2,0:T(2,128)S(1)} %select_select_fusion.4, bf16[48,16,128]{2,1,0:T(8,128)(2,1)S(1)} %gather_fusion.4, pred[48]{0:T(512)(128)(4,1)S(1)} %get-tuple-element.77, pred[48]{0:T(512)(128)(4,1)S(1)} %get-tuple-element.78), kind=kOutput, calls=%fused_computation.11 | convolution fusion | flops 25460736 | bytes 2168928 | tf_op jit(solution)/shard_map/jhpn,jtn->jthp/dot_general | solution.py:349
  75.7 1.8 %gather_fusion.1 = f32[32,16,2,64]{3,1,2,0:T(8,128)S(1)} fusion(f32[48,16,2,64]{3,1,2,0:T(8,128)} %convolution_multiply_fusion, s32[1024]{0:T(1024)} %pad_clamp_fusion), kind=kCustom, calls=%fused_computation.3 | custom fusion | bytes 524416 | tf_op jit(solution)/shard_map/jit(_take)/gather | solution.py:352
  77.6 1.4 fusion.2
  79.0 0.3 copy.77
  79.3 0.3 reshape.393
  79.8 3.0 %multiply_reduce_fusion.1 = (f32[512]{0:T(512)S(1)}, f32[512,128]{0,1:T(8,128)S(1)}) fusion(f32[512,128]{0,1:T(8,128)S(1)} %copy.78, bf16[512,2560]{1,0:T(8,128)(2,1)} %bitcast.73, bf16[2560,128]{1,0:T(8,128)(2,1)} %param.30), kind=kOutput, calls=%fused_computation.57 | convolution fusion | flops 336133632 | bytes 3803136 | tf_op jit(solution)/shard_map/dot_general | solution.py:274
  82.9 1.3 fusion.40
  84.2 0.6 scatter.15
  84.8 2.0 %convolution_convert_fusion = bf16[512,2560]{1,0:T(8,128)(2,1)S(1)} fusion(bf16[128,2560]{1,0:T(8,128)(2,1)} %param.40, f32[512,128]{0,1:T(8,128)S(1)} %get-tuple-element.76, f32[128]{0:T(128)S(1)} %copy-done.14), kind=kOutput, calls=%fused_computation.7 | convolution fusion | flops 336986112 | bytes 3539456 | tf_op jit(solution)/shard_map/dot_general | solution.py:365
  86.9 1.8 %pad_maximum_fusion = bf16[512,2688]{1,0:T(8,128)(2,1)} fusion(bf16[512,128]{1,0:T(8,128)(2,1)S(1)} %scatter.15, bf16[512,2560]{1,0:T(8,128)(2,1)S(1)} %convolution_convert_fusion), kind=kLoop, calls=%fused_computation.9 | loop fusion | flops 5505024 | bytes 5505024 | tf_op jit(solution)/shard_map/concatenate | solution.py:370
  88.6 29.9 %shard_map.195 = (bf16[4,8,16,2688]{3,2,1,0:T(8,128)(2,1)}, bf16[2,4,16,2688]{3,2,1,0:T(8,128)(2,1)}) custom-call(bf16[4,8,16,2688]{3,2,1,0:T(8,128)(2,1)} %bitcast.69), custom_call_target="tpu_custom_call" | custom-call | tf_op jit(solution)/shard_map/pallas_call | solution.py:107
  118.5 3.9 %add_convert_fusion = bf16[48,2,64,128]{3,2,1,0:T(8,128)(2,1)} fusion(f32[48,2,64,128]{3,2,1,0:T(8,128)} %fusion.10, bf16[48,2,64,128]{3,2,1,0:T(8,128)(2,1)} %all-to-all-done, f32[48,2]{1,0:T(8,128)S(1)} %select_select_fusion.5, f32[48,16,2,64]{3,1,2,0:T(8,128)S(1)} %gather_fusion.3, pred[48]{0:T(512)(128)(4,1)S(1)} %get-tuple-element.77, ...), kind=kOutput, calls=%fused_computation.8 | convolution fusion | flops 29884416 | bytes 6881760 | tf_op jit(solution)/shard_map/jshp,jsn->jhpn/dot_general | solution.py:232
  122.4 10.5 %all-to-all-start.1 = ((bf16[48,2,64,128]{3,2,1,0:T(8,128)(2,1)}), bf16[48,2,64,128]{3,2,1,0:T(8,128)(2,1)S(1)}, u32[]{:S(2)}, u32[]{:S(2)}) async-start(bf16[48,2,64,128]{3,2,1,0:T(8,128)(2,1)} %add_convert_fusion), calls=%async_computation.1 | async-start | bytes 3145728 | tf_op jit(solution)/shard_map/all_to_all | solution.py:356
  132.9 2.4 %convert_reduce_fusion = f32[8,16,2688]{2,1,0:T(8,128)S(1)} fusion(bf16[4,8,16,2688]{3,2,1,0:T(8,128)(2,1)} %get-tuple-element.52), kind=kLoop, calls=%fused_computation.6 | loop fusion | flops 2408448 | bytes 4128768 | tf_op jit(solution)/shard_map/reduce_sum | solution.py:371
  135.2 0.9 convert_element_type.172
  136.2 1.4 scatter.16
  137.7 2.0 %scatter.19.src_ref = bf16[8,16,2688]{2,1,0:T(8,128)(2,1)} dynamic-update-slice(bf16[8,16,2688]{2,1,0:T(8,128)(2,1)} %scatter.16, bf16[8,16,1]{2,1,0:T(8,128)(2,1)S(1)} %get-tuple-element.55, s32[]{:T(128)} %constant.199.clone.1, s32[]{:T(128)} %constant.199.clone.1, s32[]{:T(128)} %constant.211.clone.1) | dynamic-update-slice | bytes 516 | tf_op jit(solution)/shard_map/scatter | solution.py:376
  139.7 22.1 %shard_map.196 = bf16[8,16,2688]{2,1,0:T(8,128)(2,1)} custom-call(bf16[8,16,2688]{2,1,0:T(8,128)(2,1)} %scatter.19.src_ref), custom_call_target="tpu_custom_call" | custom-call | tf_op jit(solution)/shard_map/pallas_call | solution.py:204
  161.8 1.2 convert_reduce_fusion.1
  163.0 0.2 fusion.51
  163.2 0.7 fusion.44
  163.9 2.1 %convert_element_type.184 = f32[48,2,64,128]{3,2,1,0:T(8,128)} convert(bf16[48,2,64,128]{3,2,1,0:T(8,128)(2,1)S(1)} %all-to-all-done.1) | non-fusion elementwise | flops 786432 | bytes 4718592 | tf_op jit(solution)/shard_map/convert_element_type | solution.py:358
  (87 shorter events, 3.0 us)
Async XLA Ops:
  0.6 54.6 %copy-start = (bf16[2560,256]{1,0:T(8,128)(2,1)S(1)}, bf16[2560,256]{1,0:T(8,128)(2,1)}, u32[]{:S(2)}) copy-start(bf16[2560,256]{1,0:T(8,128)(2,1)} %param.32) | copy-start | bytes 3932164
  4.2 7.6 %copy-start.11 = (s32[32,1]{0,1:T(1,128)S(1)}, s32[32,1]{0,1:T(1,128)}, u32[]{:S(2)}) copy-start(s32[32,1]{0,1:T(1,128)} %param.45) | copy-start | bytes 388
  4.2 45.5 %copy-start.17 = (f32[2]{0:T(128)S(1)}, f32[2]{0:T(128)}, u32[]{:S(2)}) copy-start(f32[2]{0:T(128)} %param.37) | copy-start | bytes 28
  4.2 45.5 %copy-start.7 = (bf16[2560,2]{0,1:T(2,128)(2,1)S(1)}, bf16[2560,2]{0,1:T(2,128)(2,1)}, u32[]{:S(2)}) copy-start(bf16[2560,2]{0,1:T(2,128)(2,1)} %param.33) | copy-start | bytes 30724
  4.2 67.8 %all-to-all-start = ((bf16[48,2,64,128]{3,2,1,0:T(8,128)(2,1)}), bf16[48,2,64,128]{3,2,1,0:T(8,128)(2,1)}, u32[]{:S(2)}, u32[]{:S(2)}) async-start(bf16[48,2,64,128]{3,2,1,0:T(8,128)(2,1)} %convert_element_type.164), calls=%async_computation | async-start | bytes 3145728 | tf_op jit(solution)/shard_map/all_to_all | solution.py:336
  13.9 38.5 %copy-start.18 = (s32[4]{0:T(128)S(1)}, s32[4]{0:T(128)}, u32[]{:S(2)}) copy-start(s32[4]{0:T(128)} %param.44) | copy-start | bytes 52
  13.9 38.8 %copy-start.16 = (f32[4,2]{0,1:T(2,128)S(1)}, f32[4,2]{0,1:T(2,128)}, u32[]{:S(2)}) copy-start(f32[4,2]{0,1:T(2,128)} %param.36) | copy-start | bytes 100
  49.7 5.2 %copy-start.10 = (s32[32]{0:T(128)S(1)}, s32[32]{0:T(128)}, u32[]{:S(2)}) copy-start(s32[32]{0:T(128)} %param.46) | copy-start | bytes 388
  54.9 2.9 %copy-start.12 = (s32[32]{0:T(128)S(1)}, s32[32]{0:T(128)}, u32[]{:S(2)}) copy-start(s32[32]{0:T(128)} %param.47) | copy-start | bytes 388
  54.9 3.1 %copy-start.8 = (f32[4,256]{1,0:T(4,128)S(1)}, f32[4,256]{1,0:T(4,128)}, u32[]{:S(2)}) copy-start(f32[4,256]{1,0:T(4,128)} %param.35) | copy-start | bytes 12292
  55.1 3.7 %copy-start.15 = (bf16[2560,128]{1,0:T(8,128)(2,1)S(1)}, bf16[2560,128]{1,0:T(8,128)(2,1)}, u32[]{:S(2)}) copy-start(bf16[2560,128]{1,0:T(8,128)(2,1)} %param.31) | copy-start | bytes 1966084
  57.9 3.5 %copy-start.6 = (bf16[32,3,128]{2,0,1:T(8,128)(2,1)S(1)}, bf16[32,3,128]{2,0,1:T(8,128)(2,1)}, u32[]{:S(2)}) copy-start(bf16[32,3,128]{2,0,1:T(8,128)(2,1)} %param.41) | copy-start | bytes 73732
  57.9 3.6 %copy-start.9 = (f32[4,128]{1,0:T(4,128)S(1)}, f32[4,128]{1,0:T(4,128)}, u32[]{:S(2)}) copy-start(f32[4,128]{1,0:T(4,128)} %param.34) | copy-start | bytes 6148
  58.8 3.4 %copy-start.3 = (bf16[32,3,256]{2,0,1:T(8,128)(2,1)S(1)}, bf16[32,3,256]{2,0,1:T(8,128)(2,1)}, u32[]{:S(2)}) copy-start(bf16[32,3,256]{2,0,1:T(8,128)(2,1)} %param.42) | copy-start | bytes 147460
  67.3 4.7 %copy-start.1 = (f32[32,16,16]{2,1,0:T(8,128)}, f32[32,16,16]{2,1,0:T(8,128)S(1)}, u32[]{:S(2)}) copy-start(f32[32,16,16]{2,1,0:T(8,128)S(1)} %fusion.63) | copy-start | bytes 98308
  72.0 5.6 %copy-start.4 = (f32[32,16,2]{1,2,0:T(2,128)S(1)}, f32[32,16,2]{1,2,0:T(2,128)}, u32[]{:S(2)}) copy-start(f32[32,16,2]{1,2,0:T(2,128)} %copy.68) | copy-start | bytes 12292
  72.0 5.6 %copy-start.5 = (f32[32,16,2]{1,2,0:T(2,128)S(1)}, f32[32,16,2]{1,2,0:T(2,128)}, u32[]{:S(2)}) copy-start(f32[32,16,2]{1,2,0:T(2,128)} %copy.70) | copy-start | bytes 12292
  72.0 5.6 %copy-start.13 = (pred[32]{0:T(512)(128)(4,1)S(1)}, pred[32]{0:T(512)(128)(4,1)}, u32[]{:S(2)}) copy-start(pred[32]{0:T(512)(128)(4,1)} %get-tuple-element.57) | copy-start | bytes 100
  72.0 5.6 %copy-start.19 = (f32[2]{0:T(128)S(1)}, f32[2]{0:T(128)}, u32[]{:S(2)}) copy-start(f32[2]{0:T(128)} %param.38) | copy-start | bytes 28
  72.0 5.6 %copy-start.2 = (f32[32,16,16]{2,1,0:T(8,128)S(1)}, f32[32,16,16]{2,1,0:T(8,128)}, u32[]{:S(2)}) copy-start(f32[32,16,16]{2,1,0:T(8,128)} %copy-done.1) | copy-start | bytes 98308
  79.8 5.1 %copy-start.14 = (f32[128]{0:T(128)S(1)}, f32[128]{0:T(128)}, u32[]{:S(2)}) copy-start(f32[128]{0:T(128)} %param.39) | copy-start | bytes 1540
  122.4 41.5 %all-to-all-start.1 = ((bf16[48,2,64,128]{3,2,1,0:T(8,128)(2,1)}), bf16[48,2,64,128]{3,2,1,0:T(8,128)(2,1)S(1)}, u32[]{:S(2)}, u32[]{:S(2)}) async-start(bf16[48,2,64,128]{3,2,1,0:T(8,128)(2,1)} %add_convert_fusion), calls=%async_computation.1 | async-start | bytes 3145728 | tf_op jit(solution)/shard_map/all_to_all | solution.py:356

commit v10 on v9

--- a/solution.py
+++ b/solution.py
@@ -148,11 +148,10 @@
     pl.semaphore_wait(barrier, nz + 1)
     local = pltpu.make_async_copy(src_ref, dst_ref.at[y, z], local_sem)
     local.start()
-    sent = []
-    along_z = []
-    for offset in range(1, nz):
-        copy = remote(src_ref, dst_ref.at[y, z], z_sem + offset, y, lax.rem(z + offset, nz))
-        along_z.append(copy)
+    nearest = sorted(range(1, nz), key=lambda offset: (min(offset, nz - offset), offset))
+    along_z = {}
+    for offset in nearest:
+        along_z[offset] = remote(src_ref, dst_ref.at[y, z], z_sem + offset, y, lax.rem(z + offset, nz))
     to_right = [remote(src_ref, dst_ref.at[y, z], r_sem, right, z)]
     to_left = [remote(src_ref, dst_ref.at[y, z], l_sem, left, z)]
     relays = []
@@ -168,15 +167,18 @@
             remote(dst_ref.at[right, zs, second], dst_ref.at[right, zs, second], lb_sem + offset, left, z)
         )
 
-    for offset in range(1, nz):
-        along_z[offset - 1].wait_recv()
+    to_right, to_left = {0: to_right[0]}, {0: to_left[0]}
+    before = 0
+    for offset in nearest:
+        along_z[offset].wait_recv()
         zs = lax.rem(z + nz - offset, nz)
-        to_right.append(remote(dst_ref.at[y, zs], dst_ref.at[y, zs], r_sem + offset, right, z))
-        to_left.append(remote(dst_ref.at[y, zs], dst_ref.at[y, zs], l_sem + offset, left, z))
-        relay(offset - 1)
-    relay(nz - 1)
+        to_right[offset] = remote(dst_ref.at[y, zs], dst_ref.at[y, zs], r_sem + offset, right, z)
+        to_left[offset] = remote(dst_ref.at[y, zs], dst_ref.at[y, zs], l_sem + offset, left, z)
+        relay(before)
+        before = offset
+    relay(before)
     local.wait()
-    for copy in along_z + to_right + to_left:
+    for copy in list(along_z.values()) + list(to_right.values()) + list(to_left.values()):
         copy.wait_send()
     for copy in relays:
         copy.wait()

time: 167 us -> 162 us (0.970)
  Pallas kernels: 87.7 us -> 84.4 us
    pallas_call x1, Pallas kernels: 35.8 us -> 32.6 us  [gather2d(): pl.pallas_call(functools.partial(gather2d_kernel, nz), out_shape=jax.Shap...]
  transfers between devices with their start and end apart: 2 -> 2, of which waited for: 0 -> 0; matrix products, arithmetic and copies ran while one was open for 20% -> 20% of each run, Pallas kernels for 35% -> 34%
where the time goes in v10:
time: 162 us; the launch traced here: 161 us
  Pallas kernels  84.4 us (52%)
  matrix products  26.8 us (17%)
  other arithmetic  19.5 us (12%)
  starting transfers between devices  16.8 us (10%)
  local copies, waits for them, and re-layouts  12.7 us (8%)
    pallas_call x1, Pallas kernels, gather2d(): pl.pallas_call(functools.partial(gather2d_kernel, nz), out_shape=jax.Shap...  32.6 us
    pallas_call x1, Pallas kernels, exchange4(): pl.pallas_call(functools.partial(ring4_kernel, axis, gather), out_shape=(...  29.9 us
    pallas_call x1, Pallas kernels, exchange(): pl.pallas_call(functools.partial(exchange_kernel, n, axis, gather), out_s...  21.9 us
    dot_general x4, matrix products, shards(): jnp.dot(block_rows, weight_cols, preferred_element_type=jnp.float32)  10.7 us
    all_to_all x1, starting transfers between devices, shards(): lax.all_to_all(buffer.astype(jnp.bfloat16), 'rep', split_axis=0, concat_a...  9.28 us
    all_to_all x1, starting transfers between devices, shards(): lax.all_to_all(pool.astype(jnp.bfloat16), 'rep', split_axis=0, concat_axi...  7.55 us
    dot_general x2, matrix products, split_dot(): jnp.einsum(spec, low, narrow, preferred_element_type=jnp.float32)  5.37 us
    dot_general x2, matrix products, split_dot(): jnp.einsum(spec, high, narrow, preferred_element_type=jnp.float32)  4.69 us
  transfers between devices with their start and end apart: 2, of which 0 were waited for; matrix products, arithmetic and copies ran while one was open for 20% of the time, Pallas kernels for 34%

profile of v10, /device:TPU:1, one launch (start us, length us, event | category | flops | bytes accessed | tf_op | source)
XLA Modules:
  0.0 161.4 jit_solution(2788935574673541491)
XLA Ops:
  0.6 3.5 %convert_element_type.164 = bf16[48,2,64,128]{3,2,1,0:T(8,128)(2,1)} convert(f32[48,2,64,128]{3,2,1,0:T(8,128)} %param.43) | non-fusion elementwise | flops 786432 | bytes 4718592 | tf_op jit(solution)/shard_map/convert_element_type | solution.py:339
  4.2 7.6 %all-to-all-start = ((bf16[48,2,64,128]{3,2,1,0:T(8,128)(2,1)}), bf16[48,2,64,128]{3,2,1,0:T(8,128)(2,1)}, u32[]{:S(2)}, u32[]{:S(2)}) async-start(bf16[48,2,64,128]{3,2,1,0:T(8,128)(2,1)} %convert_element_type.164), calls=%async_computation | async-start | bytes 3145728 | tf_op jit(solution)/shard_map/all_to_all | solution.py:338
  12.0 0.5 and_bitcast_fusion
  12.5 0.6 compare_reduce_fusion
  13.2 0.7 compare_reduce_fusion.1
  13.9 32.6 %shard_map.194 = bf16[4,8,16,2560]{3,2,1,0:T(8,128)(2,1)} custom-call(bf16[16,2560]{1,0:T(8,128)(2,1)} %bitcast.76), custom_call_target="tpu_custom_call" | custom-call | tf_op jit(solution)/shard_map/pallas_call | solution.py:189
  46.5 2.5 %fusion.4 = f32[512,2]{0,1:T(2,128)S(1)} fusion(bf16[512,2560]{1,0:T(8,128)(2,1)} %bitcast.70, bf16[2560,2]{0,1:T(2,128)(2,1)S(1)} %copy-done.7), kind=kOutput, calls=%fused_computation.21 | convolution fusion | flops 5244928 | bytes 2635776 | tf_op jit(solution)/shard_map/dot_general | solution.py:276
  49.2 0.2 reduce-window.4
  49.5 0.2 fusion.47
  49.9 0.7 fusion.69
  50.7 0.9 copy.68
  52.0 2.6 %convolution_convert_fusion.1 = bf16[512,256]{1,0:T(8,128)(2,1)S(1)} fusion(bf16[512,2560]{1,0:T(8,128)(2,1)} %bitcast.71, bf16[2560,256]{1,0:T(8,128)(2,1)S(1)} %copy-done), kind=kOutput, calls=%fused_computation.16 | convolution fusion | flops 671219712 | bytes 4194304 | tf_op jit(solution)/shard_map/dot_general | solution.py:276
  54.9 0.7 copy.70
  55.6 2.6 %convolution_convert_fusion.3 = bf16[512,128]{1,0:T(8,128)(2,1)S(1)} fusion(bf16[512,2560]{1,0:T(8,128)(2,1)} %bitcast.72, bf16[2560,128]{1,0:T(8,128)(2,1)S(1)} %copy-done.15), kind=kOutput, calls=%fused_computation.19 | convolution fusion | flops 335609856 | bytes 3407872 | tf_op jit(solution)/shard_map/dot_general | solution.py:276
  58.7 0.3 copy.76
  59.2 0.3 multiply_convert_fusion
  59.6 0.6 pad_clamp_fusion
  60.3 0.6 gather_fusion
  61.0 0.2 convert_multiply_fusion
  61.2 0.6 gather_fusion.3
  61.8 0.6 gather_fusion.4
  62.4 0.6 gather_fusion.5
  63.0 0.6 gather_fusion.2
  63.9 0.2 fusion.63
  64.1 2.0 %fusion.30 = f32[32,2,64,16]{2,3,1,0:T(8,128)} fusion(f32[32,16,16]{2,1,0:T(8,128)S(1)} %fusion.63, f32[32,16,2]{1,2,0:T(2,128)} %copy.70, f32[32,16,2]{1,2,0:T(2,128)} %copy.68, pred[16,16]{1,0:T(8,128)(4,1)S(1)} %iota_compare_fusion.6, bf16[32,16,2,64]{3,2,1,0:T(2,128)(2,1)S(1)} %reshape.390), kind=kOutput, calls=%fused_computation.67 | convolution fusion | flops 2195456 | bytes 434432 | tf_op jit(solution)/shard_map/rtsh,rshp->rthp/dot_general | solution.py:234
  66.1 2.6 %fusion.10 = f32[48,2,64,128]{3,2,1,0:T(8,128)} fusion(f32[48,16,2,64]{3,1,2,0:T(8,128)S(1)} %gather_fusion.3, pred[48]{0:T(512)(128)(4,1)S(1)} %get-tuple-element.77, pred[48]{0:T(512)(128)(4,1)S(1)} %get-tuple-element.78, bf16[48,16,128]{2,1,0:T(8,128)(2,1)S(1)} %gather_fusion.5), kind=kOutput, calls=%fused_computation.38 | convolution fusion | flops 25559040 | bytes 3735648 | tf_op jit(solution)/shard_map/jshp,jsn->jhpn/dot_general | solution.py:234
  68.8 3.7 %convolution_multiply_fusion = f32[48,16,2,64]{3,1,2,0:T(8,128)} fusion(bf16[48,2,64,128]{3,2,1,0:T(8,128)(2,1)} %all-to-all-done, f32[48,16,2]{1,2,0:T(2,128)S(1)} %select_select_fusion.4, bf16[48,16,128]{2,1,0:T(8,128)(2,1)S(1)} %gather_fusion.4, pred[48]{0:T(512)(128)(4,1)S(1)} %get-tuple-element.77, pred[48]{0:T(512)(128)(4,1)S(1)} %get-tuple-element.78), kind=kOutput, calls=%fused_computation.11 | convolution fusion | flops 25460736 | bytes 2168928 | tf_op jit(solution)/shard_map/jhpn,jtn->jthp/dot_general | solution.py:351
  72.5 1.8 %gather_fusion.1 = f32[32,16,2,64]{3,1,2,0:T(8,128)S(1)} fusion(f32[48,16,2,64]{3,1,2,0:T(8,128)} %convolution_multiply_fusion, s32[1024]{0:T(1024)} %pad_clamp_fusion), kind=kCustom, calls=%fused_computation.3 | custom fusion | bytes 524416 | tf_op jit(solution)/shard_map/jit(_take)/gather | solution.py:354
  74.4 1.4 fusion.2
  75.8 0.3 copy.77
  76.1 0.3 reshape.393
  76.6 3.0 %multiply_reduce_fusion.1 = (f32[512]{0:T(512)S(1)}, f32[512,128]{0,1:T(8,128)S(1)}) fusion(f32[512,128]{0,1:T(8,128)S(1)} %copy.78, bf16[512,2560]{1,0:T(8,128)(2,1)} %bitcast.73, bf16[2560,128]{1,0:T(8,128)(2,1)} %param.30), kind=kOutput, calls=%fused_computation.57 | convolution fusion | flops 336133632 | bytes 3803136 | tf_op jit(solution)/shard_map/dot_general | solution.py:276
  79.7 1.3 fusion.40
  81.0 0.6 scatter.15
  81.6 2.0 %convolution_convert_fusion = bf16[512,2560]{1,0:T(8,128)(2,1)S(1)} fusion(bf16[128,2560]{1,0:T(8,128)(2,1)} %param.40, f32[512,128]{0,1:T(8,128)S(1)} %get-tuple-element.76, f32[128]{0:T(128)S(1)} %copy-done.14), kind=kOutput, calls=%fused_computation.7 | convolution fusion | flops 336986112 | bytes 3539456 | tf_op jit(solution)/shard_map/dot_general | solution.py:367
  83.7 1.8 %pad_maximum_fusion = bf16[512,2688]{1,0:T(8,128)(2,1)} fusion(bf16[512,128]{1,0:T(8,128)(2,1)S(1)} %scatter.15, bf16[512,2560]{1,0:T(8,128)(2,1)S(1)} %convolution_convert_fusion), kind=kLoop, calls=%fused_computation.9 | loop fusion | flops 5505024 | bytes 5505024 | tf_op jit(solution)/shard_map/concatenate | solution.py:372
  85.4 29.9 %shard_map.195 = (bf16[4,8,16,2688]{3,2,1,0:T(8,128)(2,1)}, bf16[2,4,16,2688]{3,2,1,0:T(8,128)(2,1)}) custom-call(bf16[4,8,16,2688]{3,2,1,0:T(8,128)(2,1)} %bitcast.69), custom_call_target="tpu_custom_call" | custom-call | tf_op jit(solution)/shard_map/pallas_call | solution.py:107
  115.3 3.9 %add_convert_fusion = bf16[48,2,64,128]{3,2,1,0:T(8,128)(2,1)} fusion(f32[48,2,64,128]{3,2,1,0:T(8,128)} %fusion.10, bf16[48,2,64,128]{3,2,1,0:T(8,128)(2,1)} %all-to-all-done, f32[48,2]{1,0:T(8,128)S(1)} %select_select_fusion.5, f32[48,16,2,64]{3,1,2,0:T(8,128)S(1)} %gather_fusion.3, pred[48]{0:T(512)(128)(4,1)S(1)} %get-tuple-element.77, ...), kind=kOutput, calls=%fused_computation.8 | convolution fusion | flops 29884416 | bytes 6881760 | tf_op jit(solution)/shard_map/jshp,jsn->jhpn/dot_general | solution.py:234
  119.2 9.3 %all-to-all-start.1 = ((bf16[48,2,64,128]{3,2,1,0:T(8,128)(2,1)}), bf16[48,2,64,128]{3,2,1,0:T(8,128)(2,1)S(1)}, u32[]{:S(2)}, u32[]{:S(2)}) async-start(bf16[48,2,64,128]{3,2,1,0:T(8,128)(2,1)} %add_convert_fusion), calls=%async_computation.1 | async-start | bytes 3145728 | tf_op jit(solution)/shard_map/all_to_all | solution.py:358
  128.5 2.4 %convert_reduce_fusion = f32[8,16,2688]{2,1,0:T(8,128)S(1)} fusion(bf16[4,8,16,2688]{3,2,1,0:T(8,128)(2,1)} %get-tuple-element.52), kind=kLoop, calls=%fused_computation.6 | loop fusion | flops 2408448 | bytes 4128768 | tf_op jit(solution)/shard_map/reduce_sum | solution.py:373
  130.9 0.9 convert_element_type.172
  131.9 1.4 scatter.16
  133.3 2.0 %scatter.19.src_ref = bf16[8,16,2688]{2,1,0:T(8,128)(2,1)} dynamic-update-slice(bf16[8,16,2688]{2,1,0:T(8,128)(2,1)} %scatter.16, bf16[8,16,1]{2,1,0:T(8,128)(2,1)S(1)} %get-tuple-element.55, s32[]{:T(128)} %constant.199.clone.1, s32[]{:T(128)} %constant.199.clone.1, s32[]{:T(128)} %constant.211.clone.1) | dynamic-update-slice | bytes 516 | tf_op jit(solution)/shard_map/scatter | solution.py:378
  135.3 21.9 %shard_map.196 = bf16[8,16,2688]{2,1,0:T(8,128)(2,1)} custom-call(bf16[8,16,2688]{2,1,0:T(8,128)(2,1)} %scatter.19.src_ref), custom_call_target="tpu_custom_call" | custom-call | tf_op jit(solution)/shard_map/pallas_call | solution.py:206
  157.2 1.2 convert_reduce_fusion.1
  158.4 0.2 fusion.51
  158.6 0.7 fusion.44
  159.4 2.1 %convert_element_type.184 = f32[48,2,64,128]{3,2,1,0:T(8,128)} convert(bf16[48,2,64,128]{3,2,1,0:T(8,128)(2,1)S(1)} %all-to-all-done.1) | non-fusion elementwise | flops 786432 | bytes 4718592 | tf_op jit(solution)/shard_map/convert_element_type | solution.py:360
  (87 shorter events, 3.0 us)
Async XLA Ops:
  0.6 51.4 %copy-start = (bf16[2560,256]{1,0:T(8,128)(2,1)S(1)}, bf16[2560,256]{1,0:T(8,128)(2,1)}, u32[]{:S(2)}) copy-start(bf16[2560,256]{1,0:T(8,128)(2,1)} %param.32) | copy-start | bytes 3932164
  4.2 7.6 %copy-start.11 = (s32[32,1]{0,1:T(1,128)S(1)}, s32[32,1]{0,1:T(1,128)}, u32[]{:S(2)}) copy-start(s32[32,1]{0,1:T(1,128)} %param.45) | copy-start | bytes 388
  4.2 42.3 %copy-start.17 = (f32[2]{0:T(128)S(1)}, f32[2]{0:T(128)}, u32[]{:S(2)}) copy-start(f32[2]{0:T(128)} %param.37) | copy-start | bytes 28
  4.2 42.3 %copy-start.7 = (bf16[2560,2]{0,1:T(2,128)(2,1)S(1)}, bf16[2560,2]{0,1:T(2,128)(2,1)}, u32[]{:S(2)}) copy-start(bf16[2560,2]{0,1:T(2,128)(2,1)} %param.33) | copy-start | bytes 30724
  4.2 64.6 %all-to-all-start = ((bf16[48,2,64,128]{3,2,1,0:T(8,128)(2,1)}), bf16[48,2,64,128]{3,2,1,0:T(8,128)(2,1)}, u32[]{:S(2)}, u32[]{:S(2)}) async-start(bf16[48,2,64,128]{3,2,1,0:T(8,128)(2,1)} %convert_element_type.164), calls=%async_computation | async-start | bytes 3145728 | tf_op jit(solution)/shard_map/all_to_all | solution.py:338
  13.9 35.3 %copy-start.18 = (s32[4]{0:T(128)S(1)}, s32[4]{0:T(128)}, u32[]{:S(2)}) copy-start(s32[4]{0:T(128)} %param.44) | copy-start | bytes 52
  13.9 35.6 %copy-start.16 = (f32[4,2]{0,1:T(2,128)S(1)}, f32[4,2]{0,1:T(2,128)}, u32[]{:S(2)}) copy-start(f32[4,2]{0,1:T(2,128)} %param.36) | copy-start | bytes 100
  46.5 5.2 %copy-start.10 = (s32[32]{0:T(128)S(1)}, s32[32]{0:T(128)}, u32[]{:S(2)}) copy-start(s32[32]{0:T(128)} %param.46) | copy-start | bytes 388
  51.7 2.9 %copy-start.12 = (s32[32]{0:T(128)S(1)}, s32[32]{0:T(128)}, u32[]{:S(2)}) copy-start(s32[32]{0:T(128)} %param.47) | copy-start | bytes 388
  51.8 3.1 %copy-start.8 = (f32[4,256]{1,0:T(4,128)S(1)}, f32[4,256]{1,0:T(4,128)}, u32[]{:S(2)}) copy-start(f32[4,256]{1,0:T(4,128)} %param.35) | copy-start | bytes 12292
  51.9 3.7 %copy-start.15 = (bf16[2560,128]{1,0:T(8,128)(2,1)S(1)}, bf16[2560,128]{1,0:T(8,128)(2,1)}, u32[]{:S(2)}) copy-start(bf16[2560,128]{1,0:T(8,128)(2,1)} %param.31) | copy-start | bytes 1966084
  54.7 3.5 %copy-start.6 = (bf16[32,3,128]{2,0,1:T(8,128)(2,1)S(1)}, bf16[32,3,128]{2,0,1:T(8,128)(2,1)}, u32[]{:S(2)}) copy-start(bf16[32,3,128]{2,0,1:T(8,128)(2,1)} %param.41) | copy-start | bytes 73732
  54.7 3.6 %copy-start.9 = (f32[4,128]{1,0:T(4,128)S(1)}, f32[4,128]{1,0:T(4,128)}, u32[]{:S(2)}) copy-start(f32[4,128]{1,0:T(4,128)} %param.34) | copy-start | bytes 6148
  55.6 3.4 %copy-start.3 = (bf16[32,3,256]{2,0,1:T(8,128)(2,1)S(1)}, bf16[32,3,256]{2,0,1:T(8,128)(2,1)}, u32[]{:S(2)}) copy-start(bf16[32,3,256]{2,0,1:T(8,128)(2,1)} %param.42) | copy-start | bytes 147460
  64.1 4.7 %copy-start.1 = (f32[32,16,16]{2,1,0:T(8,128)}, f32[32,16,16]{2,1,0:T(8,128)S(1)}, u32[]{:S(2)}) copy-start(f32[32,16,16]{2,1,0:T(8,128)S(1)} %fusion.63) | copy-start | bytes 98308
  68.8 5.6 %copy-start.4 = (f32[32,16,2]{1,2,0:T(2,128)S(1)}, f32[32,16,2]{1,2,0:T(2,128)}, u32[]{:S(2)}) copy-start(f32[32,16,2]{1,2,0:T(2,128)} %copy.68) | copy-start | bytes 12292
  68.8 5.6 %copy-start.5 = (f32[32,16,2]{1,2,0:T(2,128)S(1)}, f32[32,16,2]{1,2,0:T(2,128)}, u32[]{:S(2)}) copy-start(f32[32,16,2]{1,2,0:T(2,128)} %copy.70) | copy-start | bytes 12292
  68.8 5.6 %copy-start.13 = (pred[32]{0:T(512)(128)(4,1)S(1)}, pred[32]{0:T(512)(128)(4,1)}, u32[]{:S(2)}) copy-start(pred[32]{0:T(512)(128)(4,1)} %get-tuple-element.57) | copy-start | bytes 100
  68.8 5.6 %copy-start.19 = (f32[2]{0:T(128)S(1)}, f32[2]{0:T(128)}, u32[]{:S(2)}) copy-start(f32[2]{0:T(128)} %param.38) | copy-start | bytes 28
  68.8 5.6 %copy-start.2 = (f32[32,16,16]{2,1,0:T(8,128)S(1)}, f32[32,16,16]{2,1,0:T(8,128)}, u32[]{:S(2)}) copy-start(f32[32,16,16]{2,1,0:T(8,128)} %copy-done.1) | copy-start | bytes 98308
  76.6 5.1 %copy-start.14 = (f32[128]{0:T(128)S(1)}, f32[128]{0:T(128)}, u32[]{:S(2)}) copy-start(f32[128]{0:T(128)} %param.39) | copy-start | bytes 1540
  119.2 40.1 %all-to-all-start.1 = ((bf16[48,2,64,128]{3,2,1,0:T(8,128)(2,1)}), bf16[48,2,64,128]{3,2,1,0:T(8,128)(2,1)S(1)}, u32[]{:S(2)}, u32[]{:S(2)}) async-start(bf16[48,2,64,128]{3,2,1,0:T(8,128)(2,1)} %add_convert_fusion), calls=%async_computation.1 | async-start | bytes 3145728 | tf_op jit(solution)/shard_map/all_to_all | solution.py:358

commit v11 on v10

--- a/solution.py
+++ b/solution.py
@@ -28,7 +28,7 @@
     local = pltpu.make_async_copy(src_ref if gather else src_ref.at[me], dst_ref.at[me], local_sem)
     local.start()
     copies = []
-    for offset in range(1, n):
+    for offset in sorted(range(1, n), key=lambda offset: (min(offset, n - offset), offset)):
         peer = lax.rem(me + offset, n)
         copy = pltpu.make_async_remote_copy(
             src_ref=src_ref if gather else src_ref.at[peer],
@@ -73,6 +73,9 @@
     for peer in (left, right):
         pl.semaphore_signal(barrier, inc=1, device_id=device_of(peer), device_id_type=MESH)
     pl.semaphore_wait(barrier, 2)
+    if not gather:
+        stage_right = remote(src_ref.at[opposite, first], stage_ref.at[0], 2, right)
+        stage_left = remote(src_ref.at[opposite, second], stage_ref.at[1], 3, left)
     local = pltpu.make_async_copy(src_ref if gather else src_ref.at[me], dst_ref.at[me], local_sem)
     local.start()
     to_right = remote(src_ref if gather else src_ref.at[right], dst_ref.at[me], 0, right)
@@ -85,8 +88,6 @@
         to_right.wait_send()
         to_left.wait_send()
     else:
-        stage_right = remote(src_ref.at[opposite, first], stage_ref.at[0], 2, right)
-        stage_left = remote(src_ref.at[opposite, second], stage_ref.at[1], 3, left)
         stage_right.wait_recv()
         pass_right = remote(stage_ref.at[0], dst_ref.at[left, first], 4, right)
         stage_left.wait_recv()

time: 162 us -> 160 us (0.988)
  transfers between devices with their start and end apart: 2 -> 2, of which waited for: 0 -> 0; matrix products, arithmetic and copies ran while one was open for 20% -> 21% of each run, Pallas kernels for 34% -> 34%
where the time goes in v11:
time: 160 us; the launch traced here: 159 us
  Pallas kernels  83.3 us (52%)
  matrix products  26.8 us (17%)
  other arithmetic  19.5 us (12%)
  starting transfers between devices  15.8 us (10%)
  local copies, waits for them, and re-layouts  12.7 us (8%)
    pallas_call x1, Pallas kernels, gather2d(): pl.pallas_call(functools.partial(gather2d_kernel, nz), out_shape=jax.Shap...  32.6 us
    pallas_call x1, Pallas kernels, exchange4(): pl.pallas_call(functools.partial(ring4_kernel, axis, gather), out_shape=(...  29.5 us
    pallas_call x1, Pallas kernels, exchange(): pl.pallas_call(functools.partial(exchange_kernel, n, axis, gather), out_s...  21.2 us
    dot_general x4, matrix products, shards(): jnp.dot(block_rows, weight_cols, preferred_element_type=jnp.float32)  10.7 us
    all_to_all x1, starting transfers between devices, shards(): lax.all_to_all(buffer.astype(jnp.bfloat16), 'rep', split_axis=0, concat_a...  8.22 us
    all_to_all x1, starting transfers between devices, shards(): lax.all_to_all(pool.astype(jnp.bfloat16), 'rep', split_axis=0, concat_axi...  7.55 us
    dot_general x2, matrix products, split_dot(): jnp.einsum(spec, low, narrow, preferred_element_type=jnp.float32)  5.37 us
    dot_general x2, matrix products, split_dot(): jnp.einsum(spec, high, narrow, preferred_element_type=jnp.float32)  4.69 us
  transfers between devices with their start and end apart: 2, of which 0 were waited for; matrix products, arithmetic and copies ran while one was open for 21% of the time, Pallas kernels for 34%

profile of v11, /device:TPU:1, one launch (start us, length us, event | category | flops | bytes accessed | tf_op | source)
XLA Modules:
  0.0 159.2 jit_solution(5177934683844925756)
XLA Ops:
  0.6 3.5 %convert_element_type.164 = bf16[48,2,64,128]{3,2,1,0:T(8,128)(2,1)} convert(f32[48,2,64,128]{3,2,1,0:T(8,128)} %param.43) | non-fusion elementwise | flops 786432 | bytes 4718592 | tf_op jit(solution)/shard_map/convert_element_type | solution.py:340
  4.2 7.6 %all-to-all-start = ((bf16[48,2,64,128]{3,2,1,0:T(8,128)(2,1)}), bf16[48,2,64,128]{3,2,1,0:T(8,128)(2,1)}, u32[]{:S(2)}, u32[]{:S(2)}) async-start(bf16[48,2,64,128]{3,2,1,0:T(8,128)(2,1)} %convert_element_type.164), calls=%async_computation | async-start | bytes 3145728 | tf_op jit(solution)/shard_map/all_to_all | solution.py:339
  12.0 0.5 and_bitcast_fusion
  12.5 0.6 compare_reduce_fusion
  13.2 0.7 compare_reduce_fusion.1
  13.9 32.6 %shard_map.194 = bf16[4,8,16,2560]{3,2,1,0:T(8,128)(2,1)} custom-call(bf16[16,2560]{1,0:T(8,128)(2,1)} %bitcast.76), custom_call_target="tpu_custom_call" | custom-call | tf_op jit(solution)/shard_map/pallas_call | solution.py:190
  46.5 2.5 %fusion.4 = f32[512,2]{0,1:T(2,128)S(1)} fusion(bf16[512,2560]{1,0:T(8,128)(2,1)} %bitcast.70, bf16[2560,2]{0,1:T(2,128)(2,1)S(1)} %copy-done.7), kind=kOutput, calls=%fused_computation.21 | convolution fusion | flops 5244928 | bytes 2635776 | tf_op jit(solution)/shard_map/dot_general | solution.py:277
  49.2 0.2 reduce-window.4
  49.5 0.2 fusion.47
  49.9 0.7 fusion.69
  50.7 0.9 copy.68
  52.0 2.6 %convolution_convert_fusion.1 = bf16[512,256]{1,0:T(8,128)(2,1)S(1)} fusion(bf16[512,2560]{1,0:T(8,128)(2,1)} %bitcast.71, bf16[2560,256]{1,0:T(8,128)(2,1)S(1)} %copy-done), kind=kOutput, calls=%fused_computation.16 | convolution fusion | flops 671219712 | bytes 4194304 | tf_op jit(solution)/shard_map/dot_general | solution.py:277
  54.9 0.7 copy.70
  55.6 2.6 %convolution_convert_fusion.3 = bf16[512,128]{1,0:T(8,128)(2,1)S(1)} fusion(bf16[512,2560]{1,0:T(8,128)(2,1)} %bitcast.72, bf16[2560,128]{1,0:T(8,128)(2,1)S(1)} %copy-done.15), kind=kOutput, calls=%fused_computation.19 | convolution fusion | flops 335609856 | bytes 3407872 | tf_op jit(solution)/shard_map/dot_general | solution.py:277
  58.7 0.3 copy.76
  59.2 0.3 multiply_convert_fusion
  59.6 0.6 pad_clamp_fusion
  60.3 0.6 gather_fusion
  61.0 0.2 convert_multiply_fusion
  61.2 0.6 gather_fusion.3
  61.8 0.6 gather_fusion.4
  62.4 0.6 gather_fusion.5
  63.0 0.6 gather_fusion.2
  63.9 0.2 fusion.63
  64.1 2.0 %fusion.30 = f32[32,2,64,16]{2,3,1,0:T(8,128)} fusion(f32[32,16,16]{2,1,0:T(8,128)S(1)} %fusion.63, f32[32,16,2]{1,2,0:T(2,128)} %copy.70, f32[32,16,2]{1,2,0:T(2,128)} %copy.68, pred[16,16]{1,0:T(8,128)(4,1)S(1)} %iota_compare_fusion.6, bf16[32,16,2,64]{3,2,1,0:T(2,128)(2,1)S(1)} %reshape.390), kind=kOutput, calls=%fused_computation.67 | convolution fusion | flops 2195456 | bytes 434432 | tf_op jit(solution)/shard_map/rtsh,rshp->rthp/dot_general | solution.py:235
  66.1 2.6 %fusion.10 = f32[48,2,64,128]{3,2,1,0:T(8,128)} fusion(f32[48,16,2,64]{3,1,2,0:T(8,128)S(1)} %gather_fusion.3, pred[48]{0:T(512)(128)(4,1)S(1)} %get-tuple-element.77, pred[48]{0:T(512)(128)(4,1)S(1)} %get-tuple-element.78, bf16[48,16,128]{2,1,0:T(8,128)(2,1)S(1)} %gather_fusion.5), kind=kOutput, calls=%fused_computation.38 | convolution fusion | flops 25559040 | bytes 3735648 | tf_op jit(solution)/shard_map/jshp,jsn->jhpn/dot_general | solution.py:235
  68.8 3.7 %convolution_multiply_fusion = f32[48,16,2,64]{3,1,2,0:T(8,128)} fusion(bf16[48,2,64,128]{3,2,1,0:T(8,128)(2,1)} %all-to-all-done, f32[48,16,2]{1,2,0:T(2,128)S(1)} %select_select_fusion.4, bf16[48,16,128]{2,1,0:T(8,128)(2,1)S(1)} %gather_fusion.4, pred[48]{0:T(512)(128)(4,1)S(1)} %get-tuple-element.77, pred[48]{0:T(512)(128)(4,1)S(1)} %get-tuple-element.78), kind=kOutput, calls=%fused_computation.11 | convolution fusion | flops 25460736 | bytes 2168928 | tf_op jit(solution)/shard_map/jhpn,jtn->jthp/dot_general | solution.py:352
  72.5 1.8 %gather_fusion.1 = f32[32,16,2,64]{3,1,2,0:T(8,128)S(1)} fusion(f32[48,16,2,64]{3,1,2,0:T(8,128)} %convolution_multiply_fusion, s32[1024]{0:T(1024)} %pad_clamp_fusion), kind=kCustom, calls=%fused_computation.3 | custom fusion | bytes 524416 | tf_op jit(solution)/shard_map/jit(_take)/gather | solution.py:355
  74.4 1.4 fusion.2
  75.8 0.3 copy.77
  76.1 0.3 reshape.393
  76.6 3.0 %multiply_reduce_fusion.1 = (f32[512]{0:T(512)S(1)}, f32[512,128]{0,1:T(8,128)S(1)}) fusion(f32[512,128]{0,1:T(8,128)S(1)} %copy.78, bf16[512,2560]{1,0:T(8,128)(2,1)} %bitcast.73, bf16[2560,128]{1,0:T(8,128)(2,1)} %param.30), kind=kOutput, calls=%fused_computation.57 | convolution fusion | flops 336133632 | bytes 3803136 | tf_op jit(solution)/shard_map/dot_general | solution.py:277
  79.7 1.3 fusion.40
  81.0 0.6 scatter.15
  81.6 2.0 %convolution_convert_fusion = bf16[512,2560]{1,0:T(8,128)(2,1)S(1)} fusion(bf16[128,2560]{1,0:T(8,128)(2,1)} %param.40, f32[512,128]{0,1:T(8,128)S(1)} %get-tuple-element.76, f32[128]{0:T(128)S(1)} %copy-done.14), kind=kOutput, calls=%fused_computation.7 | convolution fusion | flops 336986112 | bytes 3539456 | tf_op jit(solution)/shard_map/dot_general | solution.py:368
  83.7 1.8 %pad_maximum_fusion = bf16[512,2688]{1,0:T(8,128)(2,1)} fusion(bf16[512,128]{1,0:T(8,128)(2,1)S(1)} %scatter.15, bf16[512,2560]{1,0:T(8,128)(2,1)S(1)} %convolution_convert_fusion), kind=kLoop, calls=%fused_computation.9 | loop fusion | flops 5505024 | bytes 5505024 | tf_op jit(solution)/shard_map/concatenate | solution.py:373
  85.4 29.5 %shard_map.195 = (bf16[4,8,16,2688]{3,2,1,0:T(8,128)(2,1)}, bf16[2,4,16,2688]{3,2,1,0:T(8,128)(2,1)}) custom-call(bf16[4,8,16,2688]{3,2,1,0:T(8,128)(2,1)} %bitcast.69), custom_call_target="tpu_custom_call" | custom-call | tf_op jit(solution)/shard_map/pallas_call | solution.py:108
  114.9 3.9 %add_convert_fusion = bf16[48,2,64,128]{3,2,1,0:T(8,128)(2,1)} fusion(f32[48,2,64,128]{3,2,1,0:T(8,128)} %fusion.10, bf16[48,2,64,128]{3,2,1,0:T(8,128)(2,1)} %all-to-all-done, f32[48,2]{1,0:T(8,128)S(1)} %select_select_fusion.5, f32[48,16,2,64]{3,1,2,0:T(8,128)S(1)} %gather_fusion.3, pred[48]{0:T(512)(128)(4,1)S(1)} %get-tuple-element.77, ...), kind=kOutput, calls=%fused_computation.8 | convolution fusion | flops 29884416 | bytes 6881760 | tf_op jit(solution)/shard_map/jshp,jsn->jhpn/dot_general | solution.py:235
  118.9 8.2 %all-to-all-start.1 = ((bf16[48,2,64,128]{3,2,1,0:T(8,128)(2,1)}), bf16[48,2,64,128]{3,2,1,0:T(8,128)(2,1)S(1)}, u32[]{:S(2)}, u32[]{:S(2)}) async-start(bf16[48,2,64,128]{3,2,1,0:T(8,128)(2,1)} %add_convert_fusion), calls=%async_computation.1 | async-start | bytes 3145728 | tf_op jit(solution)/shard_map/all_to_all | solution.py:359
  127.1 2.4 %convert_reduce_fusion = f32[8,16,2688]{2,1,0:T(8,128)S(1)} fusion(bf16[4,8,16,2688]{3,2,1,0:T(8,128)(2,1)} %get-tuple-element.52), kind=kLoop, calls=%fused_computation.6 | loop fusion | flops 2408448 | bytes 4128768 | tf_op jit(solution)/shard_map/reduce_sum | solution.py:374
  129.4 0.9 convert_element_type.172
  130.5 1.4 scatter.16
  131.9 2.0 %scatter.19.src_ref = bf16[8,16,2688]{2,1,0:T(8,128)(2,1)} dynamic-update-slice(bf16[8,16,2688]{2,1,0:T(8,128)(2,1)} %scatter.16, bf16[8,16,1]{2,1,0:T(8,128)(2,1)S(1)} %get-tuple-element.55, s32[]{:T(128)} %constant.199.clone.1, s32[]{:T(128)} %constant.199.clone.1, s32[]{:T(128)} %constant.211.clone.1) | dynamic-update-slice | bytes 516 | tf_op jit(solution)/shard_map/scatter | solution.py:379
  133.9 21.2 %shard_map.196 = bf16[8,16,2688]{2,1,0:T(8,128)(2,1)} custom-call(bf16[8,16,2688]{2,1,0:T(8,128)(2,1)} %scatter.19.src_ref), custom_call_target="tpu_custom_call" | custom-call | tf_op jit(solution)/shard_map/pallas_call | solution.py:207
  155.1 1.2 convert_reduce_fusion.1
  156.3 0.2 fusion.51
  156.5 0.7 fusion.44
  157.2 2.1 %convert_element_type.184 = f32[48,2,64,128]{3,2,1,0:T(8,128)} convert(bf16[48,2,64,128]{3,2,1,0:T(8,128)(2,1)S(1)} %all-to-all-done.1) | non-fusion elementwise | flops 786432 | bytes 4718592 | tf_op jit(solution)/shard_map/convert_element_type | solution.py:361
  (87 shorter events, 3.0 us)
Async XLA Ops:
  0.6 51.4 %copy-start = (bf16[2560,256]{1,0:T(8,128)(2,1)S(1)}, bf16[2560,256]{1,0:T(8,128)(2,1)}, u32[]{:S(2)}) copy-start(bf16[2560,256]{1,0:T(8,128)(2,1)} %param.32) | copy-start | bytes 3932164
  4.2 7.6 %copy-start.11 = (s32[32,1]{0,1:T(1,128)S(1)}, s32[32,1]{0,1:T(1,128)}, u32[]{:S(2)}) copy-start(s32[32,1]{0,1:T(1,128)} %param.45) | copy-start | bytes 388
  4.2 42.3 %copy-start.17 = (f32[2]{0:T(128)S(1)}, f32[2]{0:T(128)}, u32[]{:S(2)}) copy-start(f32[2]{0:T(128)} %param.37) | copy-start | bytes 28
  4.2 42.3 %copy-start.7 = (bf16[2560,2]{0,1:T(2,128)(2,1)S(1)}, bf16[2560,2]{0,1:T(2,128)(2,1)}, u32[]{:S(2)}) copy-start(bf16[2560,2]{0,1:T(2,128)(2,1)} %param.33) | copy-start | bytes 30724
  4.2 64.6 %all-to-all-start = ((bf16[48,2,64,128]{3,2,1,0:T(8,128)(2,1)}), bf16[48,2,64,128]{3,2,1,0:T(8,128)(2,1)}, u32[]{:S(2)}, u32[]{:S(2)}) async-start(bf16[48,2,64,128]{3,2,1,0:T(8,128)(2,1)} %convert_element_type.164), calls=%async_computation | async-start | bytes 3145728 | tf_op jit(solution)/shard_map/all_to_all | solution.py:339
  13.9 35.3 %copy-start.18 = (s32[4]{0:T(128)S(1)}, s32[4]{0:T(128)}, u32[]{:S(2)}) copy-start(s32[4]{0:T(128)} %param.44) | copy-start | bytes 52
  13.9 35.6 %copy-start.16 = (f32[4,2]{0,1:T(2,128)S(1)}, f32[4,2]{0,1:T(2,128)}, u32[]{:S(2)}) copy-start(f32[4,2]{0,1:T(2,128)} %param.36) | copy-start | bytes 100
  46.5 5.2 %copy-start.10 = (s32[32]{0:T(128)S(1)}, s32[32]{0:T(128)}, u32[]{:S(2)}) copy-start(s32[32]{0:T(128)} %param.46) | copy-start | bytes 388
  51.7 2.9 %copy-start.12 = (s32[32]{0:T(128)S(1)}, s32[32]{0:T(128)}, u32[]{:S(2)}) copy-start(s32[32]{0:T(128)} %param.47) | copy-start | bytes 388
  51.8 3.1 %copy-start.8 = (f32[4,256]{1,0:T(4,128)S(1)}, f32[4,256]{1,0:T(4,128)}, u32[]{:S(2)}) copy-start(f32[4,256]{1,0:T(4,128)} %param.35) | copy-start | bytes 12292
  51.9 3.7 %copy-start.15 = (bf16[2560,128]{1,0:T(8,128)(2,1)S(1)}, bf16[2560,128]{1,0:T(8,128)(2,1)}, u32[]{:S(2)}) copy-start(bf16[2560,128]{1,0:T(8,128)(2,1)} %param.31) | copy-start | bytes 1966084
  54.7 3.5 %copy-start.6 = (bf16[32,3,128]{2,0,1:T(8,128)(2,1)S(1)}, bf16[32,3,128]{2,0,1:T(8,128)(2,1)}, u32[]{:S(2)}) copy-start(bf16[32,3,128]{2,0,1:T(8,128)(2,1)} %param.41) | copy-start | bytes 73732
  54.7 3.6 %copy-start.9 = (f32[4,128]{1,0:T(4,128)S(1)}, f32[4,128]{1,0:T(4,128)}, u32[]{:S(2)}) copy-start(f32[4,128]{1,0:T(4,128)} %param.34) | copy-start | bytes 6148
  55.6 3.4 %copy-start.3 = (bf16[32,3,256]{2,0,1:T(8,128)(2,1)S(1)}, bf16[32,3,256]{2,0,1:T(8,128)(2,1)}, u32[]{:S(2)}) copy-start(bf16[32,3,256]{2,0,1:T(8,128)(2,1)} %param.42) | copy-start | bytes 147460
  64.1 4.7 %copy-start.1 = (f32[32,16,16]{2,1,0:T(8,128)}, f32[32,16,16]{2,1,0:T(8,128)S(1)}, u32[]{:S(2)}) copy-start(f32[32,16,16]{2,1,0:T(8,128)S(1)} %fusion.63) | copy-start | bytes 98308
  68.8 5.6 %copy-start.4 = (f32[32,16,2]{1,2,0:T(2,128)S(1)}, f32[32,16,2]{1,2,0:T(2,128)}, u32[]{:S(2)}) copy-start(f32[32,16,2]{1,2,0:T(2,128)} %copy.68) | copy-start | bytes 12292
  68.8 5.6 %copy-start.5 = (f32[32,16,2]{1,2,0:T(2,128)S(1)}, f32[32,16,2]{1,2,0:T(2,128)}, u32[]{:S(2)}) copy-start(f32[32,16,2]{1,2,0:T(2,128)} %copy.70) | copy-start | bytes 12292
  68.8 5.6 %copy-start.13 = (pred[32]{0:T(512)(128)(4,1)S(1)}, pred[32]{0:T(512)(128)(4,1)}, u32[]{:S(2)}) copy-start(pred[32]{0:T(512)(128)(4,1)} %get-tuple-element.57) | copy-start | bytes 100
  68.8 5.6 %copy-start.19 = (f32[2]{0:T(128)S(1)}, f32[2]{0:T(128)}, u32[]{:S(2)}) copy-start(f32[2]{0:T(128)} %param.38) | copy-start | bytes 28
  68.8 5.6 %copy-start.2 = (f32[32,16,16]{2,1,0:T(8,128)S(1)}, f32[32,16,16]{2,1,0:T(8,128)}, u32[]{:S(2)}) copy-start(f32[32,16,16]{2,1,0:T(8,128)} %copy-done.1) | copy-start | bytes 98308
  76.6 5.1 %copy-start.14 = (f32[128]{0:T(128)S(1)}, f32[128]{0:T(128)}, u32[]{:S(2)}) copy-start(f32[128]{0:T(128)} %param.39) | copy-start | bytes 1540
  118.9 38.3 %all-to-all-start.1 = ((bf16[48,2,64,128]{3,2,1,0:T(8,128)(2,1)}), bf16[48,2,64,128]{3,2,1,0:T(8,128)(2,1)S(1)}, u32[]{:S(2)}, u32[]{:S(2)}) async-start(bf16[48,2,64,128]{3,2,1,0:T(8,128)(2,1)} %add_convert_fusion), calls=%async_computation.1 | async-start | bytes 3145728 | tf_op jit(solution)/shard_map/all_to_all | solution.py:359

commit v12 on v11

--- a/solution.py
+++ b/solution.py
@@ -149,12 +149,12 @@
     pl.semaphore_wait(barrier, nz + 1)
     local = pltpu.make_async_copy(src_ref, dst_ref.at[y, z], local_sem)
     local.start()
+    to_right = [remote(src_ref, dst_ref.at[y, z], r_sem, right, z)]
+    to_left = [remote(src_ref, dst_ref.at[y, z], l_sem, left, z)]
     nearest = sorted(range(1, nz), key=lambda offset: (min(offset, nz - offset), offset))
     along_z = {}
     for offset in nearest:
         along_z[offset] = remote(src_ref, dst_ref.at[y, z], z_sem + offset, y, lax.rem(z + offset, nz))
-    to_right = [remote(src_ref, dst_ref.at[y, z], r_sem, right, z)]
-    to_left = [remote(src_ref, dst_ref.at[y, z], l_sem, left, z)]
     relays = []
 
     def relay(offset):

time: 160 us -> 160 us (level)
  no operation moved by 1% of the time
where the time goes in v12:
time: 160 us; the launch traced here: 159 us
  Pallas kernels  83.1 us (52%)
  matrix products  26.9 us (17%)
  other arithmetic  19.5 us (12%)
  starting transfers between devices  16 us (10%)
  local copies, waits for them, and re-layouts  12.7 us (8%)
    pallas_call x1, Pallas kernels, gather2d(): pl.pallas_call(functools.partial(gather2d_kernel, nz), out_shape=jax.Shap...  32.2 us
    pallas_call x1, Pallas kernels, exchange4(): pl.pallas_call(functools.partial(ring4_kernel, axis, gather), out_shape=(...  29.6 us
    pallas_call x1, Pallas kernels, exchange(): pl.pallas_call(functools.partial(exchange_kernel, n, axis, gather), out_s...  21.3 us
    dot_general x4, matrix products, shards(): jnp.dot(block_rows, weight_cols, preferred_element_type=jnp.float32)  10.7 us
    all_to_all x1, starting transfers between devices, shards(): lax.all_to_all(buffer.astype(jnp.bfloat16), 'rep', split_axis=0, concat_a...  8.48 us
    all_to_all x1, starting transfers between devices, shards(): lax.all_to_all(pool.astype(jnp.bfloat16), 'rep', split_axis=0, concat_axi...  7.55 us
    dot_general x2, matrix products, split_dot(): jnp.einsum(spec, low, narrow, preferred_element_type=jnp.float32)  5.37 us
    dot_general x2, matrix products, split_dot(): jnp.einsum(spec, high, narrow, preferred_element_type=jnp.float32)  4.69 us
  transfers between devices with their start and end apart: 2, of which 0 were waited for; matrix products, arithmetic and copies ran while one was open for 21% of the time, Pallas kernels for 34%

profile of v12, /device:TPU:1, one launch (start us, length us, event | category | flops | bytes accessed | tf_op | source)
XLA Modules:
  0.0 159.4 jit_solution(15880563692255899671)
XLA Ops:
  0.6 3.5 %convert_element_type.164 = bf16[48,2,64,128]{3,2,1,0:T(8,128)(2,1)} convert(f32[48,2,64,128]{3,2,1,0:T(8,128)} %param.43) | non-fusion elementwise | flops 786432 | bytes 4718592 | tf_op jit(solution)/shard_map/convert_element_type | solution.py:340
  4.2 7.6 %all-to-all-start = ((bf16[48,2,64,128]{3,2,1,0:T(8,128)(2,1)}), bf16[48,2,64,128]{3,2,1,0:T(8,128)(2,1)}, u32[]{:S(2)}, u32[]{:S(2)}) async-start(bf16[48,2,64,128]{3,2,1,0:T(8,128)(2,1)} %convert_element_type.164), calls=%async_computation | async-start | bytes 3145728 | tf_op jit(solution)/shard_map/all_to_all | solution.py:339
  12.0 0.5 and_bitcast_fusion
  12.5 0.6 compare_reduce_fusion
  13.2 0.7 compare_reduce_fusion.1
  13.9 32.2 %shard_map.194 = bf16[4,8,16,2560]{3,2,1,0:T(8,128)(2,1)} custom-call(bf16[16,2560]{1,0:T(8,128)(2,1)} %bitcast.76), custom_call_target="tpu_custom_call" | custom-call | tf_op jit(solution)/shard_map/pallas_call | solution.py:190
  46.1 2.5 %fusion.4 = f32[512,2]{0,1:T(2,128)S(1)} fusion(bf16[512,2560]{1,0:T(8,128)(2,1)} %bitcast.70, bf16[2560,2]{0,1:T(2,128)(2,1)S(1)} %copy-done.7), kind=kOutput, calls=%fused_computation.21 | convolution fusion | flops 5244928 | bytes 2635776 | tf_op jit(solution)/shard_map/dot_general | solution.py:277
  48.8 0.2 reduce-window.4
  49.1 0.2 fusion.47
  49.6 0.7 fusion.69
  50.3 0.9 copy.68
  51.7 2.6 %convolution_convert_fusion.1 = bf16[512,256]{1,0:T(8,128)(2,1)S(1)} fusion(bf16[512,2560]{1,0:T(8,128)(2,1)} %bitcast.71, bf16[2560,256]{1,0:T(8,128)(2,1)S(1)} %copy-done), kind=kOutput, calls=%fused_computation.16 | convolution fusion | flops 671219712 | bytes 4194304 | tf_op jit(solution)/shard_map/dot_general | solution.py:277
  54.5 0.7 copy.70
  55.2 2.6 %convolution_convert_fusion.3 = bf16[512,128]{1,0:T(8,128)(2,1)S(1)} fusion(bf16[512,2560]{1,0:T(8,128)(2,1)} %bitcast.72, bf16[2560,128]{1,0:T(8,128)(2,1)S(1)} %copy-done.15), kind=kOutput, calls=%fused_computation.19 | convolution fusion | flops 335609856 | bytes 3407872 | tf_op jit(solution)/shard_map/dot_general | solution.py:277
  58.3 0.3 copy.76
  58.9 0.3 multiply_convert_fusion
  59.3 0.6 pad_clamp_fusion
  60.0 0.6 gather_fusion
  60.6 0.2 convert_multiply_fusion
  60.8 0.6 gather_fusion.3
  61.4 0.6 gather_fusion.4
  62.0 0.6 gather_fusion.5
  62.7 0.6 gather_fusion.2
  63.5 0.2 fusion.63
  63.7 2.0 %fusion.30 = f32[32,2,64,16]{2,3,1,0:T(8,128)} fusion(f32[32,16,16]{2,1,0:T(8,128)S(1)} %fusion.63, f32[32,16,2]{1,2,0:T(2,128)} %copy.70, f32[32,16,2]{1,2,0:T(2,128)} %copy.68, pred[16,16]{1,0:T(8,128)(4,1)S(1)} %iota_compare_fusion.6, bf16[32,16,2,64]{3,2,1,0:T(2,128)(2,1)S(1)} %reshape.390), kind=kOutput, calls=%fused_computation.67 | convolution fusion | flops 2195456 | bytes 434432 | tf_op jit(solution)/shard_map/rtsh,rshp->rthp/dot_general | solution.py:235
  65.8 2.6 %fusion.10 = f32[48,2,64,128]{3,2,1,0:T(8,128)} fusion(f32[48,16,2,64]{3,1,2,0:T(8,128)S(1)} %gather_fusion.3, pred[48]{0:T(512)(128)(4,1)S(1)} %get-tuple-element.77, pred[48]{0:T(512)(128)(4,1)S(1)} %get-tuple-element.78, bf16[48,16,128]{2,1,0:T(8,128)(2,1)S(1)} %gather_fusion.5), kind=kOutput, calls=%fused_computation.38 | convolution fusion | flops 25559040 | bytes 3735648 | tf_op jit(solution)/shard_map/jshp,jsn->jhpn/dot_general | solution.py:235
  68.5 3.7 %convolution_multiply_fusion = f32[48,16,2,64]{3,1,2,0:T(8,128)} fusion(bf16[48,2,64,128]{3,2,1,0:T(8,128)(2,1)} %all-to-all-done, f32[48,16,2]{1,2,0:T(2,128)S(1)} %select_select_fusion.4, bf16[48,16,128]{2,1,0:T(8,128)(2,1)S(1)} %gather_fusion.4, pred[48]{0:T(512)(128)(4,1)S(1)} %get-tuple-element.77, pred[48]{0:T(512)(128)(4,1)S(1)} %get-tuple-element.78), kind=kOutput, calls=%fused_computation.11 | convolution fusion | flops 25460736 | bytes 2168928 | tf_op jit(solution)/shard_map/jhpn,jtn->jthp/dot_general | solution.py:352
  72.2 1.8 %gather_fusion.1 = f32[32,16,2,64]{3,1,2,0:T(8,128)S(1)} fusion(f32[48,16,2,64]{3,1,2,0:T(8,128)} %convolution_multiply_fusion, s32[1024]{0:T(1024)} %pad_clamp_fusion), kind=kCustom, calls=%fused_computation.3 | custom fusion | bytes 524416 | tf_op jit(solution)/shard_map/jit(_take)/gather | solution.py:355
  74.1 1.4 fusion.2
  75.5 0.3 copy.77
  75.8 0.3 reshape.393
  76.2 3.0 %multiply_reduce_fusion.1 = (f32[512]{0:T(512)S(1)}, f32[512,128]{0,1:T(8,128)S(1)}) fusion(f32[512,128]{0,1:T(8,128)S(1)} %copy.78, bf16[512,2560]{1,0:T(8,128)(2,1)} %bitcast.73, bf16[2560,128]{1,0:T(8,128)(2,1)} %param.30), kind=kOutput, calls=%fused_computation.57 | convolution fusion | flops 336133632 | bytes 3803136 | tf_op jit(solution)/shard_map/dot_general | solution.py:277
  79.3 1.3 fusion.40
  80.7 0.6 scatter.15
  81.3 2.0 %convolution_convert_fusion = bf16[512,2560]{1,0:T(8,128)(2,1)S(1)} fusion(bf16[128,2560]{1,0:T(8,128)(2,1)} %param.40, f32[512,128]{0,1:T(8,128)S(1)} %get-tuple-element.76, f32[128]{0:T(128)S(1)} %copy-done.14), kind=kOutput, calls=%fused_computation.7 | convolution fusion | flops 336986112 | bytes 3539456 | tf_op jit(solution)/shard_map/dot_general | solution.py:368
  83.3 1.8 %pad_maximum_fusion = bf16[512,2688]{1,0:T(8,128)(2,1)} fusion(bf16[512,128]{1,0:T(8,128)(2,1)S(1)} %scatter.15, bf16[512,2560]{1,0:T(8,128)(2,1)S(1)} %convolution_convert_fusion), kind=kLoop, calls=%fused_computation.9 | loop fusion | flops 5505024 | bytes 5505024 | tf_op jit(solution)/shard_map/concatenate | solution.py:373
  85.1 29.6 %shard_map.195 = (bf16[4,8,16,2688]{3,2,1,0:T(8,128)(2,1)}, bf16[2,4,16,2688]{3,2,1,0:T(8,128)(2,1)}) custom-call(bf16[4,8,16,2688]{3,2,1,0:T(8,128)(2,1)} %bitcast.69), custom_call_target="tpu_custom_call" | custom-call | tf_op jit(solution)/shard_map/pallas_call | solution.py:108
  114.7 3.9 %add_convert_fusion = bf16[48,2,64,128]{3,2,1,0:T(8,128)(2,1)} fusion(f32[48,2,64,128]{3,2,1,0:T(8,128)} %fusion.10, bf16[48,2,64,128]{3,2,1,0:T(8,128)(2,1)} %all-to-all-done, f32[48,2]{1,0:T(8,128)S(1)} %select_select_fusion.5, f32[48,16,2,64]{3,1,2,0:T(8,128)S(1)} %gather_fusion.3, pred[48]{0:T(512)(128)(4,1)S(1)} %get-tuple-element.77, ...), kind=kOutput, calls=%fused_computation.8 | convolution fusion | flops 29884416 | bytes 6881760 | tf_op jit(solution)/shard_map/jshp,jsn->jhpn/dot_general | solution.py:235
  118.6 8.5 %all-to-all-start.1 = ((bf16[48,2,64,128]{3,2,1,0:T(8,128)(2,1)}), bf16[48,2,64,128]{3,2,1,0:T(8,128)(2,1)S(1)}, u32[]{:S(2)}, u32[]{:S(2)}) async-start(bf16[48,2,64,128]{3,2,1,0:T(8,128)(2,1)} %add_convert_fusion), calls=%async_computation.1 | async-start | bytes 3145728 | tf_op jit(solution)/shard_map/all_to_all | solution.py:359
  127.1 2.4 %convert_reduce_fusion = f32[8,16,2688]{2,1,0:T(8,128)S(1)} fusion(bf16[4,8,16,2688]{3,2,1,0:T(8,128)(2,1)} %get-tuple-element.52), kind=kLoop, calls=%fused_computation.6 | loop fusion | flops 2408448 | bytes 4128768 | tf_op jit(solution)/shard_map/reduce_sum | solution.py:374
  129.5 0.9 convert_element_type.172
  130.5 1.4 scatter.16
  131.9 2.0 %scatter.19.src_ref = bf16[8,16,2688]{2,1,0:T(8,128)(2,1)} dynamic-update-slice(bf16[8,16,2688]{2,1,0:T(8,128)(2,1)} %scatter.16, bf16[8,16,1]{2,1,0:T(8,128)(2,1)S(1)} %get-tuple-element.55, s32[]{:T(128)} %constant.199.clone.1, s32[]{:T(128)} %constant.199.clone.1, s32[]{:T(128)} %constant.211.clone.1) | dynamic-update-slice | bytes 516 | tf_op jit(solution)/shard_map/scatter | solution.py:379
  133.9 21.3 %shard_map.196 = bf16[8,16,2688]{2,1,0:T(8,128)(2,1)} custom-call(bf16[8,16,2688]{2,1,0:T(8,128)(2,1)} %scatter.19.src_ref), custom_call_target="tpu_custom_call" | custom-call | tf_op jit(solution)/shard_map/pallas_call | solution.py:207
  155.2 1.2 convert_reduce_fusion.1
  156.4 0.2 fusion.51
  156.6 0.7 fusion.44
  157.3 2.1 %convert_element_type.184 = f32[48,2,64,128]{3,2,1,0:T(8,128)} convert(bf16[48,2,64,128]{3,2,1,0:T(8,128)(2,1)S(1)} %all-to-all-done.1) | non-fusion elementwise | flops 786432 | bytes 4718592 | tf_op jit(solution)/shard_map/convert_element_type | solution.py:361
  (87 shorter events, 3.0 us)
Async XLA Ops:
  0.6 51.0 %copy-start = (bf16[2560,256]{1,0:T(8,128)(2,1)S(1)}, bf16[2560,256]{1,0:T(8,128)(2,1)}, u32[]{:S(2)}) copy-start(bf16[2560,256]{1,0:T(8,128)(2,1)} %param.32) | copy-start | bytes 3932164
  4.2 7.6 %copy-start.11 = (s32[32,1]{0,1:T(1,128)S(1)}, s32[32,1]{0,1:T(1,128)}, u32[]{:S(2)}) copy-start(s32[32,1]{0,1:T(1,128)} %param.45) | copy-start | bytes 388
  4.2 41.9 %copy-start.17 = (f32[2]{0:T(128)S(1)}, f32[2]{0:T(128)}, u32[]{:S(2)}) copy-start(f32[2]{0:T(128)} %param.37) | copy-start | bytes 28
  4.2 42.0 %copy-start.7 = (bf16[2560,2]{0,1:T(2,128)(2,1)S(1)}, bf16[2560,2]{0,1:T(2,128)(2,1)}, u32[]{:S(2)}) copy-start(bf16[2560,2]{0,1:T(2,128)(2,1)} %param.33) | copy-start | bytes 30724
  4.2 64.3 %all-to-all-start = ((bf16[48,2,64,128]{3,2,1,0:T(8,128)(2,1)}), bf16[48,2,64,128]{3,2,1,0:T(8,128)(2,1)}, u32[]{:S(2)}, u32[]{:S(2)}) async-start(bf16[48,2,64,128]{3,2,1,0:T(8,128)(2,1)} %convert_element_type.164), calls=%async_computation | async-start | bytes 3145728 | tf_op jit(solution)/shard_map/all_to_all | solution.py:339
  13.9 35.0 %copy-start.18 = (s32[4]{0:T(128)S(1)}, s32[4]{0:T(128)}, u32[]{:S(2)}) copy-start(s32[4]{0:T(128)} %param.44) | copy-start | bytes 52
  13.9 35.2 %copy-start.16 = (f32[4,2]{0,1:T(2,128)S(1)}, f32[4,2]{0,1:T(2,128)}, u32[]{:S(2)}) copy-start(f32[4,2]{0,1:T(2,128)} %param.36) | copy-start | bytes 100
  46.1 5.2 %copy-start.10 = (s32[32]{0:T(128)S(1)}, s32[32]{0:T(128)}, u32[]{:S(2)}) copy-start(s32[32]{0:T(128)} %param.46) | copy-start | bytes 388
  51.4 2.9 %copy-start.12 = (s32[32]{0:T(128)S(1)}, s32[32]{0:T(128)}, u32[]{:S(2)}) copy-start(s32[32]{0:T(128)} %param.47) | copy-start | bytes 388
  51.4 3.1 %copy-start.8 = (f32[4,256]{1,0:T(4,128)S(1)}, f32[4,256]{1,0:T(4,128)}, u32[]{:S(2)}) copy-start(f32[4,256]{1,0:T(4,128)} %param.35) | copy-start | bytes 12292
  51.5 3.7 %copy-start.15 = (bf16[2560,128]{1,0:T(8,128)(2,1)S(1)}, bf16[2560,128]{1,0:T(8,128)(2,1)}, u32[]{:S(2)}) copy-start(bf16[2560,128]{1,0:T(8,128)(2,1)} %param.31) | copy-start | bytes 1966084
  54.3 3.5 %copy-start.6 = (bf16[32,3,128]{2,0,1:T(8,128)(2,1)S(1)}, bf16[32,3,128]{2,0,1:T(8,128)(2,1)}, u32[]{:S(2)}) copy-start(bf16[32,3,128]{2,0,1:T(8,128)(2,1)} %param.41) | copy-start | bytes 73732
  54.3 3.6 %copy-start.9 = (f32[4,128]{1,0:T(4,128)S(1)}, f32[4,128]{1,0:T(4,128)}, u32[]{:S(2)}) copy-start(f32[4,128]{1,0:T(4,128)} %param.34) | copy-start | bytes 6148
  55.2 3.4 %copy-start.3 = (bf16[32,3,256]{2,0,1:T(8,128)(2,1)S(1)}, bf16[32,3,256]{2,0,1:T(8,128)(2,1)}, u32[]{:S(2)}) copy-start(bf16[32,3,256]{2,0,1:T(8,128)(2,1)} %param.42) | copy-start | bytes 147460
  63.7 4.7 %copy-start.1 = (f32[32,16,16]{2,1,0:T(8,128)}, f32[32,16,16]{2,1,0:T(8,128)S(1)}, u32[]{:S(2)}) copy-start(f32[32,16,16]{2,1,0:T(8,128)S(1)} %fusion.63) | copy-start | bytes 98308
  68.4 5.6 %copy-start.4 = (f32[32,16,2]{1,2,0:T(2,128)S(1)}, f32[32,16,2]{1,2,0:T(2,128)}, u32[]{:S(2)}) copy-start(f32[32,16,2]{1,2,0:T(2,128)} %copy.68) | copy-start | bytes 12292
  68.4 5.6 %copy-start.5 = (f32[32,16,2]{1,2,0:T(2,128)S(1)}, f32[32,16,2]{1,2,0:T(2,128)}, u32[]{:S(2)}) copy-start(f32[32,16,2]{1,2,0:T(2,128)} %copy.70) | copy-start | bytes 12292
  68.4 5.6 %copy-start.13 = (pred[32]{0:T(512)(128)(4,1)S(1)}, pred[32]{0:T(512)(128)(4,1)}, u32[]{:S(2)}) copy-start(pred[32]{0:T(512)(128)(4,1)} %get-tuple-element.57) | copy-start | bytes 100
  68.4 5.6 %copy-start.19 = (f32[2]{0:T(128)S(1)}, f32[2]{0:T(128)}, u32[]{:S(2)}) copy-start(f32[2]{0:T(128)} %param.38) | copy-start | bytes 28
  68.4 5.6 %copy-start.2 = (f32[32,16,16]{2,1,0:T(8,128)S(1)}, f32[32,16,16]{2,1,0:T(8,128)}, u32[]{:S(2)}) copy-start(f32[32,16,16]{2,1,0:T(8,128)} %copy-done.1) | copy-start | bytes 98308
  76.2 5.1 %copy-start.14 = (f32[128]{0:T(128)S(1)}, f32[128]{0:T(128)}, u32[]{:S(2)}) copy-start(f32[128]{0:T(128)} %param.39) | copy-start | bytes 1540
  118.6 38.7 %all-to-all-start.1 = ((bf16[48,2,64,128]{3,2,1,0:T(8,128)(2,1)}), bf16[48,2,64,128]{3,2,1,0:T(8,128)(2,1)S(1)}, u32[]{:S(2)}, u32[]{:S(2)}) async-start(bf16[48,2,64,128]{3,2,1,0:T(8,128)(2,1)} %add_convert_fusion), calls=%async_computation.1 | async-start | bytes 3145728 | tf_op jit(solution)/shard_map/all_to_all | solution.py:359

commit v13 on v11

--- a/solution.py
+++ b/solution.py
@@ -13,33 +13,52 @@
 Y_CHIPS = 4
 
 
-def exchange_kernel(n, axis, gather, src_ref, dst_ref, send_sem, recv_sem, local_sem):
+def exchange_kernel(n, axis, gather, src_ref, dst_ref, stage_ref, send_sem, recv_sem, local_sem):
     me = lax.axis_index(axis)
     coords = {name: lax.axis_index(name) for name in AXES}
+    far = n // 2 if (not gather and n >= 4 and n % 2 == 0) else 0
+    half = dst_ref.shape[1] // 2
+    first, second = pl.ds(0, half), pl.ds(half, half)
 
     def device_of(peer):
         return tuple(peer if name == axis else coords[name] for name in AXES)
+
+    def remote(src, dst, index, peer):
+        copy = pltpu.make_async_remote_copy(
+            src_ref=src,
+            dst_ref=dst,
+            send_sem=send_sem.at[index],
+            recv_sem=recv_sem.at[index],
+            device_id=device_of(peer),
+            device_id_type=MESH,
+        )
+        copy.start()
+        return copy
 
     barrier = pltpu.get_barrier_semaphore()
     for offset in range(1, n):
         peer = lax.rem(me + offset, n)
         pl.semaphore_signal(barrier, inc=1, device_id=device_of(peer), device_id_type=MESH)
     pl.semaphore_wait(barrier, n - 1)
+    if far:
+        left = lax.rem(me + n - 1, n)
+        staged = remote(src_ref.at[lax.rem(me + far, n), second], stage_ref, n, left)
     local = pltpu.make_async_copy(src_ref if gather else src_ref.at[me], dst_ref.at[me], local_sem)
     local.start()
     copies = []
     for offset in sorted(range(1, n), key=lambda offset: (min(offset, n - offset), offset)):
         peer = lax.rem(me + offset, n)
-        copy = pltpu.make_async_remote_copy(
-            src_ref=src_ref if gather else src_ref.at[peer],
-            dst_ref=dst_ref.at[me],
-            send_sem=send_sem.at[offset],
-            recv_sem=recv_sem.at[offset],
-            device_id=device_of(peer),
-            device_id_type=MESH,
-        )
-        copy.start()
-        copies.append(copy)
+        if offset == far:
+            copies.append(remote(src_ref.at[peer, first], dst_ref.at[me, first], offset, peer))
+        else:
+            copies.append(remote(src_ref if gather else src_ref.at[peer], dst_ref.at[me], offset, peer))
+    if far:
+        staged.wait_recv()
+        origin = lax.rem(me + 1, n)
+        copies.append(
+            remote(stage_ref, dst_ref.at[origin, second], n + 1, lax.rem(origin + far, n))
+        )
+        staged.wait_send()
     local.wait()
     for copy in copies:
         copy.wait()
@@ -206,16 +225,19 @@
     block = src.shape if gather else src.shape[1:]
     return pl.pallas_call(
         functools.partial(exchange_kernel, n, axis, gather),
-        out_shape=jax.ShapeDtypeStruct((n,) + tuple(block), src.dtype),
+        out_shape=(
+            jax.ShapeDtypeStruct((n,) + tuple(block), src.dtype),
+            jax.ShapeDtypeStruct((block[0] // 2,) + tuple(block[1:]), src.dtype),
+        ),
         in_specs=[pl.BlockSpec(memory_space=pl.ANY)],
-        out_specs=pl.BlockSpec(memory_space=pl.ANY),
+        out_specs=(pl.BlockSpec(memory_space=pl.ANY), pl.BlockSpec(memory_space=pl.ANY)),
         scratch_shapes=[
-            pltpu.SemaphoreType.DMA((n,)),
-            pltpu.SemaphoreType.DMA((n,)),
+            pltpu.SemaphoreType.DMA((n + 2,)),
+            pltpu.SemaphoreType.DMA((n + 2,)),
             pltpu.SemaphoreType.DMA,
         ],
         compiler_params=pltpu.CompilerParams(collective_id=collective_id, has_side_effects=True),
-    )(src)
+    )(src)[0]
 
 
 def convolve(edge_cells, fresh_cells, kernel, edge_mask):

time: 160 us -> 161 us (level); the launches traced: 159 us -> 158 us
  transfers between devices with their start and end apart: 2 -> 2, of which waited for: 0 -> 0; matrix products, arithmetic and copies ran while one was open for 21% -> 21% of each run, Pallas kernels for 34% -> 33%
where the time goes in v13:
time: 161 us; the launch traced here: 158 us
  Pallas kernels  81.8 us (51%)
  matrix products  26.8 us (17%)
  other arithmetic  19.5 us (12%)
  starting transfers between devices  15.8 us (10%)
  local copies, waits for them, and re-layouts  12.7 us (8%)
    pallas_call x1, Pallas kernels, gather2d(): pl.pallas_call(functools.partial(gather2d_kernel, nz), out_shape=jax.Shap...  32.6 us
    pallas_call x1, Pallas kernels, exchange4(): pl.pallas_call(functools.partial(ring4_kernel, axis, gather), out_shape=(...  29.5 us
    pallas_call x1, Pallas kernels, exchange(): pl.pallas_call(functools.partial(exchange_kernel, n, axis, gather), out_s...  19.7 us
    dot_general x4, matrix products, shards(): jnp.dot(block_rows, weight_cols, preferred_element_type=jnp.float32)  10.7 us
    all_to_all x1, starting transfers between devices, shards(): lax.all_to_all(buffer.astype(jnp.bfloat16), 'rep', split_axis=0, concat_a...  8.21 us
    all_to_all x1, starting transfers between devices, shards(): lax.all_to_all(pool.astype(jnp.bfloat16), 'rep', split_axis=0, concat_axi...  7.55 us
    dot_general x2, matrix products, split_dot(): jnp.einsum(spec, low, narrow, preferred_element_type=jnp.float32)  5.37 us
    dot_general x2, matrix products, split_dot(): jnp.einsum(spec, high, narrow, preferred_element_type=jnp.float32)  4.69 us
  transfers between devices with their start and end apart: 2, of which 0 were waited for; matrix products, arithmetic and copies ran while one was open for 21% of the time, Pallas kernels for 33%

profile of v13, /device:TPU:1, one launch (start us, length us, event | category | flops | bytes accessed | tf_op | source)
XLA Modules:
  0.0 157.8 jit_solution(5944376554092081990)
XLA Ops:
  0.6 3.5 %convert_element_type.164 = bf16[48,2,64,128]{3,2,1,0:T(8,128)(2,1)} convert(f32[48,2,64,128]{3,2,1,0:T(8,128)} %param.43) | non-fusion elementwise | flops 786432 | bytes 4718592 | tf_op jit(solution)/shard_map/convert_element_type | solution.py:362
  4.2 7.6 %all-to-all-start = ((bf16[48,2,64,128]{3,2,1,0:T(8,128)(2,1)}), bf16[48,2,64,128]{3,2,1,0:T(8,128)(2,1)}, u32[]{:S(2)}, u32[]{:S(2)}) async-start(bf16[48,2,64,128]{3,2,1,0:T(8,128)(2,1)} %convert_element_type.164), calls=%async_computation | async-start | bytes 3145728 | tf_op jit(solution)/shard_map/all_to_all | solution.py:361
  12.0 0.5 and_bitcast_fusion
  12.5 0.6 compare_reduce_fusion
  13.2 0.7 compare_reduce_fusion.1
  13.9 32.6 %shard_map.194 = bf16[4,8,16,2560]{3,2,1,0:T(8,128)(2,1)} custom-call(bf16[16,2560]{1,0:T(8,128)(2,1)} %bitcast.76), custom_call_target="tpu_custom_call" | custom-call | tf_op jit(solution)/shard_map/pallas_call | solution.py:209
  46.5 2.5 %fusion.4 = f32[512,2]{0,1:T(2,128)S(1)} fusion(bf16[512,2560]{1,0:T(8,128)(2,1)} %bitcast.70, bf16[2560,2]{0,1:T(2,128)(2,1)S(1)} %copy-done.7), kind=kOutput, calls=%fused_computation.21 | convolution fusion | flops 5244928 | bytes 2635776 | tf_op jit(solution)/shard_map/dot_general | solution.py:299
  49.2 0.2 reduce-window.4
  49.5 0.2 fusion.47
  49.9 0.7 fusion.69
  50.7 0.9 copy.68
  52.0 2.6 %convolution_convert_fusion.1 = bf16[512,256]{1,0:T(8,128)(2,1)S(1)} fusion(bf16[512,2560]{1,0:T(8,128)(2,1)} %bitcast.71, bf16[2560,256]{1,0:T(8,128)(2,1)S(1)} %copy-done), kind=kOutput, calls=%fused_computation.16 | convolution fusion | flops 671219712 | bytes 4194304 | tf_op jit(solution)/shard_map/dot_general | solution.py:299
  54.9 0.7 copy.70
  55.6 2.6 %convolution_convert_fusion.3 = bf16[512,128]{1,0:T(8,128)(2,1)S(1)} fusion(bf16[512,2560]{1,0:T(8,128)(2,1)} %bitcast.72, bf16[2560,128]{1,0:T(8,128)(2,1)S(1)} %copy-done.15), kind=kOutput, calls=%fused_computation.19 | convolution fusion | flops 335609856 | bytes 3407872 | tf_op jit(solution)/shard_map/dot_general | solution.py:299
  58.7 0.3 copy.76
  59.2 0.3 multiply_convert_fusion
  59.6 0.6 pad_clamp_fusion
  60.3 0.6 gather_fusion
  61.0 0.2 convert_multiply_fusion
  61.2 0.6 gather_fusion.3
  61.8 0.6 gather_fusion.4
  62.4 0.6 gather_fusion.5
  63.0 0.6 gather_fusion.2
  63.9 0.2 fusion.63
  64.1 2.0 %fusion.30 = f32[32,2,64,16]{2,3,1,0:T(8,128)} fusion(f32[32,16,16]{2,1,0:T(8,128)S(1)} %fusion.63, f32[32,16,2]{1,2,0:T(2,128)} %copy.70, f32[32,16,2]{1,2,0:T(2,128)} %copy.68, pred[16,16]{1,0:T(8,128)(4,1)S(1)} %iota_compare_fusion.6, bf16[32,16,2,64]{3,2,1,0:T(2,128)(2,1)S(1)} %reshape.390), kind=kOutput, calls=%fused_computation.67 | convolution fusion | flops 2195456 | bytes 434432 | tf_op jit(solution)/shard_map/rtsh,rshp->rthp/dot_general | solution.py:257
  66.1 2.6 %fusion.10 = f32[48,2,64,128]{3,2,1,0:T(8,128)} fusion(f32[48,16,2,64]{3,1,2,0:T(8,128)S(1)} %gather_fusion.3, pred[48]{0:T(512)(128)(4,1)S(1)} %get-tuple-element.79, pred[48]{0:T(512)(128)(4,1)S(1)} %get-tuple-element.80, bf16[48,16,128]{2,1,0:T(8,128)(2,1)S(1)} %gather_fusion.5), kind=kOutput, calls=%fused_computation.38 | convolution fusion | flops 25559040 | bytes 3735648 | tf_op jit(solution)/shard_map/jshp,jsn->jhpn/dot_general | solution.py:257
  68.8 3.7 %convolution_multiply_fusion = f32[48,16,2,64]{3,1,2,0:T(8,128)} fusion(bf16[48,2,64,128]{3,2,1,0:T(8,128)(2,1)} %all-to-all-done, f32[48,16,2]{1,2,0:T(2,128)S(1)} %select_select_fusion.4, bf16[48,16,128]{2,1,0:T(8,128)(2,1)S(1)} %gather_fusion.4, pred[48]{0:T(512)(128)(4,1)S(1)} %get-tuple-element.79, pred[48]{0:T(512)(128)(4,1)S(1)} %get-tuple-element.80), kind=kOutput, calls=%fused_computation.11 | convolution fusion | flops 25460736 | bytes 2168928 | tf_op jit(solution)/shard_map/jhpn,jtn->jthp/dot_general | solution.py:374
  72.5 1.8 %gather_fusion.1 = f32[32,16,2,64]{3,1,2,0:T(8,128)S(1)} fusion(f32[48,16,2,64]{3,1,2,0:T(8,128)} %convolution_multiply_fusion, s32[1024]{0:T(1024)} %pad_clamp_fusion), kind=kCustom, calls=%fused_computation.3 | custom fusion | bytes 524416 | tf_op jit(solution)/shard_map/jit(_take)/gather | solution.py:377
  74.4 1.4 fusion.2
  75.8 0.3 copy.77
  76.1 0.3 reshape.393
  76.6 2.9 %multiply_reduce_fusion.1 = (f32[512]{0:T(512)S(1)}, f32[512,128]{0,1:T(8,128)S(1)}) fusion(f32[512,128]{0,1:T(8,128)S(1)} %copy.78, bf16[512,2560]{1,0:T(8,128)(2,1)} %bitcast.73, bf16[2560,128]{1,0:T(8,128)(2,1)} %param.30), kind=kOutput, calls=%fused_computation.57 | convolution fusion | flops 336133632 | bytes 3803136 | tf_op jit(solution)/shard_map/dot_general | solution.py:299
  79.7 1.3 fusion.40
  81.0 0.6 scatter.15
  81.6 2.0 %convolution_convert_fusion = bf16[512,2560]{1,0:T(8,128)(2,1)S(1)} fusion(bf16[128,2560]{1,0:T(8,128)(2,1)} %param.40, f32[512,128]{0,1:T(8,128)S(1)} %get-tuple-element.78, f32[128]{0:T(128)S(1)} %copy-done.14), kind=kOutput, calls=%fused_computation.7 | convolution fusion | flops 336986112 | bytes 3539456 | tf_op jit(solution)/shard_map/dot_general | solution.py:390
  83.7 1.8 %pad_maximum_fusion = bf16[512,2688]{1,0:T(8,128)(2,1)} fusion(bf16[512,128]{1,0:T(8,128)(2,1)S(1)} %scatter.15, bf16[512,2560]{1,0:T(8,128)(2,1)S(1)} %convolution_convert_fusion), kind=kLoop, calls=%fused_computation.9 | loop fusion | flops 5505024 | bytes 5505024 | tf_op jit(solution)/shard_map/concatenate | solution.py:395
  85.4 29.5 %shard_map.195 = (bf16[4,8,16,2688]{3,2,1,0:T(8,128)(2,1)}, bf16[2,4,16,2688]{3,2,1,0:T(8,128)(2,1)}) custom-call(bf16[4,8,16,2688]{3,2,1,0:T(8,128)(2,1)} %bitcast.69), custom_call_target="tpu_custom_call" | custom-call | tf_op jit(solution)/shard_map/pallas_call | solution.py:127
  114.9 3.9 %add_convert_fusion = bf16[48,2,64,128]{3,2,1,0:T(8,128)(2,1)} fusion(f32[48,2,64,128]{3,2,1,0:T(8,128)} %fusion.10, bf16[48,2,64,128]{3,2,1,0:T(8,128)(2,1)} %all-to-all-done, f32[48,2]{1,0:T(8,128)S(1)} %select_select_fusion.5, f32[48,16,2,64]{3,1,2,0:T(8,128)S(1)} %gather_fusion.3, pred[48]{0:T(512)(128)(4,1)S(1)} %get-tuple-element.79, ...), kind=kOutput, calls=%fused_computation.8 | convolution fusion | flops 29884416 | bytes 6881760 | tf_op jit(solution)/shard_map/jshp,jsn->jhpn/dot_general | solution.py:257
  118.9 8.2 %all-to-all-start.1 = ((bf16[48,2,64,128]{3,2,1,0:T(8,128)(2,1)}), bf16[48,2,64,128]{3,2,1,0:T(8,128)(2,1)S(1)}, u32[]{:S(2)}, u32[]{:S(2)}) async-start(bf16[48,2,64,128]{3,2,1,0:T(8,128)(2,1)} %add_convert_fusion), calls=%async_computation.1 | async-start | bytes 3145728 | tf_op jit(solution)/shard_map/all_to_all | solution.py:381
  127.1 2.4 %convert_reduce_fusion = f32[8,16,2688]{2,1,0:T(8,128)S(1)} fusion(bf16[4,8,16,2688]{3,2,1,0:T(8,128)(2,1)} %get-tuple-element.53), kind=kLoop, calls=%fused_computation.6 | loop fusion | flops 2408448 | bytes 4128768 | tf_op jit(solution)/shard_map/reduce_sum | solution.py:396
  129.4 0.9 convert_element_type.172
  130.5 1.4 scatter.16
  131.9 2.0 %scatter.19.src_ref = bf16[8,16,2688]{2,1,0:T(8,128)(2,1)} dynamic-update-slice(bf16[8,16,2688]{2,1,0:T(8,128)(2,1)} %scatter.16, bf16[8,16,1]{2,1,0:T(8,128)(2,1)S(1)} %get-tuple-element.57, s32[]{:T(128)} %constant.199.clone.1, s32[]{:T(128)} %constant.199.clone.1, s32[]{:T(128)} %constant.211.clone.1) | dynamic-update-slice | bytes 516 | tf_op jit(solution)/shard_map/scatter | solution.py:401
  133.9 19.7 %shard_map.196 = (bf16[8,16,2688]{2,1,0:T(8,128)(2,1)}, bf16[8,2688]{1,0:T(8,128)(2,1)}) custom-call(bf16[8,16,2688]{2,1,0:T(8,128)(2,1)} %scatter.19.src_ref), custom_call_target="tpu_custom_call" | custom-call | tf_op jit(solution)/shard_map/pallas_call | solution.py:226
  153.6 1.2 convert_reduce_fusion.1
  154.8 0.2 fusion.51
  155.0 0.7 fusion.44
  155.7 2.1 %convert_element_type.184 = f32[48,2,64,128]{3,2,1,0:T(8,128)} convert(bf16[48,2,64,128]{3,2,1,0:T(8,128)(2,1)S(1)} %all-to-all-done.1) | non-fusion elementwise | flops 786432 | bytes 4718592 | tf_op jit(solution)/shard_map/convert_element_type | solution.py:383
  (87 shorter events, 3.0 us)
Async XLA Ops:
  0.6 51.4 %copy-start = (bf16[2560,256]{1,0:T(8,128)(2,1)S(1)}, bf16[2560,256]{1,0:T(8,128)(2,1)}, u32[]{:S(2)}) copy-start(bf16[2560,256]{1,0:T(8,128)(2,1)} %param.32) | copy-start | bytes 3932164
  4.2 7.6 %copy-start.11 = (s32[32,1]{0,1:T(1,128)S(1)}, s32[32,1]{0,1:T(1,128)}, u32[]{:S(2)}) copy-start(s32[32,1]{0,1:T(1,128)} %param.45) | copy-start | bytes 388
  4.2 42.3 %copy-start.17 = (f32[2]{0:T(128)S(1)}, f32[2]{0:T(128)}, u32[]{:S(2)}) copy-start(f32[2]{0:T(128)} %param.37) | copy-start | bytes 28
  4.2 42.3 %copy-start.7 = (bf16[2560,2]{0,1:T(2,128)(2,1)S(1)}, bf16[2560,2]{0,1:T(2,128)(2,1)}, u32[]{:S(2)}) copy-start(bf16[2560,2]{0,1:T(2,128)(2,1)} %param.33) | copy-start | bytes 30724
  4.2 64.6 %all-to-all-start = ((bf16[48,2,64,128]{3,2,1,0:T(8,128)(2,1)}), bf16[48,2,64,128]{3,2,1,0:T(8,128)(2,1)}, u32[]{:S(2)}, u32[]{:S(2)}) async-start(bf16[48,2,64,128]{3,2,1,0:T(8,128)(2,1)} %convert_element_type.164), calls=%async_computation | async-start | bytes 3145728 | tf_op jit(solution)/shard_map/all_to_all | solution.py:361
  13.9 35.3 %copy-start.18 = (s32[4]{0:T(128)S(1)}, s32[4]{0:T(128)}, u32[]{:S(2)}) copy-start(s32[4]{0:T(128)} %param.44) | copy-start | bytes 52
  13.9 35.6 %copy-start.16 = (f32[4,2]{0,1:T(2,128)S(1)}, f32[4,2]{0,1:T(2,128)}, u32[]{:S(2)}) copy-start(f32[4,2]{0,1:T(2,128)} %param.36) | copy-start | bytes 100
  46.5 5.2 %copy-start.10 = (s32[32]{0:T(128)S(1)}, s32[32]{0:T(128)}, u32[]{:S(2)}) copy-start(s32[32]{0:T(128)} %param.46) | copy-start | bytes 388
  51.7 2.9 %copy-start.12 = (s32[32]{0:T(128)S(1)}, s32[32]{0:T(128)}, u32[]{:S(2)}) copy-start(s32[32]{0:T(128)} %param.47) | copy-start | bytes 388
  51.8 3.1 %copy-start.8 = (f32[4,256]{1,0:T(4,128)S(1)}, f32[4,256]{1,0:T(4,128)}, u32[]{:S(2)}) copy-start(f32[4,256]{1,0:T(4,128)} %param.35) | copy-start | bytes 12292
  51.9 3.7 %copy-start.15 = (bf16[2560,128]{1,0:T(8,128)(2,1)S(1)}, bf16[2560,128]{1,0:T(8,128)(2,1)}, u32[]{:S(2)}) copy-start(bf16[2560,128]{1,0:T(8,128)(2,1)} %param.31) | copy-start | bytes 1966084
  54.7 3.5 %copy-start.6 = (bf16[32,3,128]{2,0,1:T(8,128)(2,1)S(1)}, bf16[32,3,128]{2,0,1:T(8,128)(2,1)}, u32[]{:S(2)}) copy-start(bf16[32,3,128]{2,0,1:T(8,128)(2,1)} %param.41) | copy-start | bytes 73732
  54.7 3.6 %copy-start.9 = (f32[4,128]{1,0:T(4,128)S(1)}, f32[4,128]{1,0:T(4,128)}, u32[]{:S(2)}) copy-start(f32[4,128]{1,0:T(4,128)} %param.34) | copy-start | bytes 6148
  55.6 3.4 %copy-start.3 = (bf16[32,3,256]{2,0,1:T(8,128)(2,1)S(1)}, bf16[32,3,256]{2,0,1:T(8,128)(2,1)}, u32[]{:S(2)}) copy-start(bf16[32,3,256]{2,0,1:T(8,128)(2,1)} %param.42) | copy-start | bytes 147460
  64.1 4.7 %copy-start.1 = (f32[32,16,16]{2,1,0:T(8,128)}, f32[32,16,16]{2,1,0:T(8,128)S(1)}, u32[]{:S(2)}) copy-start(f32[32,16,16]{2,1,0:T(8,128)S(1)} %fusion.63) | copy-start | bytes 98308
  68.8 5.6 %copy-start.4 = (f32[32,16,2]{1,2,0:T(2,128)S(1)}, f32[32,16,2]{1,2,0:T(2,128)}, u32[]{:S(2)}) copy-start(f32[32,16,2]{1,2,0:T(2,128)} %copy.68) | copy-start | bytes 12292
  68.8 5.6 %copy-start.5 = (f32[32,16,2]{1,2,0:T(2,128)S(1)}, f32[32,16,2]{1,2,0:T(2,128)}, u32[]{:S(2)}) copy-start(f32[32,16,2]{1,2,0:T(2,128)} %copy.70) | copy-start | bytes 12292
  68.8 5.6 %copy-start.13 = (pred[32]{0:T(512)(128)(4,1)S(1)}, pred[32]{0:T(512)(128)(4,1)}, u32[]{:S(2)}) copy-start(pred[32]{0:T(512)(128)(4,1)} %get-tuple-element.59) | copy-start | bytes 100
  68.8 5.6 %copy-start.19 = (f32[2]{0:T(128)S(1)}, f32[2]{0:T(128)}, u32[]{:S(2)}) copy-start(f32[2]{0:T(128)} %param.38) | copy-start | bytes 28
  68.8 5.6 %copy-start.2 = (f32[32,16,16]{2,1,0:T(8,128)S(1)}, f32[32,16,16]{2,1,0:T(8,128)}, u32[]{:S(2)}) copy-start(f32[32,16,16]{2,1,0:T(8,128)} %copy-done.1) | copy-start | bytes 98308
  76.6 5.1 %copy-start.14 = (f32[128]{0:T(128)S(1)}, f32[128]{0:T(128)}, u32[]{:S(2)}) copy-start(f32[128]{0:T(128)} %param.39) | copy-start | bytes 1540
  118.9 36.8 %all-to-all-start.1 = ((bf16[48,2,64,128]{3,2,1,0:T(8,128)(2,1)}), bf16[48,2,64,128]{3,2,1,0:T(8,128)(2,1)S(1)}, u32[]{:S(2)}, u32[]{:S(2)}) async-start(bf16[48,2,64,128]{3,2,1,0:T(8,128)(2,1)} %add_convert_fusion), calls=%async_computation.1 | async-start | bytes 3145728 | tf_op jit(solution)/shard_map/all_to_all | solution.py:381

commit v14 on v11

--- a/solution.py
+++ b/solution.py
@@ -367,17 +367,22 @@
     scaled = (gated * norm_gain[None, :]).astype(jnp.bfloat16)
     partial = jnp.dot(scaled, w_out, preferred_element_type=jnp.float32).astype(jnp.bfloat16)
     width = partial.shape[1]
-    extra = jnp.zeros((partial.shape[0], 128), jnp.bfloat16)
-    extra = extra.at[:, 0].set(sq_hi).at[:, 1].set(sq_lo)
+    extra_column = lax.broadcasted_iota(jnp.int32, (partial.shape[0], 128), 1)
+    extra = jnp.where(
+        extra_column == 0, sq_hi[:, None], jnp.where(extra_column == 1, sq_lo[:, None], jnp.zeros((), jnp.bfloat16))
+    )
     n_y = lax.axis_size("by")
     packed = jnp.concatenate([partial, extra], 1).reshape(n_y, n_blk // n_y, local_rows, width + 128)
     half_sum = jnp.sum(exchange4(packed, "by", False, 2).astype(jnp.float32), axis=0)
     sq_mid = half_sum[:, :, width] + half_sum[:, :, width + 1]
     sq_mid_hi = sq_mid.astype(jnp.bfloat16)
     sq_mid_lo = (sq_mid - sq_mid_hi.astype(jnp.float32)).astype(jnp.bfloat16)
-    half_packed = (
-        half_sum.astype(jnp.bfloat16).at[:, :, width].set(sq_mid_hi).at[:, :, width + 1].set(sq_mid_lo)
-    )
+    column = lax.broadcasted_iota(jnp.int32, half_sum.shape, 2)
+    half_packed = jnp.where(
+        column == width,
+        sq_mid_hi.astype(jnp.float32)[:, :, None],
+        jnp.where(column == width + 1, sq_mid_lo.astype(jnp.float32)[:, :, None], half_sum),
+    ).astype(jnp.bfloat16)
     summed = jnp.sum(exchange(half_packed, "bz", False, 3).astype(jnp.float32), axis=0)
     inner_all = inner_here * n_blk
     mean_sq = (summed[:, width] + summed[:, width + 1]) / inner_all

time: 160 us -> 156 us (0.975)
  local copies, waits for them, and re-layouts: 12.7 us -> 9.9 us
    scatter x4 -> x0, local copies, waits for them, and re-layouts: 4.02 us -> none  [the longest x2 3.41 us: shards(): half_sum.astype(jnp.bfloat16).at[:, :, width].set(sq_mid_hi)]
    another operation x4 -> x1, other arithmetic: 2.83 us -> 0.18 us
    convert_element_type x2 -> x3, other arithmetic: 1.01 us -> 2.73 us  [the longest x1 2.54 us: shards(): half_packed = jnp.where(column == width, sq_mid_hi.astype(jnp.float32)[:,...]
  transfers between devices with their start and end apart: 2 -> 2, of which waited for: 0 -> 0; matrix products, arithmetic and copies ran while one was open for 21% -> 18% of each run, Pallas kernels for 34% -> 35%
where the time goes in v14:
time: 156 us
  Pallas kernels  83.5 us (54%)
  matrix products  25.4 us (16%)
  other arithmetic  19.6 us (13%)
  starting transfers between devices  16.1 us (10%)
  local copies, waits for them, and re-layouts  9.9 us (6%)
    pallas_call x1, Pallas kernels, gather2d(): pl.pallas_call(functools.partial(gather2d_kernel, nz), out_shape=jax.Shap...  32.6 us
    pallas_call x1, Pallas kernels, exchange4(): pl.pallas_call(functools.partial(ring4_kernel, axis, gather), out_shape=(...  29.4 us
    pallas_call x1, Pallas kernels, exchange(): pl.pallas_call(functools.partial(exchange_kernel, n, axis, gather), out_s...  21.4 us
    dot_general x4, matrix products, shards(): jnp.dot(block_rows, weight_cols, preferred_element_type=jnp.float32)  10.7 us
    all_to_all x1, starting transfers between devices, shards(): lax.all_to_all(buffer.astype(jnp.bfloat16), 'rep', split_axis=0, concat_a...  8.56 us
    all_to_all x1, starting transfers between devices, shards(): lax.all_to_all(pool.astype(jnp.bfloat16), 'rep', split_axis=0, concat_axi...  7.55 us
    dot_general x2, matrix products, split_dot(): jnp.einsum(spec, low, narrow, preferred_element_type=jnp.float32)  4.95 us
    dot_general x2, matrix products, split_dot(): jnp.einsum(spec, high, narrow, preferred_element_type=jnp.float32)  4.7 us
  transfers between devices with their start and end apart: 2, of which 0 were waited for; matrix products, arithmetic and copies ran while one was open for 18% of the time, Pallas kernels for 35%

profile of v14, /device:TPU:1, one launch (start us, length us, event | category | flops | bytes accessed | tf_op | source)
XLA Modules:
  0.0 155.7 jit_solution(10874705156325628753)
XLA Ops:
  0.6 3.5 %convert_element_type.165 = bf16[48,2,64,128]{3,2,1,0:T(8,128)(2,1)} convert(f32[48,2,64,128]{3,2,1,0:T(8,128)} %param.35) | non-fusion elementwise | flops 786432 | bytes 4718592 | tf_op jit(solution)/shard_map/convert_element_type | solution.py:340
  4.2 7.6 %all-to-all-start = ((bf16[48,2,64,128]{3,2,1,0:T(8,128)(2,1)}), bf16[48,2,64,128]{3,2,1,0:T(8,128)(2,1)}, u32[]{:S(2)}, u32[]{:S(2)}) async-start(bf16[48,2,64,128]{3,2,1,0:T(8,128)(2,1)} %convert_element_type.165), calls=%async_computation | async-start | bytes 3145728 | tf_op jit(solution)/shard_map/all_to_all | solution.py:339
  11.7 0.6 iota_compare_fusion.8
  12.6 0.6 and_bitcast_fusion
  13.2 32.6 %shard_map.194 = bf16[4,8,16,2560]{3,2,1,0:T(8,128)(2,1)} custom-call(bf16[16,2560]{1,0:T(8,128)(2,1)} %bitcast.75), custom_call_target="tpu_custom_call" | custom-call | tf_op jit(solution)/shard_map/pallas_call | solution.py:190
  45.9 2.5 %fusion.4 = f32[512,2]{0,1:T(2,128)S(1)} fusion(bf16[512,2560]{1,0:T(8,128)(2,1)} %bitcast.69, bf16[2560,2]{0,1:T(2,128)(2,1)S(1)} %copy-done.10), kind=kOutput, calls=%fused_computation.22 | convolution fusion | flops 5244928 | bytes 2635776 | tf_op jit(solution)/shard_map/dot_general | solution.py:277
  48.6 0.2 reduce-window.4
  48.9 0.2 fusion.46
  49.1 0.2 copy.63
  49.3 0.7 fusion.67
  50.1 0.9 copy.64
  51.4 2.6 %convolution_convert_fusion.1 = bf16[512,256]{1,0:T(8,128)(2,1)S(1)} fusion(bf16[512,2560]{1,0:T(8,128)(2,1)} %bitcast.70, bf16[2560,256]{1,0:T(8,128)(2,1)S(1)} %copy-done), kind=kOutput, calls=%fused_computation.17 | convolution fusion | flops 671219712 | bytes 4194304 | tf_op jit(solution)/shard_map/dot_general | solution.py:277
  54.3 0.7 copy.66
  55.0 2.6 %convolution_convert_fusion.3 = bf16[512,128]{1,0:T(8,128)(2,1)S(1)} fusion(bf16[512,2560]{1,0:T(8,128)(2,1)} %bitcast.71, bf16[2560,128]{1,0:T(8,128)(2,1)S(1)} %copy-done.21), kind=kOutput, calls=%fused_computation.20 | convolution fusion | flops 335609856 | bytes 3407872 | tf_op jit(solution)/shard_map/dot_general | solution.py:277
  57.8 0.2 multiply_convert_fusion.2
  58.1 0.3 copy.72
  58.6 0.3 multiply_convert_fusion
  59.0 0.6 pad_clamp_fusion
  59.7 0.6 gather_fusion
  60.4 0.2 convert_multiply_fusion
  60.6 0.6 gather_fusion.3
  61.2 0.6 gather_fusion.4
  61.8 0.7 gather_fusion.5
  62.6 0.7 gather_fusion.2
  63.5 0.2 fusion.62
  63.8 2.1 %fusion.30 = f32[32,2,64,16]{2,3,1,0:T(8,128)} fusion(f32[32,16,16]{2,1,0:T(8,128)S(1)} %fusion.62, f32[32,16,2]{1,2,0:T(2,128)} %copy.66, f32[32,16,2]{1,2,0:T(2,128)} %copy.64, pred[16,16]{1,0:T(8,128)(4,1)} %iota_compare_fusion.8, bf16[32,16,2,64]{3,2,1,0:T(2,128)(2,1)S(1)} %reshape.277), kind=kOutput, calls=%fused_computation.67 | convolution fusion | flops 2195456 | bytes 434432 | tf_op jit(solution)/shard_map/rtsh,rshp->rthp/dot_general | solution.py:235
  65.8 2.6 %fusion.10 = f32[48,2,64,128]{3,2,1,0:T(8,128)} fusion(f32[48,16,2,64]{3,1,2,0:T(8,128)S(1)} %gather_fusion.3, pred[48]{0:T(512)(128)(4,1)S(1)} %get-tuple-element.29, pred[48]{0:T(512)(128)(4,1)S(1)} %get-tuple-element.30, bf16[48,16,128]{2,1,0:T(8,128)(2,1)S(1)} %gather_fusion.5), kind=kOutput, calls=%fused_computation.39 | convolution fusion | flops 25559040 | bytes 3735648 | tf_op jit(solution)/shard_map/jshp,jsn->jhpn/dot_general | solution.py:235
  68.5 3.7 %convolution_multiply_fusion = f32[48,16,2,64]{3,1,2,0:T(8,128)} fusion(bf16[48,2,64,128]{3,2,1,0:T(8,128)(2,1)} %all-to-all-done, f32[48,16,2]{1,2,0:T(2,128)S(1)} %select_select_fusion.5, bf16[48,16,128]{2,1,0:T(8,128)(2,1)S(1)} %gather_fusion.4, pred[48]{0:T(512)(128)(4,1)S(1)} %get-tuple-element.29, pred[48]{0:T(512)(128)(4,1)S(1)} %get-tuple-element.30), kind=kOutput, calls=%fused_computation.12 | convolution fusion | flops 25460736 | bytes 2168928 | tf_op jit(solution)/shard_map/jhpn,jtn->jthp/dot_general | solution.py:352
  72.2 1.8 %gather_fusion.1 = f32[32,16,2,64]{3,1,2,0:T(8,128)S(1)} fusion(f32[48,16,2,64]{3,1,2,0:T(8,128)} %convolution_multiply_fusion, s32[1024]{0:T(1024)} %pad_clamp_fusion), kind=kCustom, calls=%fused_computation.3 | custom fusion | bytes 524416 | tf_op jit(solution)/shard_map/jit(_take)/gather | solution.py:355
  74.1 1.4 fusion.2
  75.6 0.3 copy.73
  75.8 0.3 reshape.280
  76.3 3.0 %multiply_reduce_fusion.1 = (f32[512]{0:T(512)S(1)}, f32[512,128]{0,1:T(8,128)S(1)}) fusion(f32[512,128]{0,1:T(8,128)S(1)} %copy.74, bf16[512,2560]{1,0:T(8,128)(2,1)} %bitcast.72, bf16[2560,128]{1,0:T(8,128)(2,1)} %param.22), kind=kOutput, calls=%fused_computation.57 | convolution fusion | flops 336133632 | bytes 3803136 | tf_op jit(solution)/shard_map/dot_general | solution.py:277
  79.4 0.9 convolution_convert_fusion
  80.3 0.2 select_select_fusion.4
  80.5 1.7 %pad_maximum_fusion = bf16[512,2688]{1,0:T(8,128)(2,1)} fusion(bf16[512,128]{1,0:T(8,128)(2,1)S(1)} %select_select_fusion.4, bf16[512,2560]{1,0:T(8,128)(2,1)S(1)} %convolution_convert_fusion), kind=kLoop, calls=%fused_computation.9 | loop fusion | flops 5505024 | bytes 5505024 | tf_op jit(solution)/shard_map/concatenate | solution.py:375
  82.2 29.4 %shard_map.195 = (bf16[4,8,16,2688]{3,2,1,0:T(8,128)(2,1)}, bf16[2,4,16,2688]{3,2,1,0:T(8,128)(2,1)}) custom-call(bf16[4,8,16,2688]{3,2,1,0:T(8,128)(2,1)} %bitcast.68), custom_call_target="tpu_custom_call" | custom-call | tf_op jit(solution)/shard_map/pallas_call | solution.py:108
  111.7 2.5 %convert_reduce_fusion = f32[8,16,2688]{2,1,0:T(8,128)S(1)} fusion(bf16[4,8,16,2688]{3,2,1,0:T(8,128)(2,1)} %get-tuple-element.4), kind=kLoop, calls=%fused_computation.6 | loop fusion | flops 2408448 | bytes 4128768 | tf_op jit(solution)/shard_map/reduce_sum | solution.py:376
  114.2 1.1 copy-done.2
  115.3 0.2 convert_reduce_fusion.2
  115.5 3.5 %add_convert_fusion = bf16[48,2,64,128]{3,2,1,0:T(8,128)(2,1)} fusion(f32[48,2,64,128]{3,2,1,0:T(8,128)S(1)} %copy-done.1, bf16[48,2,64,128]{3,2,1,0:T(8,128)(2,1)} %all-to-all-done, f32[48,2]{1,0:T(8,128)S(1)} %select_select_fusion.6, f32[48,16,2,64]{3,1,2,0:T(8,128)S(1)} %gather_fusion.3, pred[48]{0:T(512)(128)(4,1)S(1)} %get-tuple-element.29, ...), kind=kOutput, calls=%fused_computation.8 | convolution fusion | flops 29884416 | bytes 6881760 | tf_op jit(solution)/shard_map/jshp,jsn->jhpn/dot_general | solution.py:235
  119.0 8.6 %all-to-all-start.1 = ((bf16[48,2,64,128]{3,2,1,0:T(8,128)(2,1)}), bf16[48,2,64,128]{3,2,1,0:T(8,128)(2,1)S(1)}, u32[]{:S(2)}, u32[]{:S(2)}) async-start(bf16[48,2,64,128]{3,2,1,0:T(8,128)(2,1)} %add_convert_fusion), calls=%async_computation.1 | async-start | bytes 3145728 | tf_op jit(solution)/shard_map/all_to_all | solution.py:359
  127.6 2.5 %select_convert_fusion.src_ref = bf16[8,16,2688]{2,1,0:T(8,128)(2,1)} fusion(f32[8,16,2688]{2,1,0:T(8,128)} %copy-done.2, bf16[8,16]{1,0:T(8,128)(2,1)S(1)} %get-tuple-element.6, bf16[8,16]{1,0:T(8,128)(2,1)S(1)} %get-tuple-element.5, pred[2688]{0:T(1024)(128)(4,1)S(1)} %get-tuple-element.33, pred[2688]{0:T(1024)(128)(4,1)S(1)} %get-tuple-element.34), kind=kLoop, calls=%fused_computation.11 | loop fusion | flops 688128 | bytes 2070272 | tf_op jit(solution)/shard_map/convert_element_type | solution.py:385
  130.1 21.4 %shard_map.196 = bf16[8,16,2688]{2,1,0:T(8,128)(2,1)} custom-call(bf16[8,16,2688]{2,1,0:T(8,128)(2,1)} %select_convert_fusion.src_ref), custom_call_target="tpu_custom_call" | custom-call | tf_op jit(solution)/shard_map/pallas_call | solution.py:207
  151.6 1.2 convert_reduce_fusion.1
  152.8 0.2 fusion.50
  152.9 0.7 fusion.43
  153.7 2.1 %convert_element_type.185 = f32[48,2,64,128]{3,2,1,0:T(8,128)} convert(bf16[48,2,64,128]{3,2,1,0:T(8,128)(2,1)S(1)} %all-to-all-done.1) | non-fusion elementwise | flops 786432 | bytes 4718592 | tf_op jit(solution)/shard_map/convert_element_type | solution.py:361
  (95 shorter events, 2.4 us)
Async XLA Ops:
  0.6 50.8 %copy-start = (bf16[2560,256]{1,0:T(8,128)(2,1)S(1)}, bf16[2560,256]{1,0:T(8,128)(2,1)}, u32[]{:S(2)}) copy-start(bf16[2560,256]{1,0:T(8,128)(2,1)} %param.24) | copy-start | bytes 3932164
  4.2 8.2 %copy-start.17 = (s32[32,1]{0,1:T(1,128)S(1)}, s32[32,1]{0,1:T(1,128)}, u32[]{:S(2)}) copy-start(s32[32,1]{0,1:T(1,128)} %param.37) | copy-start | bytes 388
  4.2 41.7 %copy-start.23 = (f32[2]{0:T(128)S(1)}, f32[2]{0:T(128)}, u32[]{:S(2)}) copy-start(f32[2]{0:T(128)} %param.29) | copy-start | bytes 28
  4.2 41.7 %copy-start.10 = (bf16[2560,2]{0,1:T(2,128)(2,1)S(1)}, bf16[2560,2]{0,1:T(2,128)(2,1)}, u32[]{:S(2)}) copy-start(bf16[2560,2]{0,1:T(2,128)(2,1)} %param.25) | copy-start | bytes 30724
  4.2 64.3 %all-to-all-start = ((bf16[48,2,64,128]{3,2,1,0:T(8,128)(2,1)}), bf16[48,2,64,128]{3,2,1,0:T(8,128)(2,1)}, u32[]{:S(2)}, u32[]{:S(2)}) async-start(bf16[48,2,64,128]{3,2,1,0:T(8,128)(2,1)} %convert_element_type.165), calls=%async_computation | async-start | bytes 3145728 | tf_op jit(solution)/shard_map/all_to_all | solution.py:339
  13.2 35.4 %copy-start.24 = (s32[4]{0:T(128)S(1)}, s32[4]{0:T(128)}, u32[]{:S(2)}) copy-start(s32[4]{0:T(128)} %param.36) | copy-start | bytes 52
  13.2 35.7 %copy-start.22 = (f32[4,2]{0,1:T(2,128)S(1)}, f32[4,2]{0,1:T(2,128)}, u32[]{:S(2)}) copy-start(f32[4,2]{0,1:T(2,128)} %param.28) | copy-start | bytes 100
  45.9 5.2 %copy-start.16 = (s32[32]{0:T(128)S(1)}, s32[32]{0:T(128)}, u32[]{:S(2)}) copy-start(s32[32]{0:T(128)} %param.38) | copy-start | bytes 388
  51.1 2.9 %copy-start.18 = (s32[32]{0:T(128)S(1)}, s32[32]{0:T(128)}, u32[]{:S(2)}) copy-start(s32[32]{0:T(128)} %param.39) | copy-start | bytes 388
  51.1 3.1 %copy-start.13 = (f32[4,256]{1,0:T(4,128)S(1)}, f32[4,256]{1,0:T(4,128)}, u32[]{:S(2)}) copy-start(f32[4,256]{1,0:T(4,128)} %param.27) | copy-start | bytes 12292
  51.3 3.7 %copy-start.21 = (bf16[2560,128]{1,0:T(8,128)(2,1)S(1)}, bf16[2560,128]{1,0:T(8,128)(2,1)}, u32[]{:S(2)}) copy-start(bf16[2560,128]{1,0:T(8,128)(2,1)} %param.23) | copy-start | bytes 1966084
  54.1 3.5 %copy-start.9 = (bf16[32,3,128]{2,0,1:T(8,128)(2,1)S(1)}, bf16[32,3,128]{2,0,1:T(8,128)(2,1)}, u32[]{:S(2)}) copy-start(bf16[32,3,128]{2,0,1:T(8,128)(2,1)} %param.33) | copy-start | bytes 73732
  54.1 3.6 %copy-start.14 = (f32[4,128]{1,0:T(4,128)S(1)}, f32[4,128]{1,0:T(4,128)}, u32[]{:S(2)}) copy-start(f32[4,128]{1,0:T(4,128)} %param.26) | copy-start | bytes 6148
  55.0 3.4 %copy-start.6 = (bf16[32,3,256]{2,0,1:T(8,128)(2,1)S(1)}, bf16[32,3,256]{2,0,1:T(8,128)(2,1)}, u32[]{:S(2)}) copy-start(bf16[32,3,256]{2,0,1:T(8,128)(2,1)} %param.34) | copy-start | bytes 147460
  58.4 2.2 %copy-start.11 = (s32[1024]{0:T(1024)}, s32[1024]{0:T(1024)S(1)}, u32[]{:S(2)}) copy-start(s32[1024]{0:T(1024)S(1)} %pad_clamp_fusion.2) | copy-start | bytes 12292
  59.0 2.8 %copy-start.12 = (s32[1024]{0:T(1024)}, s32[1024]{0:T(1024)S(1)}, u32[]{:S(2)}) copy-start(s32[1024]{0:T(1024)S(1)} %pad_clamp_fusion.1) | copy-start | bytes 12292
  63.7 4.7 %copy-start.4 = (f32[32,16,16]{2,1,0:T(8,128)}, f32[32,16,16]{2,1,0:T(8,128)S(1)}, u32[]{:S(2)}) copy-start(f32[32,16,16]{2,1,0:T(8,128)S(1)} %fusion.62) | copy-start | bytes 98308
  68.5 5.6 %copy-start.7 = (f32[32,16,2]{1,2,0:T(2,128)S(1)}, f32[32,16,2]{1,2,0:T(2,128)}, u32[]{:S(2)}) copy-start(f32[32,16,2]{1,2,0:T(2,128)} %copy.64) | copy-start | bytes 12292
  68.5 5.6 %copy-start.8 = (f32[32,16,2]{1,2,0:T(2,128)S(1)}, f32[32,16,2]{1,2,0:T(2,128)}, u32[]{:S(2)}) copy-start(f32[32,16,2]{1,2,0:T(2,128)} %copy.66) | copy-start | bytes 12292
  68.5 5.6 %copy-start.15 = (pred[16,16]{1,0:T(8,128)(4,1)S(1)}, pred[16,16]{1,0:T(8,128)(4,1)}, u32[]{:S(2)}) copy-start(pred[16,16]{1,0:T(8,128)(4,1)} %iota_compare_fusion.8) | copy-start | bytes 772
  68.5 5.6 %copy-start.19 = (pred[32]{0:T(512)(128)(4,1)S(1)}, pred[32]{0:T(512)(128)(4,1)}, u32[]{:S(2)}) copy-start(pred[32]{0:T(512)(128)(4,1)} %get-tuple-element.11) | copy-start | bytes 100
  68.5 5.6 %copy-start.25 = (f32[2]{0:T(128)S(1)}, f32[2]{0:T(128)}, u32[]{:S(2)}) copy-start(f32[2]{0:T(128)} %param.30) | copy-start | bytes 28
  68.5 5.6 %copy-start.5 = (f32[32,16,16]{2,1,0:T(8,128)S(1)}, f32[32,16,16]{2,1,0:T(8,128)}, u32[]{:S(2)}) copy-start(f32[32,16,16]{2,1,0:T(8,128)} %copy-done.4) | copy-start | bytes 98308
  75.8 3.5 %copy-start.20 = (f32[128]{0:T(128)S(1)}, f32[128]{0:T(128)}, u32[]{:S(2)}) copy-start(f32[128]{0:T(128)} %param.31) | copy-start | bytes 1540
  76.3 3.1 %copy-start.3 = (bf16[128,2560]{1,0:T(8,128)(2,1)S(1)}, bf16[128,2560]{1,0:T(8,128)(2,1)}, u32[]{:S(2)}) copy-start(bf16[128,2560]{1,0:T(8,128)(2,1)} %param.32) | copy-start | bytes 1966084
  111.7 3.8 %copy-start.1 = (f32[48,2,64,128]{3,2,1,0:T(8,128)S(1)}, f32[48,2,64,128]{3,2,1,0:T(8,128)}, u32[]{:S(2)}) copy-start(f32[48,2,64,128]{3,2,1,0:T(8,128)} %fusion.10) | copy-start | bytes 9437188
  114.2 1.1 copy-start.2
  119.0 34.7 %all-to-all-start.1 = ((bf16[48,2,64,128]{3,2,1,0:T(8,128)(2,1)}), bf16[48,2,64,128]{3,2,1,0:T(8,128)(2,1)S(1)}, u32[]{:S(2)}, u32[]{:S(2)}) async-start(bf16[48,2,64,128]{3,2,1,0:T(8,128)(2,1)} %add_convert_fusion), calls=%async_computation.1 | async-start | bytes 3145728 | tf_op jit(solution)/shard_map/all_to_all | solution.py:359

commit v15 on v14

--- a/solution.py
+++ b/solution.py
@@ -365,14 +365,16 @@
     sq_hi = sq_part.astype(jnp.bfloat16)
     sq_lo = (sq_part - sq_hi.astype(jnp.float32)).astype(jnp.bfloat16)
     scaled = (gated * norm_gain[None, :]).astype(jnp.bfloat16)
-    partial = jnp.dot(scaled, w_out, preferred_element_type=jnp.float32).astype(jnp.bfloat16)
-    width = partial.shape[1]
-    extra_column = lax.broadcasted_iota(jnp.int32, (partial.shape[0], 128), 1)
-    extra = jnp.where(
-        extra_column == 0, sq_hi[:, None], jnp.where(extra_column == 1, sq_lo[:, None], jnp.zeros((), jnp.bfloat16))
-    )
+    width = w_out.shape[1]
+    wide = jnp.dot(scaled, jnp.pad(w_out, ((0, 0), (0, 128))), preferred_element_type=jnp.float32)
+    wide_column = lax.broadcasted_iota(jnp.int32, wide.shape, 1)
+    wide = jnp.where(
+        wide_column == width,
+        sq_hi.astype(jnp.float32)[:, None],
+        jnp.where(wide_column == width + 1, sq_lo.astype(jnp.float32)[:, None], wide),
+    ).astype(jnp.bfloat16)
     n_y = lax.axis_size("by")
-    packed = jnp.concatenate([partial, extra], 1).reshape(n_y, n_blk // n_y, local_rows, width + 128)
+    packed = wide.reshape(n_y, n_blk // n_y, local_rows, width + 128)
     half_sum = jnp.sum(exchange4(packed, "by", False, 2).astype(jnp.float32), axis=0)
     sq_mid = half_sum[:, :, width] + half_sum[:, :, width + 1]
     sq_mid_hi = sq_mid.astype(jnp.bfloat16)

time: 156 us -> 155 us (level)
  other arithmetic: 19.6 us -> 17.1 us
  matrix products: 25.4 us -> 27 us
    concatenate x1 -> x0, other arithmetic: 1.74 us -> none  [shards(): jnp.concatenate([partial, extra], 1)]
    dot_general x1, matrix products: 0.93 us -> 2.55 us  [shards(): jnp.dot(scaled, jnp.pad(w_out, ((0, 0), (0, 128))), preferred_element_typ...]
where the time goes in v15:
time: 155 us
  Pallas kernels  83.1 us (54%)
  matrix products  27 us (17%)
  other arithmetic  17.1 us (11%)
  starting transfers between devices  16.5 us (11%)
  local copies, waits for them, and re-layouts  9.88 us (6%)
    pallas_call x1, Pallas kernels, gather2d(): pl.pallas_call(functools.partial(gather2d_kernel, nz), out_shape=jax.Shap...  32.4 us
    pallas_call x1, Pallas kernels, exchange4(): pl.pallas_call(functools.partial(ring4_kernel, axis, gather), out_shape=(...  29.3 us
    pallas_call x1, Pallas kernels, exchange(): pl.pallas_call(functools.partial(exchange_kernel, n, axis, gather), out_s...  21.4 us
    dot_general x4, matrix products, shards(): jnp.dot(block_rows, weight_cols, preferred_element_type=jnp.float32)  10.7 us
    all_to_all x1, starting transfers between devices, shards(): lax.all_to_all(buffer.astype(jnp.bfloat16), 'rep', split_axis=0, concat_a...  8.92 us
    all_to_all x1, starting transfers between devices, shards(): lax.all_to_all(pool.astype(jnp.bfloat16), 'rep', split_axis=0, concat_axi...  7.56 us
    dot_general x2, matrix products, split_dot(): jnp.einsum(spec, low, narrow, preferred_element_type=jnp.float32)  4.95 us
    dot_general x2, matrix products, split_dot(): jnp.einsum(spec, high, narrow, preferred_element_type=jnp.float32)  4.7 us
  transfers between devices with their start and end apart: 2, of which 0 were waited for; matrix products, arithmetic and copies ran while one was open for 18% of the time, Pallas kernels for 35%

profile of v15, /device:TPU:1, one launch (start us, length us, event | category | flops | bytes accessed | tf_op | source)
XLA Modules:
  0.0 154.8 jit_solution(17730491607013131076)
XLA Ops:
  0.6 3.5 %convert_element_type.178 = bf16[48,2,64,128]{3,2,1,0:T(8,128)(2,1)} convert(f32[48,2,64,128]{3,2,1,0:T(8,128)} %param.35) | non-fusion elementwise | flops 786432 | bytes 4718592 | tf_op jit(solution)/shard_map/convert_element_type | solution.py:340
  4.2 7.6 %all-to-all-start = ((bf16[48,2,64,128]{3,2,1,0:T(8,128)(2,1)}), bf16[48,2,64,128]{3,2,1,0:T(8,128)(2,1)}, u32[]{:S(2)}, u32[]{:S(2)}) async-start(bf16[48,2,64,128]{3,2,1,0:T(8,128)(2,1)} %convert_element_type.178), calls=%async_computation | async-start | bytes 3145728 | tf_op jit(solution)/shard_map/all_to_all | solution.py:339
  11.7 0.2 convert_reduce_fusion.5
  12.0 0.5 and_bitcast_fusion
  12.6 32.4 %shard_map.194 = bf16[4,8,16,2560]{3,2,1,0:T(8,128)(2,1)} custom-call(bf16[16,2560]{1,0:T(8,128)(2,1)} %bitcast.74), custom_call_target="tpu_custom_call" | custom-call | tf_op jit(solution)/shard_map/pallas_call | solution.py:190
  45.1 2.5 %fusion.4 = f32[512,2]{0,1:T(2,128)S(1)} fusion(bf16[512,2560]{1,0:T(8,128)(2,1)} %bitcast.67, bf16[2560,2]{0,1:T(2,128)(2,1)S(1)} %copy-done.9), kind=kOutput, calls=%fused_computation.21 | convolution fusion | flops 5244928 | bytes 2635776 | tf_op jit(solution)/shard_map/dot_general | solution.py:277
  47.8 0.2 reduce-window.4
  48.1 0.2 fusion.47
  48.3 0.2 copy.63
  48.5 0.7 fusion.71
  49.3 0.9 copy.64
  50.1 0.2 copy.76
  50.6 2.6 %convolution_convert_fusion = bf16[512,256]{1,0:T(8,128)(2,1)S(1)} fusion(bf16[512,2560]{1,0:T(8,128)(2,1)} %bitcast.68, bf16[2560,256]{1,0:T(8,128)(2,1)S(1)} %copy-done), kind=kOutput, calls=%fused_computation.16 | convolution fusion | flops 671219712 | bytes 4194304 | tf_op jit(solution)/shard_map/dot_general | solution.py:277
  53.5 0.7 copy.66
  54.2 2.6 %convolution_convert_fusion.2 = bf16[512,128]{1,0:T(8,128)(2,1)S(1)} fusion(bf16[512,2560]{1,0:T(8,128)(2,1)} %bitcast.69, bf16[2560,128]{1,0:T(8,128)(2,1)S(1)} %copy-done.18), kind=kOutput, calls=%fused_computation.19 | convolution fusion | flops 335609856 | bytes 3407872 | tf_op jit(solution)/shard_map/dot_general | solution.py:277
  57.0 0.2 multiply_convert_fusion.2
  57.3 0.3 copy.72
  57.8 0.3 multiply_convert_fusion
  58.2 0.6 pad_clamp_fusion
  58.9 0.6 gather_fusion
  59.6 0.2 convert_multiply_fusion
  59.8 0.6 gather_fusion.3
  60.4 0.6 gather_fusion.4
  61.0 0.7 gather_fusion.5
  61.8 0.7 gather_fusion.2
  62.6 0.2 select_select_fusion.4
  62.7 0.2 fusion.65
  62.9 2.1 %fusion.31 = f32[32,2,64,16]{2,3,1,0:T(8,128)} fusion(f32[32,16,16]{2,1,0:T(8,128)S(1)} %fusion.65, f32[32,16,2]{1,2,0:T(2,128)} %copy.66, f32[32,16,2]{1,2,0:T(2,128)} %copy.64, pred[16,16]{1,0:T(8,128)(4,1)S(1)} %iota_compare_fusion.8, bf16[32,16,2,64]{3,2,1,0:T(2,128)(2,1)S(1)} %reshape.278), kind=kOutput, calls=%fused_computation.67 | convolution fusion | flops 2195456 | bytes 434432 | tf_op jit(solution)/shard_map/rtsh,rshp->rthp/dot_general | solution.py:235
  65.0 2.6 %fusion.11 = f32[48,2,64,128]{3,2,1,0:T(8,128)} fusion(f32[48,16,2,64]{3,1,2,0:T(8,128)S(1)} %gather_fusion.3, pred[48]{0:T(512)(128)(4,1)S(1)} %get-tuple-element.29, pred[48]{0:T(512)(128)(4,1)S(1)} %get-tuple-element.30, bf16[48,16,128]{2,1,0:T(8,128)(2,1)S(1)} %gather_fusion.5), kind=kOutput, calls=%fused_computation.39 | convolution fusion | flops 25559040 | bytes 3735648 | tf_op jit(solution)/shard_map/jshp,jsn->jhpn/dot_general | solution.py:235
  67.7 3.7 %convolution_multiply_fusion = f32[48,16,2,64]{3,1,2,0:T(8,128)} fusion(bf16[48,2,64,128]{3,2,1,0:T(8,128)(2,1)} %all-to-all-done, f32[48,16,2]{1,2,0:T(2,128)S(1)} %select_select_fusion.4, bf16[48,16,128]{2,1,0:T(8,128)(2,1)S(1)} %gather_fusion.4, pred[48]{0:T(512)(128)(4,1)S(1)} %get-tuple-element.29, pred[48]{0:T(512)(128)(4,1)S(1)} %get-tuple-element.30), kind=kOutput, calls=%fused_computation.11 | convolution fusion | flops 25460736 | bytes 2168928 | tf_op jit(solution)/shard_map/jhpn,jtn->jthp/dot_general | solution.py:352
  71.4 1.8 %gather_fusion.1 = f32[32,16,2,64]{3,1,2,0:T(8,128)S(1)} fusion(f32[48,16,2,64]{3,1,2,0:T(8,128)} %convolution_multiply_fusion, s32[1024]{0:T(1024)} %pad_clamp_fusion), kind=kCustom, calls=%fused_computation.3 | custom fusion | bytes 524416 | tf_op jit(solution)/shard_map/jit(_take)/gather | solution.py:355
  73.3 1.4 fusion.2
  74.7 0.3 copy.73
  75.0 0.3 reshape.281
  75.5 3.0 %multiply_reduce_fusion.1 = (f32[512]{0:T(512)S(1)}, f32[512,128]{0,1:T(8,128)S(1)}) fusion(f32[512,128]{0,1:T(8,128)S(1)} %copy.74, bf16[512,2560]{1,0:T(8,128)(2,1)} %bitcast.70, bf16[2560,128]{1,0:T(8,128)(2,1)} %param.22), kind=kOutput, calls=%fused_computation.58 | convolution fusion | flops 336133632 | bytes 3803136 | tf_op jit(solution)/shard_map/dot_general | solution.py:277
  78.5 2.5 %select_convert_fusion = bf16[512,2688]{1,0:T(8,128)(2,1)} fusion(bf16[512]{0:T(512)(128)(2,1)S(1)} %get-tuple-element.22, bf16[512]{0:T(512)(128)(2,1)S(1)} %get-tuple-element.21, pred[2688]{0:T(1024)(128)(4,1)S(1)} %get-tuple-element.31, pred[2688]{0:T(1024)(128)(4,1)S(1)} %get-tuple-element.32, bf16[128,2560]{1,0:T(8,128)(2,1)S(1)} %copy-done.19, ...), kind=kOutput, calls=%fused_computation.7 | convolution fusion | flops 355205120 | bytes 3677952 | tf_op jit(solution)/shard_map/dot_general | solution.py:369
  81.1 29.3 %shard_map.195 = (bf16[4,8,16,2688]{3,2,1,0:T(8,128)(2,1)}, bf16[2,4,16,2688]{3,2,1,0:T(8,128)(2,1)}) custom-call(bf16[4,8,16,2688]{3,2,1,0:T(8,128)(2,1)} %bitcast.71), custom_call_target="tpu_custom_call" | custom-call | tf_op jit(solution)/shard_map/pallas_call | solution.py:108
  110.4 2.5 %convert_reduce_fusion = f32[8,16,2688]{2,1,0:T(8,128)S(1)} fusion(bf16[4,8,16,2688]{3,2,1,0:T(8,128)(2,1)} %get-tuple-element.4), kind=kLoop, calls=%fused_computation.6 | loop fusion | flops 2408448 | bytes 4128768 | tf_op jit(solution)/shard_map/reduce_sum | solution.py:378
  112.9 1.1 copy-done.2
  114.0 0.2 convert_reduce_fusion.2
  114.2 3.5 %add_convert_fusion = bf16[48,2,64,128]{3,2,1,0:T(8,128)(2,1)} fusion(f32[48,2,64,128]{3,2,1,0:T(8,128)S(1)} %copy-done.1, bf16[48,2,64,128]{3,2,1,0:T(8,128)(2,1)} %all-to-all-done, f32[48,2]{1,0:T(8,128)S(1)} %select_select_fusion.5, f32[48,16,2,64]{3,1,2,0:T(8,128)S(1)} %gather_fusion.3, pred[48]{0:T(512)(128)(4,1)S(1)} %get-tuple-element.29, ...), kind=kOutput, calls=%fused_computation.8 | convolution fusion | flops 29884416 | bytes 6881760 | tf_op jit(solution)/shard_map/jshp,jsn->jhpn/dot_general | solution.py:235
  117.7 8.9 %all-to-all-start.1 = ((bf16[48,2,64,128]{3,2,1,0:T(8,128)(2,1)}), bf16[48,2,64,128]{3,2,1,0:T(8,128)(2,1)S(1)}, u32[]{:S(2)}, u32[]{:S(2)}) async-start(bf16[48,2,64,128]{3,2,1,0:T(8,128)(2,1)} %add_convert_fusion), calls=%async_computation.1 | async-start | bytes 3145728 | tf_op jit(solution)/shard_map/all_to_all | solution.py:359
  126.6 2.6 %select_convert_fusion.1.src_ref = bf16[8,16,2688]{2,1,0:T(8,128)(2,1)} fusion(f32[8,16,2688]{2,1,0:T(8,128)} %copy-done.2, bf16[8,16]{1,0:T(8,128)(2,1)S(1)} %get-tuple-element.6, bf16[8,16]{1,0:T(8,128)(2,1)S(1)} %get-tuple-element.5, pred[2688]{0:T(1024)(128)(4,1)S(1)} %get-tuple-element.31, pred[2688]{0:T(1024)(128)(4,1)S(1)} %get-tuple-element.32), kind=kLoop, calls=%fused_computation.10 | loop fusion | flops 688128 | bytes 2070272 | tf_op jit(solution)/shard_map/convert_element_type | solution.py:387
  129.1 21.4 %shard_map.196 = bf16[8,16,2688]{2,1,0:T(8,128)(2,1)} custom-call(bf16[8,16,2688]{2,1,0:T(8,128)(2,1)} %select_convert_fusion.1.src_ref), custom_call_target="tpu_custom_call" | custom-call | tf_op jit(solution)/shard_map/pallas_call | solution.py:207
  150.6 1.2 convert_reduce_fusion.1
  151.8 0.2 fusion.51
  152.0 0.7 fusion.44
  152.7 2.1 %convert_element_type.199 = f32[48,2,64,128]{3,2,1,0:T(8,128)} convert(bf16[48,2,64,128]{3,2,1,0:T(8,128)(2,1)S(1)} %all-to-all-done.1) | non-fusion elementwise | flops 786432 | bytes 4718592 | tf_op jit(solution)/shard_map/convert_element_type | solution.py:361
  (90 shorter events, 1.9 us)
Async XLA Ops:
  0.6 50.0 %copy-start = (bf16[2560,256]{1,0:T(8,128)(2,1)S(1)}, bf16[2560,256]{1,0:T(8,128)(2,1)}, u32[]{:S(2)}) copy-start(bf16[2560,256]{1,0:T(8,128)(2,1)} %param.24) | copy-start | bytes 3932164
  4.2 7.6 %copy-start.15 = (s32[32,1]{0,1:T(1,128)S(1)}, s32[32,1]{0,1:T(1,128)}, u32[]{:S(2)}) copy-start(s32[32,1]{0,1:T(1,128)} %param.37) | copy-start | bytes 388
  4.2 40.9 %copy-start.21 = (f32[2]{0:T(128)S(1)}, f32[2]{0:T(128)}, u32[]{:S(2)}) copy-start(f32[2]{0:T(128)} %param.29) | copy-start | bytes 28
  4.2 40.9 %copy-start.9 = (bf16[2560,2]{0,1:T(2,128)(2,1)S(1)}, bf16[2560,2]{0,1:T(2,128)(2,1)}, u32[]{:S(2)}) copy-start(bf16[2560,2]{0,1:T(2,128)(2,1)} %param.25) | copy-start | bytes 30724
  4.2 63.5 %all-to-all-start = ((bf16[48,2,64,128]{3,2,1,0:T(8,128)(2,1)}), bf16[48,2,64,128]{3,2,1,0:T(8,128)(2,1)}, u32[]{:S(2)}, u32[]{:S(2)}) async-start(bf16[48,2,64,128]{3,2,1,0:T(8,128)(2,1)} %convert_element_type.178), calls=%async_computation | async-start | bytes 3145728 | tf_op jit(solution)/shard_map/all_to_all | solution.py:339
  12.6 35.2 %copy-start.22 = (s32[4]{0:T(128)S(1)}, s32[4]{0:T(128)}, u32[]{:S(2)}) copy-start(s32[4]{0:T(128)} %param.36) | copy-start | bytes 52
  12.6 35.5 %copy-start.20 = (f32[4,2]{0,1:T(2,128)S(1)}, f32[4,2]{0,1:T(2,128)}, u32[]{:S(2)}) copy-start(f32[4,2]{0,1:T(2,128)} %param.28) | copy-start | bytes 100
  45.1 5.2 %copy-start.14 = (s32[32]{0:T(128)S(1)}, s32[32]{0:T(128)}, u32[]{:S(2)}) copy-start(s32[32]{0:T(128)} %param.38) | copy-start | bytes 388
  50.3 2.9 %copy-start.16 = (s32[32]{0:T(128)S(1)}, s32[32]{0:T(128)}, u32[]{:S(2)}) copy-start(s32[32]{0:T(128)} %param.39) | copy-start | bytes 388
  50.3 3.1 %copy-start.12 = (f32[4,256]{1,0:T(4,128)S(1)}, f32[4,256]{1,0:T(4,128)}, u32[]{:S(2)}) copy-start(f32[4,256]{1,0:T(4,128)} %param.27) | copy-start | bytes 12292
  50.5 3.7 %copy-start.18 = (bf16[2560,128]{1,0:T(8,128)(2,1)S(1)}, bf16[2560,128]{1,0:T(8,128)(2,1)}, u32[]{:S(2)}) copy-start(bf16[2560,128]{1,0:T(8,128)(2,1)} %param.23) | copy-start | bytes 1966084
  53.3 3.5 %copy-start.8 = (bf16[32,3,128]{2,0,1:T(8,128)(2,1)S(1)}, bf16[32,3,128]{2,0,1:T(8,128)(2,1)}, u32[]{:S(2)}) copy-start(bf16[32,3,128]{2,0,1:T(8,128)(2,1)} %param.33) | copy-start | bytes 73732
  53.3 3.6 %copy-start.13 = (f32[4,128]{1,0:T(4,128)S(1)}, f32[4,128]{1,0:T(4,128)}, u32[]{:S(2)}) copy-start(f32[4,128]{1,0:T(4,128)} %param.26) | copy-start | bytes 6148
  54.2 3.4 %copy-start.5 = (bf16[32,3,256]{2,0,1:T(8,128)(2,1)S(1)}, bf16[32,3,256]{2,0,1:T(8,128)(2,1)}, u32[]{:S(2)}) copy-start(bf16[32,3,256]{2,0,1:T(8,128)(2,1)} %param.34) | copy-start | bytes 147460
  57.6 2.2 %copy-start.10 = (s32[1024]{0:T(1024)}, s32[1024]{0:T(1024)S(1)}, u32[]{:S(2)}) copy-start(s32[1024]{0:T(1024)S(1)} %pad_clamp_fusion.2) | copy-start | bytes 12292
  58.2 2.8 %copy-start.11 = (s32[1024]{0:T(1024)}, s32[1024]{0:T(1024)S(1)}, u32[]{:S(2)}) copy-start(s32[1024]{0:T(1024)S(1)} %pad_clamp_fusion.1) | copy-start | bytes 12292
  62.9 4.7 %copy-start.3 = (f32[32,16,16]{2,1,0:T(8,128)}, f32[32,16,16]{2,1,0:T(8,128)S(1)}, u32[]{:S(2)}) copy-start(f32[32,16,16]{2,1,0:T(8,128)S(1)} %fusion.65) | copy-start | bytes 98308
  67.6 5.6 %copy-start.6 = (f32[32,16,2]{1,2,0:T(2,128)S(1)}, f32[32,16,2]{1,2,0:T(2,128)}, u32[]{:S(2)}) copy-start(f32[32,16,2]{1,2,0:T(2,128)} %copy.64) | copy-start | bytes 12292
  67.6 5.6 %copy-start.7 = (f32[32,16,2]{1,2,0:T(2,128)S(1)}, f32[32,16,2]{1,2,0:T(2,128)}, u32[]{:S(2)}) copy-start(f32[32,16,2]{1,2,0:T(2,128)} %copy.66) | copy-start | bytes 12292
  67.6 5.6 %copy-start.17 = (pred[32]{0:T(512)(128)(4,1)S(1)}, pred[32]{0:T(512)(128)(4,1)}, u32[]{:S(2)}) copy-start(pred[32]{0:T(512)(128)(4,1)} %get-tuple-element.9) | copy-start | bytes 100
  67.6 5.6 %copy-start.23 = (f32[2]{0:T(128)S(1)}, f32[2]{0:T(128)}, u32[]{:S(2)}) copy-start(f32[2]{0:T(128)} %param.30) | copy-start | bytes 28
  67.7 5.6 %copy-start.4 = (f32[32,16,16]{2,1,0:T(8,128)S(1)}, f32[32,16,16]{2,1,0:T(8,128)}, u32[]{:S(2)}) copy-start(f32[32,16,16]{2,1,0:T(8,128)} %copy-done.3) | copy-start | bytes 98308
  75.0 3.5 %copy-start.24 = (f32[128]{0:T(128)S(1)}, f32[128]{0:T(128)}, u32[]{:S(2)}) copy-start(f32[128]{0:T(128)} %param.31) | copy-start | bytes 1540
  75.4 3.0 %copy-start.19 = (bf16[128,2560]{1,0:T(8,128)(2,1)S(1)}, bf16[128,2560]{1,0:T(8,128)(2,1)}, u32[]{:S(2)}) copy-start(bf16[128,2560]{1,0:T(8,128)(2,1)} %param.32) | copy-start | bytes 1966084
  110.3 3.8 %copy-start.1 = (f32[48,2,64,128]{3,2,1,0:T(8,128)S(1)}, f32[48,2,64,128]{3,2,1,0:T(8,128)}, u32[]{:S(2)}) copy-start(f32[48,2,64,128]{3,2,1,0:T(8,128)} %fusion.11) | copy-start | bytes 9437188
  112.9 1.1 copy-start.2
  117.7 35.0 %all-to-all-start.1 = ((bf16[48,2,64,128]{3,2,1,0:T(8,128)(2,1)}), bf16[48,2,64,128]{3,2,1,0:T(8,128)(2,1)S(1)}, u32[]{:S(2)}, u32[]{:S(2)}) async-start(bf16[48,2,64,128]{3,2,1,0:T(8,128)(2,1)} %add_convert_fusion), calls=%async_computation.1 | async-start | bytes 3145728 | tf_op jit(solution)/shard_map/all_to_all | solution.py:359
